TPU v7x, 32 devices: a whole 2x2x4 slice. The times are simulated.
32 devices in a mesh: dp: 4 (over z), seq: 8 (over y, x, core).
Axes of the slice: x: 2, y: 2, z: 4, core: 2. Of those that a mesh axis runs over, the one named last changes fastest.
Arguments:
- states: bfloat16 [4, 2048, 768], P('dp', 'seq'), may hold values from -6 to 6
- segment_ids: int32 [4, 2048], P('dp', 'seq'), may hold values from 0 to 7, as said below
- project_weight: bfloat16 [2, 768, 2304], P(None, ('dp', 'seq')), may hold values from -0.3125 to 0.3125
- query_bias: bfloat16 [2, 768], P(None, ('dp', 'seq')), may hold values from -4 to 4
- value_bias: bfloat16 [2, 768], P(None, ('dp', 'seq')), may hold values from -1.5 to 1.5
- output_weight: bfloat16 [2, 768, 768], P(None, ('dp', 'seq')), may hold values from -1.75 to 1.75
- output_bias: bfloat16 [2, 768], P(None, ('dp', 'seq')), may hold values from -4 to 4
- attention_gain: bfloat16 [2, 768], P(None, ('dp', 'seq')), may hold values from 0.5 to 1.5
- attention_shift: bfloat16 [2, 768], P(None, ('dp', 'seq')), may hold values from -4 to 4
- up_weight: bfloat16 [2, 768, 3072], P(None, ('dp', 'seq')), may hold values from -0.21875 to 0.21875
- up_bias: bfloat16 [2, 3072], P(None, ('dp', 'seq')), may hold values from -6 to 6
- down_weight: bfloat16 [2, 3072, 768], P(None, ('dp', 'seq')), may hold values from -0.109375 to 0.109375
- down_bias: bfloat16 [2, 768], P(None, ('dp', 'seq')), may hold values from -4 to 4
- feed_gain: bfloat16 [2, 768], P(None, ('dp', 'seq')), may hold values from 0.5 to 1.5
- feed_shift: bfloat16 [2, 768], P(None, ('dp', 'seq')), may hold values from -4 to 4
- cotangent: bfloat16 [4, 2048, 768], P('dp', 'seq'), may hold values from -6 to 6
Outputs:
- output: bfloat16 [4, 2048, 768], P('dp', 'seq')
- input_grad: float32 [4, 2048, 768], P('dp', 'seq')
- grad_project_weight: float32 [2, 768, 2304], P(None, 'seq')
- grad_query_bias: float32 [2, 768], P(None, 'seq')
- grad_value_bias: float32 [2, 768], P(None, 'seq')
- grad_output_weight: float32 [2, 768, 768], P(None, 'seq')
- grad_output_bias: float32 [2, 768], P(None, 'seq')
- grad_attention_gain: float32 [2, 768], P(None, 'seq')
- grad_attention_shift: float32 [2, 768], P(None, 'seq')
- grad_up_weight: float32 [2, 768, 3072], P(None, 'seq')
- grad_up_bias: float32 [2, 3072], P(None, 'seq')
- grad_down_weight: float32 [2, 3072, 768], P(None, 'seq')
- grad_down_bias: float32 [2, 768], P(None, 'seq')
- grad_feed_gain: float32 [2, 768], P(None, 'seq')
- grad_feed_shift: float32 [2, 768], P(None, 'seq')
Inputs may be any that keep to these rules, and one draw needn't show every extreme that they name: `segment_ids`: within each sequence the ids never fall and run over 0 .. 7; each document holds 60 to 800 tokens and one holds exactly 800.
All inputs are finite; a program needn't handle non-finite values.
Results may differ from a plain program's by a relative error of at most 0.035.
Values may be sent and summed in bfloat16 or wider, within the bound.
No kernel may reach another device: no remote copies, remote signals or barrier semaphores. Data moves between devices by JAX's collectives and lax.ppermute only.
A program may use at most 192 MiB of HBM per device.

v0:
```python
import math

import jax
import jax.numpy as jnp
from jax import lax
from jax.sharding import PartitionSpec as P

HEADS = 12
HEAD_DIM = 64
LAYERS = 2


MASKED_SCORE = -1000000000.0
EPSILON = 1e-12


def as_sent(value):

    def short(part):
        return part.astype(jnp.bfloat16) if part.dtype == jnp.float32 else part

    return jax.tree.map(short, value)


def layer_norm(rows, gain, shift):
    centre = rows - jnp.mean(rows, axis=-1, keepdims=True)
    spread = jnp.mean(centre * centre, axis=-1, keepdims=True)
    return centre * lax.rsqrt(spread + EPSILON) * gain + shift


def gelu_exact(inner):
    return 0.5 * inner * (1.0 + lax.erf(inner * 0.7071067811865476))


def split_blocks(arrays, count):
    size = math.gcd(count, 512)
    return tuple((item.reshape((count // size, size) + item.shape[1:]) for item in arrays))


def head_view(rows):
    return rows.reshape(rows.shape[:-1] + (HEADS, HEAD_DIM))


def fetch_forward(stacked, layer_index):
    return lax.all_gather(
        as_sent(tuple((item[layer_index] for item in stacked))), ("dp", "seq"), axis=0, tiled=True
    )


def fetch_backward(stacked, layer_index):
    return lax.all_gather(
        as_sent(tuple((item[layer_index] for item in stacked))), ("dp", "seq"), axis=0, tiled=True
    )


def attend_forward(queries_heads, seg_here, keys_local, values_local, scale):
    sequences, tokens = seg_here.shape

    def stats_one(carry, query_seq, seg_query, keys_piece, seg_piece):
        blocks = split_blocks((head_view(keys_piece), seg_piece), keys_piece.shape[0])

        def stats_inner_step(state, block):
            top, total = state
            keys_block, seg_block = block
            scores = (
                jnp.einsum(
                    "thd,nhd->htn", query_seq, keys_block, preferred_element_type=jnp.float32
                )
                * scale
            )
            allowed = (seg_query[:, None] == seg_block[None, :])[None]
            masked = jnp.where(allowed, scores, MASKED_SCORE)
            new_top = jnp.maximum(top, jnp.max(masked, axis=-1))
            weights = jnp.where(allowed, jnp.exp(masked - new_top[:, :, None]), 0.0)
            return ((new_top, total * jnp.exp(top - new_top) + jnp.sum(weights, axis=-1)), None)

        result, unused = lax.scan(stats_inner_step, carry, blocks)
        return result

    initial = (
        jnp.full((sequences, HEADS, tokens), MASKED_SCORE, jnp.float32),
        jnp.zeros((sequences, HEADS, tokens), jnp.float32),
    )
    keys_piece = lax.all_gather(keys_local, "seq", axis=1, tiled=True)
    seg_piece = lax.all_gather(seg_here, "seq", axis=1, tiled=True)
    top, total = jax.vmap(stats_one)(initial, queries_heads, seg_here, keys_piece, seg_piece)
    log_total = top + jnp.log(total)

    def value_one(carry, query_seq, seg_query, log_seq, keys_piece, values_piece, seg_piece):
        blocks = split_blocks(
            (head_view(keys_piece), head_view(values_piece), seg_piece), keys_piece.shape[0]
        )

        def value_inner_step(state, block):
            keys_block, values_block, seg_block = block
            scores = (
                jnp.einsum(
                    "thd,nhd->htn", query_seq, keys_block, preferred_element_type=jnp.float32
                )
                * scale
            )
            allowed = (seg_query[:, None] == seg_block[None, :])[None]
            probs = jnp.where(allowed, jnp.exp(scores - log_seq[:, :, None]), 0.0).astype(
                jnp.bfloat16
            )
            return (
                state
                + jnp.einsum(
                    "htn,nhd->thd", probs, values_block, preferred_element_type=jnp.float32
                ),
                None,
            )

        result, unused = lax.scan(value_inner_step, carry, blocks)
        return result

    empty = jnp.zeros((sequences, tokens, HEADS, HEAD_DIM), jnp.float32)
    keys_piece = lax.all_gather(keys_local, "seq", axis=1, tiled=True)
    values_piece = lax.all_gather(values_local, "seq", axis=1, tiled=True)
    seg_piece = lax.all_gather(seg_here, "seq", axis=1, tiled=True)
    attended = jax.vmap(value_one)(
        empty, queries_heads, seg_here, log_total, keys_piece, values_piece, seg_piece
    )
    return (attended, log_total)


def attend_backward(
    queries_local, keys_local, values_local, seg_here, log_total, grad_context, attended, scale
):
    sequences, tokens = seg_here.shape
    queries_heads = head_view(queries_local)
    grad_heads = head_view(grad_context)
    delta_rows = jnp.sum(grad_heads.astype(jnp.float32) * attended, axis=-1)
    delta = jnp.swapaxes(delta_rows, 1, 2)

    def query_one(
        carry,
        query_seq,
        grad_seq,
        seg_query,
        log_seq,
        delta_seq,
        keys_piece,
        values_piece,
        seg_piece,
    ):
        blocks = split_blocks(
            (head_view(keys_piece), head_view(values_piece), seg_piece), keys_piece.shape[0]
        )

        def query_inner_step(state, block):
            keys_block, values_block, seg_block = block
            scores = (
                jnp.einsum(
                    "thd,nhd->htn", query_seq, keys_block, preferred_element_type=jnp.float32
                )
                * scale
            )
            allowed = (seg_query[:, None] == seg_block[None, :])[None]
            probs = jnp.where(allowed, jnp.exp(scores - log_seq[:, :, None]), 0.0)
            grad_probs = jnp.einsum(
                "thd,nhd->htn", grad_seq, values_block, preferred_element_type=jnp.float32
            )
            grad_scores = (probs * (grad_probs - delta_seq[:, :, None])).astype(jnp.bfloat16)
            return (
                state
                + jnp.einsum(
                    "htn,nhd->thd", grad_scores, keys_block, preferred_element_type=jnp.float32
                ),
                None,
            )

        result, unused = lax.scan(query_inner_step, carry, blocks)
        return result

    empty = jnp.zeros((sequences, tokens, HEADS, HEAD_DIM), jnp.float32)
    keys_piece = lax.all_gather(keys_local, "seq", axis=1, tiled=True)
    values_piece = lax.all_gather(values_local, "seq", axis=1, tiled=True)
    seg_piece = lax.all_gather(seg_here, "seq", axis=1, tiled=True)
    grad_queries = jax.vmap(query_one)(
        empty,
        queries_heads,
        grad_heads,
        seg_here,
        log_total,
        delta,
        keys_piece,
        values_piece,
        seg_piece,
    )
    keys_heads = head_view(keys_local)
    values_heads = head_view(values_local)

    def owner_one(
        carry,
        keys_seq,
        values_seq,
        seg_key,
        query_piece,
        grad_piece,
        log_piece,
        delta_piece,
        seg_piece,
    ):
        count = query_piece.shape[0]
        blocks = split_blocks(
            (
                head_view(query_piece.astype(jnp.bfloat16)),
                head_view(grad_piece.astype(jnp.bfloat16)),
                log_piece,
                delta_piece,
                seg_piece,
            ),
            count,
        )

        def owner_inner_step(state, block):
            grad_keys, grad_values = state
            query_block, grad_block, log_block, delta_block, seg_block = block
            scores = (
                jnp.einsum(
                    "bhd,thd->hbt", query_block, keys_seq, preferred_element_type=jnp.float32
                )
                * scale
            )
            allowed = (seg_block[:, None] == seg_key[None, :])[None]
            probs = jnp.where(allowed, jnp.exp(scores - log_block.T[:, :, None]), 0.0)
            grad_values = grad_values + jnp.einsum(
                "hbt,bhd->thd",
                probs.astype(jnp.bfloat16),
                grad_block,
                preferred_element_type=jnp.float32,
            )
            grad_probs = jnp.einsum(
                "bhd,thd->hbt", grad_block, values_seq, preferred_element_type=jnp.float32
            )
            grad_scores = (probs * (grad_probs - delta_block.T[:, :, None])).astype(jnp.bfloat16)
            grad_keys = grad_keys + jnp.einsum(
                "hbt,bhd->thd", grad_scores, query_block, preferred_element_type=jnp.float32
            )
            return ((grad_keys, grad_values), None)

        result, unused = lax.scan(owner_inner_step, carry, blocks)
        return result

    query_piece = lax.all_gather(queries_local.astype(jnp.float32), "seq", axis=1, tiled=True)
    grad_piece = lax.all_gather(grad_context.astype(jnp.float32), "seq", axis=1, tiled=True)
    log_piece = lax.all_gather(jnp.swapaxes(log_total, 1, 2), "seq", axis=1, tiled=True)
    delta_piece = lax.all_gather(delta_rows, "seq", axis=1, tiled=True)
    seg_piece = lax.all_gather(seg_here, "seq", axis=1, tiled=True)
    grad_keys, grad_values = jax.vmap(owner_one)(
        (empty, empty),
        keys_heads,
        values_heads,
        seg_here,
        query_piece,
        grad_piece,
        log_piece,
        delta_piece,
        seg_piece,
    )
    rows = sequences * tokens
    grad_queries = (grad_queries * scale).reshape(rows, -1).astype(jnp.bfloat16)
    grad_keys = (grad_keys * scale).reshape(rows, -1).astype(jnp.bfloat16)
    grad_values = grad_values.reshape(rows, -1).astype(jnp.bfloat16)
    return (grad_queries, grad_keys, grad_values)


def layer_stack(results, slot):
    return jnp.stack([item[slot] for item in results])


def per_device(
    states,
    segment_ids,
    project_weight,
    query_bias,
    value_bias,
    output_weight,
    output_bias,
    attention_gain,
    attention_shift,
    up_weight,
    up_bias,
    down_weight,
    down_bias,
    feed_gain,
    feed_shift,
    cotangent,
):
    stacked = (
        project_weight,
        query_bias,
        value_bias,
        output_weight,
        output_bias,
        attention_gain,
        attention_shift,
        up_weight,
        up_bias,
        down_weight,
        down_bias,
        feed_gain,
        feed_shift,
    )
    scale = HEAD_DIM ** (-0.5)
    sequences, tokens, width = states.shape
    rows = sequences * tokens
    current = states.reshape(rows, width).astype(jnp.float32)
    saved = []
    for layer_index in range(LAYERS):
        params = fetch_forward(stacked, layer_index)
        (
            w_project,
            b_query,
            b_value,
            w_output,
            b_output,
            g_attention,
            s_attention,
            w_up,
            b_up,
            w_down,
            b_down,
            g_feed,
            s_feed,
        ) = params
        entered = current.astype(jnp.bfloat16)
        projected = jnp.dot(entered, w_project, preferred_element_type=jnp.float32)
        queries = (projected[:, :width] + b_query.astype(jnp.float32)).astype(jnp.bfloat16)
        keys_flat = projected[:, width : 2 * width].astype(jnp.bfloat16)
        values_flat = (projected[:, 2 * width :] + b_value.astype(jnp.float32)).astype(jnp.bfloat16)
        queries_seq = queries.reshape(sequences, tokens, width)
        keys_local = keys_flat.reshape(sequences, tokens, width)
        values_local = values_flat.reshape(sequences, tokens, width)
        attended, log_total = attend_forward(
            head_view(queries_seq), segment_ids, keys_local, values_local, scale
        )
        context = attended.reshape(rows, width).astype(jnp.bfloat16)
        branch = jnp.dot(context, w_output, preferred_element_type=jnp.float32) + b_output.astype(
            jnp.float32
        )
        sum_first = current + branch
        hidden = layer_norm(
            sum_first, g_attention.astype(jnp.float32), s_attention.astype(jnp.float32)
        )
        hidden_low = hidden.astype(jnp.bfloat16)
        inner = jnp.dot(hidden_low, w_up, preferred_element_type=jnp.float32) + b_up.astype(
            jnp.float32
        )
        activated = gelu_exact(inner).astype(jnp.bfloat16)
        outward = jnp.dot(activated, w_down, preferred_element_type=jnp.float32) + b_down.astype(
            jnp.float32
        )
        sum_second = hidden + outward
        kept = None
        saved.append(
            (
                entered,
                queries_seq,
                keys_local,
                values_local,
                attended,
                log_total,
                context,
                sum_first,
                hidden_low,
                inner,
                activated,
                sum_second,
                kept,
            )
        )
        current = layer_norm(sum_second, g_feed.astype(jnp.float32), s_feed.astype(jnp.float32))
    output = current.reshape(sequences, tokens, width).astype(jnp.bfloat16)
    grad_current = cotangent.reshape(rows, width).astype(jnp.float32)
    results = [None] * LAYERS
    for layer_index in reversed(range(LAYERS)):
        (
            entered,
            queries_seq,
            keys_local,
            values_local,
            attended,
            log_total,
            context,
            sum_first,
            hidden_low,
            inner,
            activated,
            sum_second,
            kept,
        ) = saved[layer_index]
        params = fetch_backward(stacked, layer_index)
        (
            w_project,
            b_query,
            b_value,
            w_output,
            b_output,
            g_attention,
            s_attention,
            w_up,
            b_up,
            w_down,
            b_down,
            g_feed,
            s_feed,
        ) = params
        unused, norm_second = jax.vjp(
            layer_norm, sum_second, g_feed.astype(jnp.float32), s_feed.astype(jnp.float32)
        )
        grad_sum2, grad_feed_gain, grad_feed_shift = norm_second(grad_current)
        grad_outward = grad_sum2.astype(jnp.bfloat16)
        grad_down_bias = jnp.sum(grad_outward.astype(jnp.float32), axis=0)
        grad_down_weight = jnp.einsum(
            "tf,td->fd", activated, grad_outward, preferred_element_type=jnp.float32
        )
        grad_activated = jnp.einsum(
            "td,fd->tf", grad_outward, w_down, preferred_element_type=jnp.float32
        )
        unused, gelu_back = jax.vjp(gelu_exact, inner)
        grad_inner = gelu_back(grad_activated)[0].astype(jnp.bfloat16)
        grad_up_bias = jnp.sum(grad_inner.astype(jnp.float32), axis=0)
        grad_up_weight = jnp.einsum(
            "td,tf->df", hidden_low, grad_inner, preferred_element_type=jnp.float32
        )
        grad_hidden = grad_sum2 + jnp.einsum(
            "tf,df->td", grad_inner, w_up, preferred_element_type=jnp.float32
        )
        unused, norm_first = jax.vjp(
            layer_norm, sum_first, g_attention.astype(jnp.float32), s_attention.astype(jnp.float32)
        )
        grad_sum1, grad_attention_gain, grad_attention_shift = norm_first(grad_hidden)
        grad_branch = grad_sum1.astype(jnp.bfloat16)
        grad_output_bias = jnp.sum(grad_branch.astype(jnp.float32), axis=0)
        grad_output_weight = jnp.einsum(
            "td,te->de", context, grad_branch, preferred_element_type=jnp.float32
        )
        grad_context = jnp.einsum(
            "te,de->td", grad_branch, w_output, preferred_element_type=jnp.float32
        ).astype(jnp.bfloat16)
        grad_queries, grad_keys, grad_values = attend_backward(
            queries_seq,
            keys_local,
            values_local,
            segment_ids,
            log_total,
            grad_context.reshape(sequences, tokens, width),
            attended,
            scale,
        )
        grad_projected = jnp.concatenate([grad_queries, grad_keys, grad_values], axis=1)
        grad_query_bias = jnp.sum(grad_queries.astype(jnp.float32), axis=0)
        grad_value_bias = jnp.sum(grad_values.astype(jnp.float32), axis=0)
        grad_project_weight = jnp.einsum(
            "td,te->de", entered, grad_projected, preferred_element_type=jnp.float32
        )
        grad_current = grad_sum1 + jnp.einsum(
            "te,de->td", grad_projected, w_project, preferred_element_type=jnp.float32
        )
        reduced = (
            lax.psum_scatter(grad_project_weight, "seq", scatter_dimension=0, tiled=True),
            lax.psum_scatter(grad_query_bias, "seq", scatter_dimension=0, tiled=True),
            lax.psum_scatter(grad_value_bias, "seq", scatter_dimension=0, tiled=True),
            lax.psum_scatter(grad_output_weight, "seq", scatter_dimension=0, tiled=True),
            lax.psum_scatter(grad_output_bias, "seq", scatter_dimension=0, tiled=True),
            lax.psum_scatter(grad_attention_gain, "seq", scatter_dimension=0, tiled=True),
            lax.psum_scatter(grad_attention_shift, "seq", scatter_dimension=0, tiled=True),
            lax.psum_scatter(grad_up_weight, "seq", scatter_dimension=0, tiled=True),
            lax.psum_scatter(grad_up_bias, "seq", scatter_dimension=0, tiled=True),
            lax.psum_scatter(grad_down_weight, "seq", scatter_dimension=0, tiled=True),
            lax.psum_scatter(grad_down_bias, "seq", scatter_dimension=0, tiled=True),
            lax.psum_scatter(grad_feed_gain, "seq", scatter_dimension=0, tiled=True),
            lax.psum_scatter(grad_feed_shift, "seq", scatter_dimension=0, tiled=True),
        )
        results[layer_index] = lax.psum(
            (
                reduced[0],
                reduced[1],
                reduced[2],
                reduced[3],
                reduced[4],
                reduced[5],
                reduced[6],
                reduced[7],
                reduced[8],
                reduced[9],
                reduced[10],
                reduced[11],
                reduced[12],
            ),
            "dp",
        )
    finals = tuple((layer_stack(results, slot) for slot in range(13)))
    (
        final_project,
        final_query,
        final_value,
        final_output_weight,
        final_output_bias,
        final_att_gain,
        final_att_shift,
        final_up_weight,
        final_up_bias,
        final_down_weight,
        final_down_bias,
        final_feed_gain,
        final_feed_shift,
    ) = finals
    return (
        output,
        grad_current.reshape(sequences, tokens, width),
        final_project,
        final_query,
        final_value,
        final_output_weight,
        final_output_bias,
        final_att_gain,
        final_att_shift,
        final_up_weight,
        final_up_bias,
        final_down_weight,
        final_down_bias,
        final_feed_gain,
        final_feed_shift,
    )


def solution(mesh):
    in_specs = (
        P("dp", "seq", None),
        P("dp", "seq"),
        P(None, ("dp", "seq"), None),
        P(None, ("dp", "seq")),
        P(None, ("dp", "seq")),
        P(None, ("dp", "seq"), None),
        P(None, ("dp", "seq")),
        P(None, ("dp", "seq")),
        P(None, ("dp", "seq")),
        P(None, ("dp", "seq"), None),
        P(None, ("dp", "seq")),
        P(None, ("dp", "seq"), None),
        P(None, ("dp", "seq")),
        P(None, ("dp", "seq")),
        P(None, ("dp", "seq")),
        P("dp", "seq", None),
    )
    out_specs = (
        P("dp", "seq", None),
        P("dp", "seq", None),
        P(None, "seq", None),
        P(None, "seq"),
        P(None, "seq"),
        P(None, "seq", None),
        P(None, "seq"),
        P(None, "seq"),
        P(None, "seq"),
        P(None, "seq", None),
        P(None, "seq"),
        P(None, "seq", None),
        P(None, "seq"),
        P(None, "seq"),
        P(None, "seq"),
    )
    return jax.shard_map(
        per_device, mesh=mesh, in_specs=in_specs, out_specs=out_specs, check_vma=False
    )
```

profile of v0, /device:TPU:0, one launch (start us, length us, event | category | flops | bytes accessed | tf_op | source)
XLA Modules:
  0.0 1925.3 jit_solution(10699492963418150292)
XLA Ops:
  9.0 65.2 %all-gather.53.cloned.1.call-done = bf16[1,768,2304]{2,1,0:T(8,128)(2,1)} async-done(((bf16[1,24,2304]{2,1,0:T(8,128)(2,1)}), bf16[1,768,2304]{2,1,0:T(8,128)(2,1)}) %all-gather.53.cloned.1.call-update) | async-done | bytes 3538960 | tf_op jit(solution)/shard_map/all_gather | solution.py:45
  94.4 40.7 %all-reduce.39 = (bf16[3072]{0:T(1024)(128)(2,1)}, bf16[3072]{0:T(1024)(128)(2,1)S(1)}, bf16[768]{0:T(1024)(128)(2,1)S(1)}, bf16[768]{0:T(1024)(128)(2,1)S(1)}, ...) all-reduce(bf16[3072]{0:T(1024)(128)(2,1)S(1)} %dynamic-update-slic, ...), channel_id=27, replica_groups=mesh['dp'=4,'seq'=8] {'dp','seq'}, use_global_device_ids=true, to_apply=%add.14 | all-reduce | flops 18432 | bytes 73728
  164.4 46.0 %while.96 = (s32[]{:T(128)}, f32[1,12,256]{2,1,0:T(8,128)S(1)}, f32[1,12,256]{2,1,0:T(8,128)}, s32[1,256]{1,0:T(1,128)}, s32[4,1,512]{2,1,0:T(1,128)}, /*index=5...) while((s32[]{:T(128)}, f32[1,12,256]{2,1,0:T(8,128)S(1)}, ...), condition=%wide.region_3.4_spmd.clone, body=%wide.region_0.3_spmd.clone.sunk | while | flops 214055936 | bytes 14945476 | solution.py:77
  226.1 25.7 %while.97 = (s32[]{:T(128)}, f32[1,256,12,64]{1,3,2,0:T(8,128)}, bf16[4,1,512,12,64]{2,4,3,1,0:T(8,128)(2,1)}, s32[1,256]{1,0:T(1,128)}, s32[4,1,512]{2,1,0:T(1,...) while((s32[]{:T(128)}, f32[1,256,12,64]{1,3,2,0:T(8,128)}, ...), condition=%wide.region_5.6_spmd.clone, body=%wide.region_4.5_spmd.clone.sunk | while | flops 409468928 | bytes 3825779 | solution.py:114
  258.2 32.9 %all-gather.61.cloned.1.call-done = bf16[1,768,3072]{2,1,0:T(8,128)(2,1)} async-done(((bf16[1,24,3072]{2,1,0:T(8,128)(2,1)}), bf16[1,768,3072]{2,1,0:T(8,128)(2,1)}) %all-gather.61.cloned.1.call-update) | async-done | bytes 4718608 | tf_op jit(solution)/shard_map/all_gather | solution.py:45
  297.6 58.8 %all-gather.63.cloned.1.call-done = bf16[1,3072,768]{2,1,0:T(8,128)(2,1)} async-done(((bf16[1,96,768]{2,1,0:T(8,128)(2,1)}), bf16[1,3072,768]{2,1,0:T(8,128)(2,1)}) %all-gather.63.cloned.1.call-update) | async-done | bytes 4718608 | tf_op jit(solution)/shard_map/all_gather | solution.py:45
  361.7 55.9 %all-gather.65.cloned.1.call-done = bf16[1,768,2304]{2,1,0:T(8,128)(2,1)} async-done(((bf16[1,24,2304]{2,1,0:T(8,128)(2,1)}), bf16[1,768,2304]{2,1,0:T(8,128)(2,1)}) %all-gather.65.cloned.1.call-update) | async-done | bytes 3538960 | tf_op jit(solution)/shard_map/all_gather | solution.py:45
  495.0 46.0 %while.98 = (s32[]{:T(128)}, f32[1,12,256]{2,1,0:T(8,128)S(1)}, f32[1,12,256]{2,1,0:T(8,128)}, s32[1,256]{1,0:T(1,128)}, s32[4,1,512]{2,1,0:T(1,128)}, /*index=5...) while((s32[]{:T(128)}, f32[1,12,256]{2,1,0:T(8,128)S(1)}, ...), condition=%wide.region_13.14_spmd.clone, body=%wide.region_10.13_spmd.clone.sunk | while | flops 214055936 | bytes 14945476 | solution.py:77
  556.9 25.3 %while.99 = (s32[]{:T(128)}, f32[1,256,12,64]{1,3,2,0:T(8,128)}, bf16[4,1,512,12,64]{2,4,3,1,0:T(8,128)(2,1)}, s32[1,256]{1,0:T(1,128)}, s32[4,1,512]{2,1,0:T(1,...) while((s32[]{:T(128)}, f32[1,256,12,64]{1,3,2,0:T(8,128)}, ...), condition=%wide.region_15.16_spmd.clone, body=%wide.region_14.15_spmd.clone.sunk | while | flops 409468928 | bytes 3825779 | solution.py:114
  588.7 52.5 %all-gather.73.cloned.1.call-done = bf16[1,768,3072]{2,1,0:T(8,128)(2,1)} async-done(((bf16[1,24,3072]{2,1,0:T(8,128)(2,1)}), bf16[1,768,3072]{2,1,0:T(8,128)(2,1)}) %all-gather.73.cloned.1.call-update) | async-done | bytes 4718608 | tf_op jit(solution)/shard_map/all_gather | solution.py:45
  647.8 58.3 %all-gather.75.cloned.1.call-done = bf16[1,3072,768]{2,1,0:T(8,128)(2,1)} async-done(((bf16[1,96,768]{2,1,0:T(8,128)(2,1)}), bf16[1,3072,768]{2,1,0:T(8,128)(2,1)}) %all-gather.75.cloned.1.call-update) | async-done | bytes 4718608 | tf_op jit(solution)/shard_map/all_gather | solution.py:45
  767.4 44.2 %while.100 = (s32[]{:T(128)}, f32[1,256,12,64]{1,3,2,0:T(8,128)}, bf16[4,1,512,12,64]{2,4,3,1,0:T(8,128)(2,1)S(1)}, s32[1,256]{1,0:T(1,128)S(1)}, s32[4,1,512]{2...) while((s32[]{:T(128)}, f32[1,256,12,64]{1,3,2,0:T(8,128)}, ...), condition=%wide.region_26.27_spmd.clone, body=%wide.region_25.26_spmd.clone.sunk | while | flops 613941248 | bytes 17604744 | solution.py:173
  825.7 77.1 %while.101 = (s32[]{:T(128)}, f32[1,256,12,64]{1,3,2,0:T(8,128)}, f32[1,256,12,64]{1,3,2,0:T(8,128)}, bf16[4,1,512,12,64]{2,4,3,1,0:T(8,128)(2,1)S(1)}, s32[4,1,...) while((s32[]{:T(128)}, f32[1,256,12,64]{1,3,2,0:T(8,128)}, ...), condition=%wide.region_28.29_spmd.clone, body=%wide.region_27.28_spmd.clone.sunk | while | flops 821952512 | bytes 26649240 | solution.py:243
  942.0 44.5 %while.102 = (s32[]{:T(128)}, f32[1,256,12,64]{1,3,2,0:T(8,128)}, bf16[4,1,512,12,64]{2,4,3,1,0:T(8,128)(2,1)S(1)}, s32[1,256]{1,0:T(1,128)S(1)}, s32[4,1,512]{2...) while((s32[]{:T(128)}, f32[1,256,12,64]{1,3,2,0:T(8,128)}, ...), condition=%wide.region_35.36_spmd.clone, body=%wide.region_34.35_spmd.clone.sunk | while | flops 613941248 | bytes 17604744 | solution.py:173
  1001.3 78.4 %while.103 = (s32[]{:T(128)}, f32[1,256,12,64]{1,3,2,0:T(8,128)}, f32[1,256,12,64]{1,3,2,0:T(8,128)}, bf16[4,1,512,12,64]{2,4,3,1,0:T(8,128)(2,1)S(1)}, s32[4,1,...) while((s32[]{:T(128)}, f32[1,256,12,64]{1,3,2,0:T(8,128)}, ...), condition=%wide.region_37.38_spmd.clone, body=%wide.region_36.37_spmd.clone.sunk | while | flops 821952512 | bytes 26649240 | solution.py:243
  1135.9 24.2 %reduce-scatter.25.cloned.1.call-done = f32[96,2304]{1,0:T(8,128)} async-done(((f32[768,2304]{1,0:T(8,128)}), f32[96,2304]{1,0:T(8,128)}) %reduce-scatter.25.cloned.1.call-update) | async-done | bytes 884752
  1162.7 43.7 %reduce-scatter.15.cloned.1.call-done = f32[96,768]{1,0:T(8,128)} async-done(((f32[768,768]{1,0:T(8,128)}), f32[96,768]{1,0:T(8,128)}) %reduce-scatter.15.cloned.1.call-update) | async-done | bytes 294928 | tf_op jit(solution)/shard_map/reduce_scatter | solution.py:466
  1206.4 46.1 %reduce-scatter.13.cloned.1.call-done = f32[96,768]{1,0:T(8,128)} async-done(((f32[768,768]{1,0:T(8,128)}), f32[96,768]{1,0:T(8,128)}) %reduce-scatter.13.cloned.1.call-update) | async-done | bytes 294928 | tf_op jit(solution)/shard_map/reduce_scatter | solution.py:466
  1252.6 80.4 %reduce-scatter.19.cloned.1.call-done = f32[96,3072]{1,0:T(8,128)} async-done(((f32[768,3072]{1,0:T(8,128)}), f32[96,3072]{1,0:T(8,128)}) %reduce-scatter.19.cloned.1.call-update) | async-done | bytes 1179664 | tf_op jit(solution)/shard_map/reduce_scatter | solution.py:470
  1332.9 80.3 %reduce-scatter.23.cloned.1.call-done = f32[384,768]{1,0:T(8,128)} async-done(((f32[3072,768]{1,0:T(8,128)}), f32[384,768]{1,0:T(8,128)}) %reduce-scatter.23.cloned.1.call-update) | async-done | bytes 1179664 | tf_op jit(solution)/shard_map/reduce_scatter | solution.py:472
  1413.3 80.4 %reduce-scatter.17.cloned.1.call-done = f32[96,3072]{1,0:T(8,128)} async-done(((f32[768,3072]{1,0:T(8,128)}), f32[96,3072]{1,0:T(8,128)}) %reduce-scatter.17.cloned.1.call-update) | async-done | bytes 1179664 | tf_op jit(solution)/shard_map/reduce_scatter | solution.py:470
  1493.6 80.2 %reduce-scatter.21.cloned.1.call-done = f32[384,768]{1,0:T(8,128)} async-done(((f32[3072,768]{1,0:T(8,128)}), f32[384,768]{1,0:T(8,128)}) %reduce-scatter.21.cloned.1.call-update) | async-done | bytes 1179664 | tf_op jit(solution)/shard_map/reduce_scatter | solution.py:472
  1579.9 57.0 %all-reduce.43.cloned.1.call-done = (f32[768]{0:T(1024)}, f32[768]{0:T(1024)}, f32[768]{0:T(1024)}, f32[768]{0:T(1024)}, f32[768]{0:T(1024)}, /*index=5*/f32[768...) async-done(((f32[768]{0:T(1024)}, f32[768]{0:T(1024)}, ...) | async-done | bytes 73744
  1679.2 230.1 %all-reduce.45.cloned.1.call-done = (f32[1,96,2304]{1,2,0:T(8,128)}, f32[1,96,2304]{1,2,0:T(8,128)}, f32[1,96,768]{2,1,0:T(8,128)}, f32[1,96,768]{2,1,0:T(8,128)...) async-done(((f32[1,96,2304]{1,2,0:T(8,128)}, f32[1,96,2304]{1,2,0:T(8,128)}, f32[1,96,768]{2,1,0:T(8,128)}, ...) | async-done | bytes 7077904 | tf_op jit(solution)/shard_map/psum | solution.py:477
  (778 shorter events, 820.0 us)
Async XLA Ops:
  9.0 145.5 %all-gather.57.cloned.1.call-start = ((), (), s32[]{:S(2)}) async-start(), calls=%async_computation.16 | async-start | bytes 3538944 | tf_op jit(solution)/shard_map/all_gather | solution.py:118
  78.3 132.1 %all-gather.55.cloned.1.call-start = ((), (), s32[]{:S(2)}) async-start(), calls=%async_computation.15 | async-start | bytes 3538944 | tf_op jit(solution)/shard_map/all_gather | solution.py:119
  135.9 118.5 %all-gather.59.cloned.1.call-start = ((), (), s32[]{:S(2)}) async-start(), calls=%async_computation.17 | async-start | bytes 1216512 | tf_op jit(solution)/shard_map/all_gather | solution.py:45
  136.7 154.3 %all-gather.61.cloned.1.call-start = ((), (), s32[]{:S(2)}) async-start(), calls=%async_computation.18 | async-start | bytes 4866048 | tf_op jit(solution)/shard_map/all_gather | solution.py:45
  137.6 218.8 %all-gather.63.cloned.1.call-start = ((), (), s32[]{:S(2)}) async-start(), calls=%async_computation.19 | async-start | bytes 4866048 | tf_op jit(solution)/shard_map/all_gather | solution.py:45
  138.4 279.2 %all-gather.65.cloned.1.call-start = ((), (), s32[]{:S(2)}) async-start(), calls=%async_computation.20 | async-start | bytes 3649536 | tf_op jit(solution)/shard_map/all_gather | solution.py:45
  139.1 311.9 %all-gather.81.cloned.1.call-start = ((), (), s32[]{:S(2)}) async-start(), calls=%async_computation.28 | async-start | bytes 3538944 | tf_op jit(solution)/shard_map/all_gather | solution.py:246
  154.1 331.0 %all-gather.69.cloned.1.call-start = ((), (), s32[]{:S(2)}) async-start(), calls=%async_computation.22 | async-start | bytes 3538944 | tf_op jit(solution)/shard_map/all_gather | solution.py:118
  421.6 119.4 %all-gather.67.cloned.1.call-start = ((), (), s32[]{:S(2)}) async-start(), calls=%async_computation.21 | async-start | bytes 3538944 | tf_op jit(solution)/shard_map/all_gather | solution.py:119
  422.6 161.5 %all-gather.71.cloned.1.call-start = ((), (), s32[]{:S(2)}) async-start(), calls=%async_computation.23 | async-start | bytes 1216512 | tf_op jit(solution)/shard_map/all_gather | solution.py:45
  423.4 217.9 %all-gather.73.cloned.1.call-start = ((), (), s32[]{:S(2)}) async-start(), calls=%async_computation.24 | async-start | bytes 4866048 | tf_op jit(solution)/shard_map/all_gather | solution.py:45
  423.9 282.1 %all-gather.75.cloned.1.call-start = ((), (), s32[]{:S(2)}) async-start(), calls=%async_computation.25 | async-start | bytes 4866048 | tf_op jit(solution)/shard_map/all_gather | solution.py:45
  424.7 327.1 %all-gather.77.cloned.1.call-start = ((), (), s32[]{:S(2)}) async-start(), calls=%async_computation.26 | async-start | bytes 3538944 | tf_op jit(solution)/shard_map/all_gather | solution.py:246
  438.6 375.6 %all-gather.79.cloned.1.call-start = ((), (), s32[]{:S(2)}) async-start(), calls=%async_computation.27 | async-start | bytes 3538944 | tf_op jit(solution)/shard_map/all_gather | solution.py:247
  740.1 249.0 %all-gather.83.cloned.1.call-start = ((), (), s32[]{:S(2)}) async-start(), calls=%async_computation.29 | async-start | bytes 3538944 | tf_op jit(solution)/shard_map/all_gather | solution.py:247
  923.1 210.3 %reduce-scatter.27.cloned.1.call-start = ((), (), s32[]{:S(2)}) async-start(), calls=%async_computation.31 | async-start | bytes 7962624
  986.5 173.6 %reduce-scatter.25.cloned.1.call-start = ((), (), s32[]{:S(2)}) async-start(), calls=%async_computation.30 | async-start | bytes 7962624
  1099.3 153.3 %reduce-scatter.13.cloned.1.call-start = ((), (), s32[]{:S(2)}) async-start(), calls=%async_computation.8 | async-start | bytes 2654208 | tf_op jit(solution)/shard_map/reduce_scatter | solution.py:466
  1101.3 231.6 %reduce-scatter.19.cloned.1.call-start = ((), (), s32[]{:S(2)}) async-start(), calls=%async_computation.11 | async-start | bytes 10616832 | tf_op jit(solution)/shard_map/reduce_scatter | solution.py:470
  1108.5 304.7 %reduce-scatter.23.cloned.1.call-start = ((), (), s32[]{:S(2)}) async-start(), calls=%async_computation.13 | async-start | bytes 10616832 | tf_op jit(solution)/shard_map/reduce_scatter | solution.py:472
  1115.1 378.5 %reduce-scatter.17.cloned.1.call-start = ((), (), s32[]{:S(2)}) async-start(), calls=%async_computation.10 | async-start | bytes 10616832 | tf_op jit(solution)/shard_map/reduce_scatter | solution.py:470
  1122.4 451.4 %reduce-scatter.21.cloned.1.call-start = ((), (), s32[]{:S(2)}) async-start(), calls=%async_computation.12 | async-start | bytes 10616832 | tf_op jit(solution)/shard_map/reduce_scatter | solution.py:472
  1129.0 507.9 %all-reduce.43.cloned.1.call-start = ((), (), s32[]{:S(2)}) async-start(), calls=%async_computation.32 | async-start | bytes 180224
  1133.3 776.1 %all-reduce.45.cloned.1.call-start = ((), (), s32[]{:S(2)}) async-start(), calls=%async_computation.33 | async-start | bytes 15335424 | tf_op jit(solution)/shard_map/psum | solution.py:477
  (154 other events, 2644.0 us)
Sparse Core Ops, SparseCore 0:
  11.5 62.7 all-gather.52
  78.4 31.6 all-gather.56
  136.1 32.3 all-gather.54
  171.2 53.9 all-gather.58
  228.5 62.4 all-gather.60
  294.4 61.9 all-gather.62
  359.3 58.3 all-gather.64
  419.5 31.4 all-gather.80
  452.9 32.1 all-gather.68
  486.8 32.1 all-gather.66
  522.0 53.9 all-gather.70
  578.7 62.5 all-gather.72
  644.1 61.9 all-gather.74
  740.6 32.1 all-gather.78
  986.7 64.0 reduce-scatter.26
  1096.4 63.6 reduce-scatter.24
  1164.0 42.3 reduce-scatter.14
  1210.2 42.3 reduce-scatter.12
  1256.1 76.8 reduce-scatter.18
  1336.4 76.8 reduce-scatter.22
  1416.8 76.8 reduce-scatter.16
  1497.0 76.8 reduce-scatter.20
  1579.6 57.1 all-reduce.42
  1640.2 269.0 all-reduce.44
  (2 shorter events, 62.1 us)
where the time goes:
time: 1940 us; the launch traced here: 1930 us
  waiting for transfers between devices  1070 us (55%)
  matrix products  372 us (19%)
  local copies, waits for them, and re-layouts  220 us (11%)
  other arithmetic  124 us (6%)
  blocking collectives  115 us (6%)
    all_gather x8, waiting for transfers between devices, fetch_forward(): lax.all_gather(as_sent(tuple((item[layer_index] for item in stacked))), (...  324 us
    psum x1, waiting for transfers between devices, per_device(): lax.psum((reduced[0], reduced[1], reduced[2], reduced[3], reduced[4], red...  230 us
    reduce_scatter x2, waiting for transfers between devices, per_device(): lax.psum_scatter(grad_up_weight, 'seq', scatter_dimension=0, tiled=True)  161 us
    reduce_scatter x2, waiting for transfers between devices, per_device(): lax.psum_scatter(grad_down_weight, 'seq', scatter_dimension=0, tiled=True)  161 us
    reduce_scatter x2, waiting for transfers between devices, per_device(): lax.psum_scatter(grad_output_weight, 'seq', scatter_dimension=0, tiled=True)  89.9 us
    unnamed x29, waiting for transfers between devices  84.1 us
    unnamed x316, local copies, waits for them, and re-layouts  82.6 us
    dot_general x8, matrix products, owner_inner_step(): jnp.einsum('hbt,bhd->thd', grad_scores, query_block, preferred_element_ty...  55.7 us
  transfers between devices with their start and end apart: 26, of which 17 were waited for; matrix products, arithmetic and copies ran while one was open for 30% of the time, Pallas kernels for 0%

commit v1 on v0

v1 whole, which is shorter than its diff:
```python
import functools
import math

import jax
import jax.numpy as jnp
from jax import lax
from jax.experimental import pallas as pl
from jax.experimental.pallas import tpu as pltpu
from jax.sharding import PartitionSpec as P

HEADS = 12
HEAD_DIM = 64
LAYERS = 2
EPSILON = 1e-12
MASKED = -2.0e9
LOWEST = -1.0e9
SCALE = HEAD_DIM**-0.5
BF16 = jnp.bfloat16
F32 = jnp.float32
VMEM_LIMIT = 58 * 1024 * 1024
RSQRT2 = 0.7071067811865476
PDF_SCALE = 0.3989422804014327


def nn(a, b):
    return lax.dot_general(a, b, (((1,), (0,)), ((), ())), preferred_element_type=F32)


def nt(a, b):
    return lax.dot_general(a, b, (((1,), (1,)), ((), ())), preferred_element_type=F32)


def tn(a, b):
    return lax.dot_general(a, b, (((0,), (0,)), ((), ())), preferred_element_type=F32)


def exchange(value, axis, size, mask):
    return lax.ppermute(value, axis, [(i, i ^ mask) for i in range(size)])


def resident(shape):
    return pl.BlockSpec(shape, lambda *unused: (0,) * len(shape))


def params(count=1):
    return pltpu.CompilerParams(
        dimension_semantics=("arbitrary",) * count, vmem_limit_bytes=VMEM_LIMIT
    )


SMEM_SPEC = pl.BlockSpec(memory_space=pltpu.SMEM)
ANY_SPEC = pl.BlockSpec(memory_space=pl.ANY)


def project_body(groups, span, order, x_ref, w_ref, b_ref, *rest):
    outs, flipped = rest[:groups], rest[groups]
    rows = nn(x_ref[...].astype(BF16), w_ref[...]) + b_ref[0]
    flipped[...] = rows.T.astype(BF16)
    for r in range(groups):
        start = pl.multiple_of(order[r] * span, span)
        outs[r][0] = flipped[pl.ds(start, span), :]


def project(order, rows, weight, bias, groups):
    tokens, width = rows.shape
    span = width // groups
    return pl.pallas_call(
        functools.partial(project_body, groups, span),
        out_shape=[jax.ShapeDtypeStruct((3, span, tokens), BF16)] * groups,
        grid=(3,),
        in_specs=[
            SMEM_SPEC,
            resident((tokens, width)),
            pl.BlockSpec((width, width), lambda j: (0, j)),
            pl.BlockSpec((1, 1, width), lambda j: (j, 0, 0)),
        ],
        out_specs=[pl.BlockSpec((1, span, tokens), lambda j: (j, 0, 0))] * groups,
        scratch_shapes=[pltpu.VMEM((width, tokens), BF16)],
        compiler_params=params(),
        cost_estimate=pl.CostEstimate(
            flops=6 * tokens * width * width, bytes_accessed=6 * width * width, transcendentals=0
        ),
        name="project",
    )(order, rows, weight, bias)


def load_stack(parts, stack, sems):
    copies = [pltpu.make_async_copy(part, stack.at[i], sems.at[i]) for i, part in enumerate(parts)]
    for copy in copies:
        copy.start()
    for copy in copies:
        copy.wait()


def attend_body(groups, members, heads, active, seg_row, seg_col, *rest):
    count = groups * members
    parts, rest = rest[:count], rest[count:]
    outs, rest = rest[:groups], rest[groups:]
    exact, log_total, stack, top, total, gathered, sems = rest
    load_stack(parts, stack, sems)
    tokens = stack.shape[-1]

    def one_block(r, unused):
        seg_query = seg_row[r]
        top[...] = jnp.full_like(top, LOWEST)
        total[...] = jnp.zeros_like(total)
        gathered[...] = jnp.zeros_like(gathered)

        def one_key(kb, unused):
            @pl.when(active[r, kb] != 0)
            def _():
                allowed = jnp.broadcast_to(seg_col[kb], (tokens, tokens)) == seg_query
                for h in range(heads):
                    part = pl.ds(h * HEAD_DIM, HEAD_DIM)
                    query = stack[r, 0, part, :] * SCALE
                    scores = tn(stack[kb, 1, part, :], query.astype(BF16))
                    scores = jnp.where(allowed, scores, MASKED)
                    old = top[h]
                    new = jnp.maximum(old, jnp.max(scores, axis=0, keepdims=True))
                    weights = jnp.exp(scores - new)
                    fade = jnp.exp(old - new)
                    total[h] = total[h] * fade + jnp.sum(weights, axis=0, keepdims=True)
                    top[h] = new
                    gathered[h] = gathered[h] * fade + nn(
                        stack[kb, 2, part, :], weights.astype(BF16)
                    )

            return unused

        lax.fori_loop(0, count, one_key, 0)
        for h in range(heads):
            exact[r, pl.ds(h * HEAD_DIM, HEAD_DIM), :] = gathered[h] / total[h]
            log_total[r, h] = top[h] + jnp.log(total[h])
        return unused

    lax.fori_loop(0, groups, one_block, 0)
    for r in range(groups):
        outs[r][...] = exact[r].astype(BF16)


def attend(active, seg_row, seg_col, parts, groups, members):
    unused, span, tokens = parts[0].shape
    heads = span // HEAD_DIM
    count = groups * members
    return pl.pallas_call(
        functools.partial(attend_body, groups, members, heads),
        out_shape=[jax.ShapeDtypeStruct((span, tokens), BF16)] * groups
        + [
            jax.ShapeDtypeStruct((groups, span, tokens), F32),
            jax.ShapeDtypeStruct((groups, heads, 1, tokens), F32),
        ],
        in_specs=[SMEM_SPEC, resident(seg_row.shape), resident(seg_col.shape)]
        + [ANY_SPEC] * count,
        out_specs=[resident((span, tokens))] * groups
        + [resident((groups, span, tokens)), resident((groups, heads, 1, tokens))],
        grid=(1,),
        scratch_shapes=[
            pltpu.VMEM((count, 3, span, tokens), BF16),
            pltpu.VMEM((heads, 1, tokens), F32),
            pltpu.VMEM((heads, 1, tokens), F32),
            pltpu.VMEM((heads, HEAD_DIM, tokens), F32),
            pltpu.SemaphoreType.DMA((count,)),
        ],
        compiler_params=params(),
        cost_estimate=pl.CostEstimate(
            flops=2 * span * groups * count * tokens * tokens,
            bytes_accessed=10 * span * tokens * count,
            transcendentals=heads * groups * count * tokens * tokens // 2,
        ),
        name="attend",
    )(active, seg_row, seg_col, *parts)


def attend_back_body(groups, members, heads, active, seg_row, seg_col, *rest):
    count = groups * members
    parts, rest = rest[:count], rest[count:]
    grads, rest = rest[:groups], rest[groups:]
    exact, log_total, rest = rest[0], rest[1], rest[2:]
    out_query, out_own, rest = rest[0], rest[1], rest[2:]
    out_send, rest = rest[: members - 1], rest[members - 1 :]
    stack, grad_stack, delta, grad_query, grad_kv, sems = rest
    load_stack(parts, stack, sems)
    tokens = stack.shape[-1]
    for r in range(groups):
        grad_stack[r] = grads[r][...]
    grad_kv[...] = jnp.zeros_like(grad_kv)

    def one_block(r, unused):
        seg_query = seg_row[r]
        grad_query[...] = jnp.zeros_like(grad_query)
        for h in range(heads):
            part = pl.ds(h * HEAD_DIM, HEAD_DIM)
            delta[h] = jnp.sum(
                grad_stack[r, part, :].astype(F32) * exact[r, part, :], axis=0, keepdims=True
            )

        def one_key(kb, unused):
            @pl.when(active[r, kb] != 0)
            def _():
                allowed = jnp.broadcast_to(seg_col[kb], (tokens, tokens)) == seg_query
                for h in range(heads):
                    part = pl.ds(h * HEAD_DIM, HEAD_DIM)
                    query = (stack[r, 0, part, :] * SCALE).astype(BF16)
                    grad = grad_stack[r, part, :]
                    keys = stack[kb, 1, part, :]
                    scores = jnp.where(allowed, tn(keys, query), MASKED)
                    weights = jnp.exp(scores - log_total[r, h])
                    grad_kv[kb, 1, part, :] += nt(grad, weights.astype(BF16))
                    grad_weights = tn(stack[kb, 2, part, :], grad)
                    grad_scores = (weights * (grad_weights - delta[h])).astype(BF16)
                    grad_kv[kb, 0, part, :] += nt(query, grad_scores)
                    grad_query[part, :] += nn(keys, grad_scores)

            return unused

        lax.fori_loop(0, count, one_key, 0)
        out_query[r] = (grad_query[...] * SCALE).astype(BF16)
        return unused

    lax.fori_loop(0, groups, one_block, 0)
    out_own[...] = grad_kv[:groups]
    for j in range(1, members):
        out_send[j - 1][...] = grad_kv[j * groups : (j + 1) * groups].astype(BF16)


def attend_back(active, seg_row, seg_col, parts, grads, exact, log_total, groups, members):
    unused, span, tokens = parts[0].shape
    heads = span // HEAD_DIM
    count = groups * members
    kv_shape = (groups, 2, span, tokens)
    return pl.pallas_call(
        functools.partial(attend_back_body, groups, members, heads),
        out_shape=[
            jax.ShapeDtypeStruct((groups, span, tokens), BF16),
            jax.ShapeDtypeStruct(kv_shape, F32),
        ]
        + [jax.ShapeDtypeStruct(kv_shape, BF16)] * (members - 1),
        in_specs=[SMEM_SPEC, resident(seg_row.shape), resident(seg_col.shape)]
        + [ANY_SPEC] * count
        + [resident((span, tokens))] * groups
        + [resident(exact.shape), resident(log_total.shape)],
        out_specs=[resident((groups, span, tokens)), resident(kv_shape)]
        + [resident(kv_shape)] * (members - 1),
        grid=(1,),
        scratch_shapes=[
            pltpu.VMEM((count, 3, span, tokens), BF16),
            pltpu.VMEM((groups, span, tokens), BF16),
            pltpu.VMEM((heads, 1, tokens), F32),
            pltpu.VMEM((span, tokens), F32),
            pltpu.VMEM((count, 2, span, tokens), F32),
            pltpu.SemaphoreType.DMA((count,)),
        ],
        compiler_params=params(),
        cost_estimate=pl.CostEstimate(
            flops=5 * span * groups * count * tokens * tokens,
            bytes_accessed=20 * span * tokens * count,
            transcendentals=heads * groups * count * tokens * tokens // 2,
        ),
        name="attend_back",
    )(active, seg_row, seg_col, *parts, *grads, exact, log_total)


OUT_BIAS, ATT_GAIN, ATT_SHIFT, DOWN_BIAS, FEED_GAIN, FEED_SHIFT = range(6)


def normalized(rows):
    centre = rows - jnp.mean(rows, axis=-1, keepdims=True)
    spread = jnp.mean(centre * centre, axis=-1, keepdims=True)
    inverse = lax.rsqrt(spread + EPSILON)
    return centre * inverse, inverse


def norm_back(grad, gain, normal, inverse):
    scaled = grad * gain
    mean_scaled = jnp.mean(scaled, axis=-1, keepdims=True)
    mean_both = jnp.mean(scaled * normal, axis=-1, keepdims=True)
    return inverse * (scaled - mean_scaled - normal * mean_both)


def feed_body(groups, span, blocks, order, x_ref, wo_ref, wu_ref, wd_ref, vec, ub_ref, *rest):
    contexts, rest = rest[:groups], rest[groups:]
    sum_first, hidden_low, sum_second, out, hidden, outward = rest
    j = pl.program_id(0)

    @pl.when(j == 0)
    def _():
        rows = x_ref[...] + vec[OUT_BIAS : OUT_BIAS + 1, :]
        for r in range(groups):
            start = pl.multiple_of(order[r] * span, span)
            rows += tn(contexts[r][...], wo_ref[pl.ds(start, span), :])
        sum_first[...] = rows
        normal, unused = normalized(rows)
        value = normal * vec[ATT_GAIN : ATT_GAIN + 1, :] + vec[ATT_SHIFT : ATT_SHIFT + 1, :]
        hidden[...] = value
        hidden_low[...] = value.astype(BF16)
        outward[...] = jnp.zeros_like(outward)

    inner = nn(hidden_low[...], wu_ref[...]) + ub_ref[0]
    activated = (0.5 * inner * (1.0 + lax.erf(inner * RSQRT2))).astype(BF16)
    outward[...] += nn(activated, wd_ref[...])

    @pl.when(j == blocks - 1)
    def _():
        rows = hidden[...] + outward[...] + vec[DOWN_BIAS : DOWN_BIAS + 1, :]
        sum_second[...] = rows
        normal, unused = normalized(rows)
        out[...] = normal * vec[FEED_GAIN : FEED_GAIN + 1, :] + vec[FEED_SHIFT : FEED_SHIFT + 1, :]


def feed(order, rows, w_output, w_up, w_down, vectors, up_bias, contexts):
    tokens, width = rows.shape
    groups, span = len(contexts), contexts[0].shape[0]
    blocks = w_up.shape[1] // width
    full = jax.ShapeDtypeStruct((tokens, width), F32)
    return pl.pallas_call(
        functools.partial(feed_body, groups, span, blocks),
        out_shape=[full, jax.ShapeDtypeStruct((tokens, width), BF16), full, full],
        grid=(blocks,),
        in_specs=[
            SMEM_SPEC,
            resident((tokens, width)),
            resident((width, width)),
            pl.BlockSpec((width, width), lambda j: (0, j)),
            pl.BlockSpec((width, width), lambda j: (j, 0)),
            resident(vectors.shape),
            pl.BlockSpec((1, 1, width), lambda j: (j, 0, 0)),
        ]
        + [resident((span, tokens))] * groups,
        out_specs=[resident((tokens, width))] * 4,
        scratch_shapes=[pltpu.VMEM((tokens, width), F32)] * 2,
        compiler_params=params(),
        cost_estimate=pl.CostEstimate(
            flops=(4 * blocks + 2) * tokens * width * width,
            bytes_accessed=(4 * blocks + 2) * width * width,
            transcendentals=0,
        ),
        name="feed",
    )(order, rows, w_output, w_up, w_down, vectors, up_bias, *contexts)


def feed_back_body(
    groups, span, blocks, devices, order, place, grad_ref, first_ref, second_ref, low_ref, *rest
):
    wo_ref, wu_ref, wd_ref, vec, ub_ref = rest[:5]
    contexts, rest = rest[5 : 5 + groups], rest[5 + groups :]
    own, send, grad_first, small = rest[:4]
    grad_contexts, rest = rest[4 : 4 + groups], rest[4 + groups :]
    grad_out, grad_hidden, tile = rest
    width = vec.shape[-1]
    me = place[0]
    j = pl.program_id(0)
    share = width // devices
    down_share = blocks * share
    per_block = width // down_share

    @pl.when(j == 0)
    def _():
        small[...] = jnp.zeros_like(small)
        grad = grad_ref[...]
        normal, inverse = normalized(second_ref[...])
        value = norm_back(grad, vec[FEED_GAIN : FEED_GAIN + 1, :], normal, inverse)
        grad_hidden[...] = value
        low = value.astype(BF16)
        grad_out[...] = low
        small[DOWN_BIAS : DOWN_BIAS + 1, :] = jnp.sum(low.astype(F32), axis=0, keepdims=True)
        small[FEED_GAIN : FEED_GAIN + 1, :] = jnp.sum(grad * normal, axis=0, keepdims=True)
        small[FEED_SHIFT : FEED_SHIFT + 1, :] = jnp.sum(grad, axis=0, keepdims=True)

    inner = nn(low_ref[...], wu_ref[...]) + ub_ref[0]
    below = 0.5 * (1.0 + lax.erf(inner * RSQRT2))
    activated = (inner * below).astype(BF16)
    slope = below + inner * (PDF_SCALE * jnp.exp(-0.5 * inner * inner))
    grad_inner = (nt(grad_out[...], wd_ref[...]) * slope).astype(BF16)
    small[pl.ds(8 + j, 1), :] = jnp.sum(grad_inner.astype(F32), axis=0, keepdims=True)
    grad_hidden[...] += nt(grad_inner, wu_ref[...])

    tile[...] = tn(activated, grad_out[...]).astype(BF16)
    for k in range(per_block):
        owner = (j * per_block + k) ^ me
        slot = lax.shift_right_logical(owner, 1)
        rows = pl.ds(k * down_share, down_share)

        @pl.when((owner & 1) == 0)
        def _():
            own[slot, pl.ds(0, down_share), :] = tile[rows, :]

        @pl.when((owner & 1) == 1)
        def _():
            send[slot, pl.ds(0, down_share), :] = tile[rows, :]

    tile[...] = tn(low_ref[...], grad_inner).astype(BF16)
    for i in range(devices // 2):
        for bit, target in ((0, own), (1, send)):
            start = pl.multiple_of((me ^ (2 * i + bit)) * share, share)
            base = pl.multiple_of(down_share + j * share, share)
            target[i, pl.ds(base, share), :] = tile[pl.ds(start, share), :]

    @pl.when(j == blocks - 1)
    def _():
        grad = grad_hidden[...]
        normal, inverse = normalized(first_ref[...])
        value = norm_back(grad, vec[ATT_GAIN : ATT_GAIN + 1, :], normal, inverse)
        grad_first[...] = value
        low = value.astype(BF16)
        small[OUT_BIAS : OUT_BIAS + 1, :] = jnp.sum(low.astype(F32), axis=0, keepdims=True)
        small[ATT_GAIN : ATT_GAIN + 1, :] = jnp.sum(grad * normal, axis=0, keepdims=True)
        small[ATT_SHIFT : ATT_SHIFT + 1, :] = jnp.sum(grad, axis=0, keepdims=True)
        for r in range(groups):
            start = pl.multiple_of(order[r] * span, span)
            tile[pl.ds(start, span), :] = nn(contexts[r][...], low).astype(BF16)
            grad_contexts[r][...] = nt(wo_ref[pl.ds(start, span), :], low).astype(BF16)
        for i in range(devices // 2):
            for bit, target in ((0, own), (1, send)):
                start = pl.multiple_of((me ^ (2 * i + bit)) * share, share)
                base = down_share + blocks * share
                target[i, base : base + share, :] = tile[pl.ds(start, share), :]


def feed_back(
    order, place, grad, first, second, low, w_output, w_up, w_down, vectors, up_bias, contexts, devices
):
    tokens, width = grad.shape
    groups, span = len(contexts), contexts[0].shape[0]
    blocks = w_up.shape[1] // width
    share = width // devices
    kept = (devices // 2, (2 * blocks + 1) * share, width)
    return pl.pallas_call(
        functools.partial(feed_back_body, groups, span, blocks, devices),
        out_shape=[
            jax.ShapeDtypeStruct(kept, BF16),
            jax.ShapeDtypeStruct(kept, BF16),
            jax.ShapeDtypeStruct((tokens, width), F32),
            jax.ShapeDtypeStruct((16, width), F32),
        ]
        + [jax.ShapeDtypeStruct((span, tokens), BF16)] * groups,
        grid=(blocks,),
        in_specs=[SMEM_SPEC, SMEM_SPEC]
        + [resident((tokens, width))] * 4
        + [
            resident((width, width)),
            pl.BlockSpec((width, width), lambda j: (0, j)),
            pl.BlockSpec((width, width), lambda j: (j, 0)),
            resident(vectors.shape),
            pl.BlockSpec((1, 1, width), lambda j: (j, 0, 0)),
        ]
        + [resident((span, tokens))] * groups,
        out_specs=[resident(kept), resident(kept), resident((tokens, width)), resident((16, width))]
        + [resident((span, tokens))] * groups,
        scratch_shapes=[
            pltpu.VMEM((tokens, width), BF16),
            pltpu.VMEM((tokens, width), F32),
            pltpu.VMEM((width, width), BF16),
        ],
        compiler_params=params(),
        cost_estimate=pl.CostEstimate(
            flops=(10 * blocks + 4) * tokens * width * width,
            bytes_accessed=(8 * blocks + 4) * width * width,
            transcendentals=0,
        ),
        name="feed_back",
    )(
        order,
        place,
        grad,
        first,
        second,
        low,
        w_output,
        w_up,
        w_down,
        vectors,
        up_bias,
        *contexts,
    )


def project_back_body(groups, span, devices, order, place, x_ref, grad_ref, w_ref, *rest):
    pieces, rest = rest[:groups], rest[groups:]
    own, send, out, small, joined, tile = rest
    width = w_ref.shape[0]
    me = place[0]
    j = pl.program_id(0)
    share = width // devices

    @pl.when(j == 0)
    def _():
        out[...] = grad_ref[...]
        small[...] = jnp.zeros_like(small)

    for r in range(groups):
        start = pl.multiple_of(order[r] * span, span)
        joined[pl.ds(start, span), :] = pieces[r][0]
    grad = joined[...].T
    small[pl.ds(j, 1), :] = jnp.sum(grad.astype(F32), axis=0, keepdims=True)
    out[...] += nt(grad, w_ref[...])
    tile[...] = tn(x_ref[...].astype(BF16), grad).astype(BF16)
    for i in range(devices // 2):
        for bit, target in ((0, own), (1, send)):
            start = pl.multiple_of((me ^ (2 * i + bit)) * share, share)
            base = pl.multiple_of(j * share, share)
            target[i, pl.ds(base, share), :] = tile[pl.ds(start, share), :]


def project_back(order, place, rows, grad, weight, pieces, devices):
    tokens, width = rows.shape
    groups, span = len(pieces), pieces[0].shape[1]
    kept = (devices // 2, 3 * (width // devices), width)
    return pl.pallas_call(
        functools.partial(project_back_body, groups, span, devices),
        out_shape=[
            jax.ShapeDtypeStruct(kept, BF16),
            jax.ShapeDtypeStruct(kept, BF16),
            jax.ShapeDtypeStruct((tokens, width), F32),
            jax.ShapeDtypeStruct((8, width), F32),
        ],
        grid=(3,),
        in_specs=[
            SMEM_SPEC,
            SMEM_SPEC,
            resident((tokens, width)),
            resident((tokens, width)),
            pl.BlockSpec((width, width), lambda j: (0, j)),
        ]
        + [pl.BlockSpec((1, span, tokens), lambda j: (j, 0, 0))] * groups,
        out_specs=[resident(kept), resident(kept), resident((tokens, width)), resident((8, width))],
        scratch_shapes=[pltpu.VMEM((width, tokens), BF16), pltpu.VMEM((width, width), BF16)],
        compiler_params=params(),
        cost_estimate=pl.CostEstimate(
            flops=12 * tokens * width * width, bytes_accessed=12 * width * width, transcendentals=0
        ),
        name="project_back",
    )(order, place, rows, grad, weight, *pieces)


class Stream:
    def __init__(self, steps):
        self.steps, self.result = steps, None
        self.flying = next(steps)

    def resume(self, arrived):
        try:
            self.flying = self.steps.send(arrived)
        except StopIteration as stop:
            self.flying, self.result = None, stop.value


def tick(streams, values=()):
    streams = [item for item in streams if item.flying is not None]
    values, flying = lax.optimization_barrier((values, [item.flying for item in streams]))
    for item, arrived in zip(streams, flying):
        item.resume(arrived)
    return values


def gather_steps(shard, devices, dp_size, masks):
    arrived = yield [exchange(shard, "dp", dp_size, m) for m in range(1, dp_size)]
    stack = jnp.stack([shard] + list(arrived))
    offsets = [(m, 0) for m in range(dp_size)]
    stacks = [stack]
    for mask in masks:
        (other,) = yield [exchange(stack, "seq", devices, mask)]
        offsets += [(d, q ^ mask) for d, q in offsets]
        stacks = [stack, other]
        stack = jnp.concatenate(stacks)
    arrived = yield [exchange(item, "seq", devices, 1) for item in stacks]
    offsets += [(d, q ^ 1) for d, q in offsets]
    return stacks + list(arrived), offsets


def sum_steps(own, send, devices, dp_size, dp_me):
    (arrived,) = yield [exchange(send, "seq", devices, 1)]
    rows, width = own.shape[1:]
    cut = rows // 2
    bits = int(math.log2(devices)) - 1
    masks = [2 << b for b in range(bits)]
    orders = (masks, masks[::-1])
    axes = [masks[::-1], masks[::-1]]
    kept = [
        add_low(own[:, part], arrived[:, part]).reshape((2,) * bits + (-1, width))
        for part in (slice(0, cut), slice(cut, rows))
    ]
    for step in range(bits):
        stay, leave = [], []
        for k in range(2):
            mask = orders[k][step]
            at = axes[k].index(mask)
            axes[k] = [m for m in axes[k] if m != mask]
            stay.append(lax.index_in_dim(kept[k], 0, at, keepdims=False))
            leave.append(
                exchange(lax.index_in_dim(kept[k], 1, at, keepdims=False), "seq", devices, mask)
            )
        leave = yield leave
        kept = [add_low(a, b) for a, b in zip(stay, leave)]
    total = jnp.concatenate(kept, axis=0)
    if dp_size != 4:
        return lax.psum(total, "dp")
    pieces = total.reshape(dp_size, rows // dp_size, width)

    def piece(m):
        return lax.dynamic_index_in_dim(pieces, dp_me ^ m, 0, keepdims=False)

    arrived = yield [exchange(piece(m), "dp", dp_size, m) for m in range(1, dp_size)]
    mine = sum((item.astype(F32) for item in arrived), piece(0).astype(F32)).astype(BF16)
    arrived = yield [exchange(mine, "dp", dp_size, m) for m in range(1, dp_size)]
    stack = [mine] + list(arrived)
    for bit in (1, 2):
        flip = (dp_me & bit) != 0
        stack = [jnp.where(flip, stack[i ^ bit], stack[i]) for i in range(dp_size)]
    return jnp.concatenate(stack, axis=0)


def vector_sum_steps(value, devices, dp_size):
    for axis, size in (("seq", devices), ("dp", dp_size)):
        for bit in range(int(math.log2(size))):
            (other,) = yield [exchange(value, axis, size, 1 << bit)]
            value = value + other
    return value


def add_low(a, b):
    return (a.astype(F32) + b.astype(F32)).astype(BF16)


def place_body(sources, layout, outs_count, table, *rest):
    parts, rest = rest[:sources], rest[sources:]
    outs, (buffer, in_sems, out_sems) = rest[:outs_count], rest[outs_count:]
    per = buffer.shape[0] // sources

    def into(a, k):
        i = a * per + k
        return pltpu.make_async_copy(parts[a].at[k], buffer.at[i], in_sems.at[i])

    def onward(a, k):
        i = a * per + k
        half = a * 2 // sources
        copies = []
        for at, (target, index, column, size, first) in enumerate(layout[half]):
            if index is None:
                goal = outs[target].at[table[i], :, pl.ds(first, size)]
            else:
                goal = outs[target].at[table[i], index]
            copies.append(
                pltpu.make_async_copy(
                    buffer.at[i, :, pl.ds(column, size)], goal, out_sems.at[i, at]
                )
            )
        return copies

    for a in range(sources):

        def begin(k, unused, a=a):
            into(a, k).start()
            return unused

        lax.fori_loop(0, per, begin, 0)
    for a in range(sources):

        def middle(k, unused, a=a):
            into(a, k).wait()
            for copy in onward(a, k):
                copy.start()
            return unused

        lax.fori_loop(0, per, middle, 0)
    for a in range(sources):

        def finish(k, unused, a=a):
            for copy in onward(a, k):
                copy.wait()
            return unused

        lax.fori_loop(0, per, finish, 0)


def put_in_place(first, second, layout, shapes, me, dp_me, devices):
    parts = first[0] + second[0]
    offsets = jnp.array(first[1] + second[1], jnp.int32)
    table = (dp_me ^ offsets[:, 0]) * devices + (me ^ offsets[:, 1])
    depth, columns = parts[0].shape[1:]
    count = len(first[1]) * 2
    most = max(len(item) for item in layout)
    size = 4 * count * depth * columns
    return pl.pallas_call(
        functools.partial(place_body, len(parts), layout, len(shapes)),
        out_shape=[jax.ShapeDtypeStruct(shape, BF16) for shape in shapes],
        in_specs=[SMEM_SPEC] + [ANY_SPEC] * len(parts),
        out_specs=[ANY_SPEC] * len(shapes),
        scratch_shapes=[
            pltpu.VMEM((count, depth, columns), BF16),
            pltpu.SemaphoreType.DMA((count,)),
            pltpu.SemaphoreType.DMA((count, most)),
        ],
        compiler_params=pltpu.CompilerParams(vmem_limit_bytes=VMEM_LIMIT),
        cost_estimate=pl.CostEstimate(flops=0, bytes_accessed=size, transcendentals=0),
        name="put_in_place",
    )(table, *parts)


def per_device(
    seq_size,
    dp_size,
    states,
    segment_ids,
    project_weight,
    query_bias,
    value_bias,
    output_weight,
    output_bias,
    attention_gain,
    attention_shift,
    up_weight,
    up_bias,
    down_weight,
    down_bias,
    feed_gain,
    feed_shift,
    cotangent,
):
    unused, tokens, width = states.shape
    groups = math.gcd(HEADS, seq_size)
    members = seq_size // groups
    share = width // seq_size
    inner_width = up_weight.shape[2]
    blocks = inner_width // width
    depth = width // (seq_size * dp_size)
    everyone = seq_size * dp_size
    me = lax.axis_index("seq")
    dp_me = lax.axis_index("dp")
    order = (me // members) ^ jnp.arange(groups, dtype=jnp.int32)
    place = me.reshape(1).astype(jnp.int32)
    both = ("dp", "seq")
    plain = depth % 8 != 0 or dp_size != 4

    vectors = jnp.stack(
        [
            output_bias,
            attention_gain,
            attention_shift,
            down_bias,
            feed_gain,
            feed_shift,
            query_bias,
            value_bias,
        ],
        axis=1,
    )
    flat = jnp.concatenate(
        [vectors.reshape(-1), up_bias.reshape(-1), segment_ids.astype(BF16).reshape(-1)]
    )
    used = flat.shape[0]
    flat = jnp.pad(flat, (0, -used % 1024)).reshape(-1, 128)

    def chunk_project(layer, half):
        cut = 3 * width // 2
        return project_weight[layer, :, half * cut : (half + 1) * cut]

    def chunk_rest(layer, half):
        cut = down_weight.shape[1] // 2
        down = down_weight[layer, half * cut : (half + 1) * cut]
        return jnp.concatenate(
            [
                output_weight[layer, :, half * (width // 2) : (half + 1) * (width // 2)],
                up_weight[layer, :, half * (inner_width // 2) : (half + 1) * (inner_width // 2)],
            ]
            + [down[t * depth : (t + 1) * depth] for t in range(blocks // 2)],
            axis=1,
        )

    masks = [2 << b for b in range(int(math.log2(seq_size)) - 1)]

    def gather(chunk, half=0):
        return Stream(gather_steps(chunk, seq_size, dp_size, masks[::-1] if half else masks))

    def project_streams(layer):
        return [gather(chunk_project(layer, half), half) for half in range(2)]

    def rest_streams(layer):
        return [gather(chunk_rest(layer, half), half) for half in range(2)]

    def placed_project(streams):
        cut = 3 * width // 2
        layout = [[(0, None, 0, cut, half * cut)] for half in range(2)]
        (made,) = put_in_place(
            streams[0].result,
            streams[1].result,
            layout,
            [(everyone, depth, 3 * width)],
            me,
            dp_me,
            seq_size,
        )
        return made.reshape(width, 3 * width)

    def placed_rest(streams):
        a, b = width // 2, inner_width // 2
        layout = [
            [(0, None, 0, a, half * a), (1, None, a, b, half * b)]
            + [
                (2, half * (blocks // 2) + t, a + b + t * width, width, 0)
                for t in range(blocks // 2)
            ]
            for half in range(2)
        ]
        w_output, w_up, w_down = put_in_place(
            streams[0].result,
            streams[1].result,
            layout,
            [
                (everyone, depth, width),
                (everyone, depth, inner_width),
                (everyone, blocks, depth, width),
            ],
            me,
            dp_me,
            seq_size,
        )
        return (
            w_output.reshape(width, width),
            w_up.reshape(width, inner_width),
            w_down.reshape(inner_width, width),
        )

    def swap_groups(items):
        return [items[0]] + [
            exchange(items[r], "seq", seq_size, r * members) for r in range(1, groups)
        ]

    def with_members(items):
        items = list(items)
        own = list(items)
        for j in range(1, members):
            items += [exchange(item, "seq", seq_size, j) for item in own]
        return items

    w_project, w_rest = [None] * LAYERS, [None] * LAYERS
    if plain:
        table = lax.all_gather(flat, both, axis=0, tiled=False)
        for layer in range(LAYERS):
            w_project[layer] = lax.all_gather(project_weight[layer], both, axis=0, tiled=True)
            w_rest[layer] = tuple(
                lax.all_gather(item[layer], both, axis=0, tiled=True)
                for item in (output_weight, up_weight, down_weight)
            )
        projects = rests = [[]] * LAYERS
    else:
        small = gather(flat)
        projects, rests = [project_streams(0), None], [None, None]
        first = projects[0] + [small]
        tick(first)
        rests[0] = rest_streams(0)
        tick(first)
        tick(first)
        tick(rests[0])
        tick(first)
        stacks, offsets = small.result
        offsets = jnp.array(offsets, jnp.int32)
        where = {pair: i for i, pair in enumerate(small.result[1])}
        lookup = jnp.array(
            [where[(d, q)] for d in range(dp_size) for q in range(seq_size)], jnp.int32
        )
        wanted = jnp.arange(everyone, dtype=jnp.int32) ^ (dp_me * seq_size + me)
        table = jnp.take(jnp.concatenate(stacks), jnp.take(lookup, wanted), axis=0)

    table = table.reshape(everyone, -1)
    small_rows = LAYERS * 8 * depth
    up_share = inner_width // everyone
    vectors = (
        table[:, :small_rows]
        .reshape(everyone, LAYERS, 8, depth)
        .transpose(1, 2, 0, 3)
        .reshape(LAYERS, 8, width)
        .astype(F32)
    )
    up_biases = (
        table[:, small_rows : small_rows + LAYERS * up_share]
        .reshape(everyone, LAYERS, up_share)
        .transpose(1, 0, 2)
        .reshape(LAYERS, blocks, 1, width)
        .astype(F32)
    )
    relative = jnp.array([r * members + j for j in range(members) for r in range(groups)], jnp.int32)
    segments = jnp.take(
        table[:, used - tokens : used], dp_me * seq_size + (me ^ relative), axis=0
    ).astype(jnp.int32)
    first_id, last_id = segments[:, 0], segments[:, -1]
    active = (
        (first_id[:groups, None] <= last_id[None, :])
        & (first_id[None, :] <= last_id[:groups, None])
    ).astype(jnp.int32)
    seg_row = segments[:groups, None, :]
    seg_col = segments[:, :, None]

    def projected(layer, current):
        vec = vectors[layer]
        bias = jnp.stack([vec[6], jnp.zeros_like(vec[6]), vec[7]])[:, None, :]
        return project(order, current, w_project[layer], bias, groups)

    current = states[0].astype(F32)
    saved = []
    for layer in range(LAYERS):
        last = layer == LAYERS - 1
        if not plain:
            w_project[layer] = placed_project(projects[layer])
        made = projected(layer, current)
        parts = with_members(swap_groups(made))
        parts = tick(rests[layer], tuple(parts))
        if not plain and not last:
            projects[layer + 1] = project_streams(layer + 1)
            rests[layer + 1] = rest_streams(layer + 1)
        *mixed, exact, log_total = attend(active, seg_row, seg_col, parts, groups, members)
        contexts = tuple(swap_groups(mixed))
        ahead = [] if plain or last else projects[layer + 1]
        contexts = tick(rests[layer] + ahead, contexts)
        contexts = tick(rests[layer] + ahead, contexts)
        if not plain:
            w_rest[layer] = placed_rest(rests[layer])
        w_output, w_up, w_down = w_rest[layer]
        sum_first, low, sum_second, following = feed(
            order,
            current,
            w_output,
            w_up,
            w_down,
            vectors[layer],
            up_biases[layer],
            contexts,
        )
        saved.append((current, parts, exact, log_total, contexts, sum_first, low, sum_second))
        current = following
        if not plain and not last:
            current = tick(ahead + rests[layer + 1], current)
            current = tick(ahead, current)
    output = current.astype(BF16)[None]

    grad = cotangent[0].astype(F32)
    smalls = [None] * LAYERS
    feeds, backs = [None] * LAYERS, [None] * LAYERS
    behind = []
    for layer in reversed(range(LAYERS)):
        w_output, w_up, w_down = w_rest[layer]
        entered, parts, exact, log_total, contexts, sum_first, low, sum_second = saved[layer]
        own, send, grad_first, small_feed, *grad_mixed = feed_back(
            order,
            place,
            grad,
            sum_first,
            sum_second,
            low,
            w_output,
            w_up,
            w_down,
            vectors[layer],
            up_biases[layer],
            contexts,
            seq_size,
        )
        grad_mixed = tick(behind, tuple(grad_mixed))
        feeds[layer] = Stream(sum_steps(own, send, seq_size, dp_size, dp_me))
        grads = tuple(swap_groups(grad_mixed))
        grads = tick(behind + [feeds[layer]], grads)
        grad_query, kept_kv, *sent_kv = attend_back(
            active, seg_row, seg_col, parts, grads, exact, log_total, groups, members
        )
        for j in range(1, members):
            kept_kv = kept_kv + exchange(sent_kv[j - 1], "seq", seq_size, j).astype(F32)
        messages = [
            jnp.concatenate([grad_query[r][None], kept_kv[r].astype(BF16)], axis=0)
            for r in range(groups)
        ]
        messages = tick(behind, tuple(messages))
        pieces = tuple(swap_groups(messages))
        pieces = tick(behind + [feeds[layer]], pieces)
        own, send, grad, small_project = project_back(
            order, place, entered, grad_first, w_project[layer], pieces, seq_size
        )
        backs[layer] = Stream(sum_steps(own, send, seq_size, dp_size, dp_me))
        behind = [feeds[layer], backs[layer]]
        smalls[layer] = jnp.concatenate(
            [small_feed[:6], small_feed[8 : 8 + blocks], small_project[0:1], small_project[2:3]],
            axis=0,
        )
    vector_sum = Stream(vector_sum_steps(jnp.stack(smalls), seq_size, dp_size))
    behind = feeds + backs + [vector_sum]
    while any(item.flying is not None for item in behind):
        tick(behind)
    small = vector_sum.result
    results = [(feeds[layer].result, backs[layer].result) for layer in range(LAYERS)]

    def mine(rows, size):
        return lax.dynamic_slice_in_dim(rows, me * size, size, axis=1)

    def columns(part, which):
        return jnp.concatenate([part[i * share : (i + 1) * share] for i in which], axis=1).astype(F32)

    down_rows = blocks * share
    g_project = jnp.stack([columns(item[1], range(3)) for item in results])
    g_up = jnp.stack([columns(item[0], range(blocks, 2 * blocks)) for item in results])
    g_down = jnp.stack([item[0][:down_rows].astype(F32) for item in results])
    g_output = jnp.stack([item[0][down_rows + blocks * share :].astype(F32) for item in results])
    wide = small[:, 6 : 6 + blocks].reshape(LAYERS, blocks * width)
    return (
        output,
        grad[None],
        g_project,
        mine(small[:, 6 + blocks], share),
        mine(small[:, 7 + blocks], share),
        g_output,
        mine(small[:, OUT_BIAS], share),
        mine(small[:, ATT_GAIN], share),
        mine(small[:, ATT_SHIFT], share),
        g_up,
        mine(wide, blocks * share),
        g_down,
        mine(small[:, DOWN_BIAS], share),
        mine(small[:, FEED_GAIN], share),
        mine(small[:, FEED_SHIFT], share),
    )


def solution(mesh):
    row, spread = P("dp", "seq", None), ("dp", "seq")
    matrix, vector = P(None, spread, None), P(None, spread)
    in_specs = (
        row,
        P("dp", "seq"),
        matrix,
        vector,
        vector,
        matrix,
        vector,
        vector,
        vector,
        matrix,
        vector,
        matrix,
        vector,
        vector,
        vector,
        row,
    )
    kept, line = P(None, "seq", None), P(None, "seq")
    out_specs = (row, row, kept, line, line, kept, line, line, line, kept, line, kept, line, line, line)
    return jax.shard_map(
        functools.partial(per_device, mesh.shape["seq"], mesh.shape["dp"]),
        mesh=mesh,
        in_specs=in_specs,
        out_specs=out_specs,
        check_vma=False,
    )
```

time: 1940 us -> 751 us (0.39)
  waiting for transfers between devices: 1070 us -> 246 us
  matrix products: 372 us -> 0 us
  Pallas kernels: 0 us -> 192 us
  starting transfers between devices: 1.61 us -> 170 us
  local copies, waits for them, and re-layouts: 220 us -> 69 us
  blocking collectives: 115 us -> 0 us
  other arithmetic: 124 us -> 59.3 us
    reduce_scatter x6 -> x0, waiting for transfers between devices: 411 us -> none  [the longest x2 161 us: per_device(): lax.psum_scatter(grad_up_weight, 'seq', scatter_dimension=0, tiled=True)]
    dot_general x79 -> x0, matrix products: 367 us -> none  [the longest x8 55.7 us: owner_inner_step(): jnp.einsum('hbt,bhd->thd', grad_scores, query_block, preferred_element_ty...]
    all_gather x16 -> x0, waiting for transfers between devices: 348 us -> none  [the longest x8 324 us: fetch_forward(): lax.all_gather(as_sent(tuple((item[layer_index] for item in stacked))), (...]
    ppermute x0 -> x146, waiting for transfers between devices: none -> 246 us  [exchange(): return lax.ppermute(value, axis, [(i, i ^ mask) for i in range(size)])]
    psum x1 -> x0, waiting for transfers between devices: 230 us -> none  [per_device(): lax.psum((reduced[0], reduced[1], reduced[2], reduced[3], reduced[4], red...]
    pallas_call x0 -> x16, Pallas kernels: none -> 192 us  [the longest x2 40.5 us: attend_back(): pl.pallas_call(functools.partial(attend_back_body, groups, members, heads...]
    ppermute x0 -> x146, starting transfers between devices: none -> 170 us  [exchange(): return lax.ppermute(value, axis, [(i, i ^ mask) for i in range(size)])]
    unnamed x29 -> x0, waiting for transfers between devices: 84.1 us -> none
  transfers between devices with their start and end apart: 26 -> 146, of which waited for: 17 -> 46; matrix products, arithmetic and copies ran while one was open for 30% -> 14% of each run, Pallas kernels for 0% -> 14%
where the time goes in v1:
time: 751 us; the launch traced here: 739 us
  waiting for transfers between devices  246 us (33%)
  Pallas kernels  192 us (26%)
  starting transfers between devices  170 us (23%)
  local copies, waits for them, and re-layouts  69 us (9%)
  other arithmetic  59.3 us (8%)
    ppermute x146, waiting for transfers between devices, exchange(): return lax.ppermute(value, axis, [(i, i ^ mask) for i in range(size)])  246 us
    ppermute x146, starting transfers between devices, exchange(): return lax.ppermute(value, axis, [(i, i ^ mask) for i in range(size)])  170 us
    pallas_call x2, Pallas kernels, attend_back(): pl.pallas_call(functools.partial(attend_back_body, groups, members, heads...  40.5 us
    pallas_call x2, Pallas kernels, feed_back(): pl.pallas_call(functools.partial(feed_back_body, groups, span, blocks, de...  38.4 us
    pallas_call x2, Pallas kernels, attend(): pl.pallas_call(functools.partial(attend_body, groups, members, heads), ou...  34.3 us
    pallas_call x4, Pallas kernels, put_in_place(): pl.pallas_call(functools.partial(place_body, len(parts), layout, len(shap...  34 us
    unnamed x225, local copies, waits for them, and re-layouts  30.7 us
    convert_element_type x20, other arithmetic, add_low(): return (a.astype(F32) + b.astype(F32)).astype(BF16)  24.9 us
  transfers between devices with their start and end apart: 146, of which 46 were waited for; matrix products, arithmetic and copies ran while one was open for 14% of the time, Pallas kernels for 14%

profile of v1, /device:TPU:0, one launch (start us, length us, event | category | flops | bytes accessed | tf_op | source)
XLA Modules:
  0.0 739.1 jit_solution(13077544459766273469)
XLA Ops:
  57.6 7.4 collective-permute-done.4
  142.5 17.0 %attend.2 = (bf16[192,256]{1,0:T(8,128)(2,1)}, bf16[192,256]{1,0:T(8,128)(2,1)}, bf16[192,256]{1,0:T(8,128)(2,1)}, bf16[192,256]{1,0:T(8,128)(2,1)}, f32[4,192,256]{2,1,0:T(8,128)}, /*index=5*/f32[4,3,1,256]{3,2,1,0:T(1,128)}) custom-call(s32[4,8]{1,0:T(4,128)} %and_convert_fusion.active, s32[4,1,256]{2,1,0:T(1,128)} %broadcast_in_dim.60.seg_row, ...), custom_call_target="tpu_custom_call" | custom-call | flops 805306368 | bytes 3932160 | tf_op jit(solution)/shard_map/attend/pallas_call | solution.py:145
  187.0 11.6 %put_in_place.5 = (bf16[32,24,768]{2,1,0:T(8,128)(2,1)}, bf16[32,24,3072]{2,1,0:T(8,128)(2,1)}, bf16[32,4,24,768]{3,2,1,0:T(8,128)(2,1)}) custom-call(s32[64]{0:T(128)} %add_bitcast_fusion.table, bf16[8,24,3456]{2,1,0:T(8,128)(2,1)} %constant_dynamic-update-slice_fusion.31.rest_0_, bf16[8,24,3456]{2,1,0:T(8,128)(2,1)} %collective-permute-done.39.rest_1_, ...), custom_call_target="tpu_custom_call" | custom-call | bytes 21233664 | tf_op jit(solution)/shard_map/put_in_place/pallas_call | solution.py:683
  203.1 10.1 %feed.2 = (f32[256,768]{1,0:T(8,128)}, bf16[256,768]{1,0:T(8,128)(2,1)}, f32[256,768]{1,0:T(8,128)}, f32[256,768]{1,0:T(8,128)}) custom-call(s32[4]{0:T(128)} %iota_xor_fusion.order, f32[256,768]{1,0:T(8,128)} %bitcast_convert_fusion.1.x_ref, bf16[768,768]{1,0:T(8,128)(2,1)} %bitcast.425, bf16[768,3072]{1,0:T(8,128)(2,1)} %bitcast.407, ...), custom_call_target="tpu_custom_call" | custom-call | flops 2717908992 | bytes 10616832 | tf_op jit(solution)/shard_map/feed/pallas_call | solution.py:315
  249.2 17.3 %attend.3 = (bf16[192,256]{1,0:T(8,128)(2,1)}, bf16[192,256]{1,0:T(8,128)(2,1)}, bf16[192,256]{1,0:T(8,128)(2,1)}, bf16[192,256]{1,0:T(8,128)(2,1)}, f32[4,192,256]{2,1,0:T(8,128)}, /*index=5*/f32[4,3,1,256]{3,2,1,0:T(1,128)}) custom-call(s32[4,8]{1,0:T(4,128)} %and_convert_fusion.active, s32[4,1,256]{2,1,0:T(1,128)} %broadcast_in_dim.60.seg_row, ...), custom_call_target="tpu_custom_call" | custom-call | flops 805306368 | bytes 3932160 | tf_op jit(solution)/shard_map/attend/pallas_call | solution.py:145
  270.1 12.7 %collective-permute-done.74.rest_1_.rest_6_ = bf16[192,256]{1,0:T(8,128)(2,1)S(1)} collective-permute-done((bf16[192,256]{1,0:T(8,128)(2,1)}, bf16[192,256]{1,0:T(8,128)(2,1)S(1)}, u32[]{:S(2)}, u32[]{:S(2)}) %collective-permute-start.74) | collective-permute-done | bytes 98336 | tf_op jit(solution)/shard_map/ppermute | solution.py:38
  291.7 11.4 %put_in_place.7 = (bf16[32,24,768]{2,1,0:T(8,128)(2,1)}, bf16[32,24,3072]{2,1,0:T(8,128)(2,1)}, bf16[32,4,24,768]{3,2,1,0:T(8,128)(2,1)}) custom-call(s32[64]{0:T(128)} %add_bitcast_fusion.table, bf16[8,24,3456]{2,1,0:T(8,128)(2,1)} %copy-done.7, bf16[8,24,3456]{2,1,0:T(8,128)(2,1)} %collective-permute-done.77.rest_1_, ...), custom_call_target="tpu_custom_call" | custom-call | bytes 21233664 | tf_op jit(solution)/shard_map/put_in_place/pallas_call | solution.py:683
  303.2 10.1 %feed.3 = (f32[256,768]{1,0:T(8,128)}, bf16[256,768]{1,0:T(8,128)(2,1)}, f32[256,768]{1,0:T(8,128)}, f32[256,768]{1,0:T(8,128)}) custom-call(s32[4]{0:T(128)} %iota_xor_fusion.order, f32[256,768]{1,0:T(8,128)} %get-tuple-element.331.x_ref, bf16[768,768]{1,0:T(8,128)(2,1)} %bitcast.427, bf16[768,3072]{1,0:T(8,128)(2,1)} %bitcast.411, ...), custom_call_target="tpu_custom_call" | custom-call | flops 2717908992 | bytes 10616832 | tf_op jit(solution)/shard_map/feed/pallas_call | solution.py:315
  313.3 19.3 %feed_back.2 = (bf16[4,864,768]{2,1,0:T(8,128)(2,1)}, bf16[4,864,768]{2,1,0:T(8,128)(2,1)}, f32[256,768]{1,0:T(8,128)}, f32[16,768]{1,0:T(8,128)}, bf16[192,256]...) custom-call(s32[4]{0:T(128)} %iota_xor_fusion.order, ...), custom_call_target="tpu_custom_call" | custom-call | flops 6643777536 | bytes 21233664 | tf_op jit(solution)/shard_map/feed_back/pallas_call | solution.py:427
  341.8 20.3 %attend_back.2 = (bf16[4,192,256]{2,1,0:T(8,128)(2,1)}, f32[4,2,192,256]{3,2,1,0:T(8,128)}, bf16[4,2,192,256]{3,2,1,0:T(8,128)(2,1)}) custom-call(s32[4,8]{1,0:T(4,128)} %and_convert_fusion.active, s32[4,1,256]{2,1,0:T(1,128)} %broadcast_in_dim.60.seg_row, s32[8,256,1]{2,1,0:T(8,128)} %select_convert_fusion.seg_col, ...), custom_call_target="tpu_custom_call" | custom-call | flops 2013265920 | bytes 7864320 | tf_op jit(solution)/shard_map/attend_back/pallas_call | solution.py:231
  374.5 31.1 %collective-permute-done.88.rest_1_ = bf16[3,192,256]{2,1,0:T(8,128)(2,1)S(1)} collective-permute-done((bf16[3,192,256]{2,1,0:T(8,128)(2,1)S(1)}, bf16[3,192,256]{2,1,0:T(8,128)(2,1)S(1)}, u32[]{:S(2)}, u32[]{:S(2)}) %collective-permute-start.88) | collective-permute-done | bytes 294944 | tf_op jit(solution)/shard_map/ppermute | solution.py:38
  414.2 7.5 %project_back.2 = (bf16[4,288,768]{2,1,0:T(8,128)(2,1)}, bf16[4,288,768]{2,1,0:T(8,128)(2,1)}, f32[256,768]{1,0:T(8,128)}, f32[8,768]{1,0:T(8,128)}) custom-call(s32[4]{0:T(128)} %iota_xor_fusion.order, s32[1]{0:T(128)} %bitcast.84.place, f32[256,768]{1,0:T(8,128)} %get-tuple-element.331.x_ref, f32[256,768]{1,0:T(8,128)} %get-tuple-element.381.grad_ref, ...), custom_call_target="tpu_custom_call" | custom-call | flops 1811939328 | bytes 7077888 | tf_op jit(solution)/shard_map/project_back/pallas_call | solution.py:508
  421.7 19.1 %feed_back.3 = (bf16[4,864,768]{2,1,0:T(8,128)(2,1)}, bf16[4,864,768]{2,1,0:T(8,128)(2,1)}, f32[256,768]{1,0:T(8,128)}, f32[16,768]{1,0:T(8,128)}, bf16[192,256]...) custom-call(s32[4]{0:T(128)} %iota_xor_fusion.order, ...), custom_call_target="tpu_custom_call" | custom-call | flops 6643777536 | bytes 21233664 | tf_op jit(solution)/shard_map/feed_back/pallas_call | solution.py:427
  447.1 13.0 %collective-permute-done.93 = bf16[432,768]{1,0:T(8,128)(2,1)} collective-permute-done((bf16[432,768]{1,0:T(8,128)(2,1)S(1)}, bf16[432,768]{1,0:T(8,128)(2,1)}, u32[]{:S(2)}, u32[]{:S(2)}) %collective-permute-start.93) | collective-permute-done | bytes 663584 | tf_op jit(solution)/shard_map/ppermute | solution.py:38
  477.0 8.3 %collective-permute-done.98.rest_11_ = bf16[192,256]{1,0:T(8,128)(2,1)S(1)} collective-permute-done((bf16[192,256]{1,0:T(8,128)(2,1)S(1)}, bf16[192,256]{1,0:T(8,128)(2,1)S(1)}, u32[]{:S(2)}, u32[]{:S(2)}) %collective-permute-start.98) | collective-permute-done | bytes 98336 | tf_op jit(solution)/shard_map/ppermute | solution.py:38
  489.6 18.9 %collective-permute-done.100 = bf16[216,768]{1,0:T(8,128)(2,1)} collective-permute-done((bf16[216,768]{1,0:T(8,128)(2,1)}, bf16[216,768]{1,0:T(8,128)(2,1)}, u32[]{:S(2)}, u32[]{:S(2)}) %collective-permute-start.100) | collective-permute-done | bytes 331808 | tf_op jit(solution)/shard_map/ppermute | solution.py:38
  519.2 20.2 %attend_back.3 = (bf16[4,192,256]{2,1,0:T(8,128)(2,1)}, f32[4,2,192,256]{3,2,1,0:T(8,128)}, bf16[4,2,192,256]{3,2,1,0:T(8,128)(2,1)}) custom-call(s32[4,8]{1,0:T(4,128)} %and_convert_fusion.active, s32[4,1,256]{2,1,0:T(1,128)} %broadcast_in_dim.60.seg_row, s32[8,256,1]{2,1,0:T(8,128)} %select_convert_fusion.seg_col, ...), custom_call_target="tpu_custom_call" | custom-call | flops 2013265920 | bytes 7864320 | tf_op jit(solution)/shard_map/attend_back/pallas_call | solution.py:231
  576.8 17.2 %collective-permute-done.111.rest_1_ = bf16[3,192,256]{2,1,0:T(8,128)(2,1)S(1)} collective-permute-done((bf16[3,192,256]{2,1,0:T(8,128)(2,1)S(1)}, bf16[3,192,256]{2,1,0:T(8,128)(2,1)S(1)}, u32[]{:S(2)}, u32[]{:S(2)}) %collective-permute-start.111) | collective-permute-done | bytes 294944 | tf_op jit(solution)/shard_map/ppermute | solution.py:38
  594.1 7.7 %collective-permute-done.112.rest_2_ = bf16[3,192,256]{2,1,0:T(8,128)(2,1)S(1)} collective-permute-done((bf16[3,192,256]{2,1,0:T(8,128)(2,1)}, bf16[3,192,256]{2,1,0:T(8,128)(2,1)S(1)}, u32[]{:S(2)}, u32[]{:S(2)}) %collective-permute-start.112) | collective-permute-done | bytes 294944 | tf_op jit(solution)/shard_map/ppermute | solution.py:38
  605.6 7.3 project_back.3
  641.0 7.3 collective-permute-done.131
  653.5 10.5 %collective-permute-done.127 = bf16[216,768]{1,0:T(8,128)(2,1)S(1)} collective-permute-done((bf16[216,768]{1,0:T(8,128)(2,1)S(1)}, bf16[216,768]{1,0:T(8,128)(2,1)S(1)}, u32[]{:S(2)}, u32[]{:S(2)}) %collective-permute-start.127) | collective-permute-done | bytes 331808 | tf_op jit(solution)/shard_map/ppermute | solution.py:38
  688.3 8.8 %collective-permute-done.133 = bf16[216,768]{1,0:T(8,128)(2,1)S(1)} collective-permute-done((bf16[216,768]{1,0:T(8,128)(2,1)S(1)}, bf16[216,768]{1,0:T(8,128)(2,1)S(1)}, u32[]{:S(2)}, u32[]{:S(2)}) %collective-permute-start.133) | collective-permute-done | bytes 331808 | tf_op jit(solution)/shard_map/ppermute | solution.py:38
  719.7 11.8 %collective-permute-done.145 = f32[2,12,768]{2,1,0:T(8,128)S(1)} collective-permute-done((f32[2,12,768]{2,1,0:T(8,128)S(1)}, f32[2,12,768]{2,1,0:T(8,128)S(1)}, u32[]{:S(2)}, u32[]{:S(2)}) %collective-permute-start.145) | collective-permute-done | bytes 73760 | tf_op jit(solution)/shard_map/ppermute | solution.py:38
  (688 shorter events, 410.3 us)
Async XLA Ops:
  2.5 31.6 %collective-permute-start.6 = (bf16[24,1152]{1,0:T(8,128)(2,1)}, bf16[24,1152]{1,0:T(8,128)(2,1)}, u32[]{:S(2)}, u32[]{:S(2)}) collective-permute-start(bf16[24,1152]{1,0:T(8,128)(2,1)} %get-tuple-element.582), channel_id=1, source_target_pairs={{0,8},{8,0},{16,24},{24,16},{1,9},{9,1},{17,25},{25,17},{2,10},{10... | collective-permute-start | bytes 165896 | tf_op jit(solution)/shard_map/ppermute | solution.py:38
  5.5 29.2 %collective-permute-start.7 = (bf16[24,1152]{1,0:T(8,128)(2,1)}, bf16[24,1152]{1,0:T(8,128)(2,1)}, u32[]{:S(2)}, u32[]{:S(2)}) collective-permute-start(bf16[24,1152]{1,0:T(8,128)(2,1)} %get-tuple-element.582), channel_id=1, source_target_pairs={{0,16},{8,24},{16,0},{24,8},{1,17},{9,25},{17,1},{25,9},{2,18},{10... | collective-permute-start | bytes 165896 | tf_op jit(solution)/shard_map/ppermute | solution.py:38
  82.2 35.1 %collective-permute-start.35 = (bf16[4,24,3456]{2,1,0:T(8,128)(2,1)}, bf16[4,24,3456]{2,1,0:T(8,128)(2,1)}, u32[]{:S(2)}, u32[]{:S(2)}) collective-permute-start(bf16[4,24,3456]{2,1,0:T(8,128)(2,1)} %pad_maximum_fusion.3), channel_id=1, source_target_pairs={{0,4},{1,5},{2,6},{3,7},{4,0},{5,1},{6,2},{7,3},{8,12},{9,13},{10,... | collective-permute-start | bytes 1990664 | tf_op jit(solution)/shard_map/ppermute | solution.py:38
  125.9 40.7 %collective-permute-start.39 = (bf16[8,24,3456]{2,1,0:T(8,128)(2,1)}, bf16[8,24,3456]{2,1,0:T(8,128)(2,1)}, u32[]{:S(2)}, u32[]{:S(2)}) collective-permute-start(bf16[8,24,3456]{2,1,0:T(8,128)(2,1)} %constant_dynamic-update-slice_fusion.31.rest_0_), channel_id=1, source_target_pairs={{0,4},{1,5},{2,6},{3,7},{4,0},{5,1},{6,2},{7,3},{8,12},{9,13},{10,... | collective-permute-start | bytes 3981320 | tf_op jit(solution)/shard_map/ppermute | solution.py:38
  129.2 37.4 %collective-permute-start.40 = (bf16[8,24,3456]{2,1,0:T(8,128)(2,1)}, bf16[8,24,3456]{2,1,0:T(8,128)(2,1)}, u32[]{:S(2)}, u32[]{:S(2)}) collective-permute-start(bf16[8,24,3456]{2,1,0:T(8,128)(2,1)} %constant_dynamic-update-slice_fusion.36.rest_4_), channel_id=1, source_target_pairs={{0,2},{1,3},{2,0},{3,1},{4,6},{5,7},{6,4},{7,5},{8,10},{9,11},{10,... | collective-permute-start | bytes 3981320 | tf_op jit(solution)/shard_map/ppermute | solution.py:38
  183.1 30.6 %collective-permute-start.53 = (bf16[8,24,1152]{2,1,0:T(8,128)(2,1)}, bf16[8,24,1152]{2,1,0:T(8,128)(2,1)}, u32[]{:S(2)}, u32[]{:S(2)}) collective-permute-start(bf16[8,24,1152]{2,1,0:T(8,128)(2,1)} %constant_dynamic-update-slice_fusion.41.rest_0_), channel_id=1, source_target_pairs={{0,4},{1,5},{2,6},{3,7},{4,0},{5,1},{6,2},{7,3},{8,12},{9,13},{10,... | collective-permute-start | bytes 1327112 | tf_op jit(solution)/shard_map/ppermute | solution.py:38
  185.2 28.5 %collective-permute-start.54 = (bf16[8,24,1152]{2,1,0:T(8,128)(2,1)}, bf16[8,24,1152]{2,1,0:T(8,128)(2,1)}, u32[]{:S(2)}, u32[]{:S(2)}) collective-permute-start(bf16[8,24,1152]{2,1,0:T(8,128)(2,1)} %constant_dynamic-update-slice_fusion.46.rest_4_), channel_id=1, source_target_pairs={{0,2},{1,3},{2,0},{3,1},{4,6},{5,7},{6,4},{7,5},{8,10},{9,11},{10,... | collective-permute-start | bytes 1327112 | tf_op jit(solution)/shard_map/ppermute | solution.py:38
  216.3 29.9 %collective-permute-start.73 = (bf16[4,24,3456]{2,1,0:T(8,128)(2,1)S(1)}, bf16[4,24,3456]{2,1,0:T(8,128)(2,1)S(1)}, u32[]{:S(2)}, u32[]{:S(2)}) collective-permute-start(bf16[4,24,3456]{2,1,0:T(8,128)(2,1)S(1)} %pad_maximum_fusion.5), channel_id=1, source_target_pairs={{0,4},{1,5},{2,6},{3,7},{4,0},{5,1},{6,2},{7,3},{8,12},{9,13},{10,... | collective-permute-start | bytes 1990664 | tf_op jit(solution)/shard_map/ppermute | solution.py:38
  247.8 36.8 %collective-permute-start.77 = (bf16[8,24,3456]{2,1,0:T(8,128)(2,1)S(1)}, bf16[8,24,3456]{2,1,0:T(8,128)(2,1)}, u32[]{:S(2)}, u32[]{:S(2)}) collective-permute-start(bf16[8,24,3456]{2,1,0:T(8,128)(2,1)S(1)} %constant_dynamic-update-slice_fusion.51.rest_0_), channel_id=1, source_target_pairs={{0,4},{1,5},{2,6},{3,7},{4,0},{5,1},{6,2},{7,3},{8,12},{9,13},{10,... | collective-permute-start | bytes 3981320 | tf_op jit(solution)/shard_map/ppermute | solution.py:38
  248.7 36.0 %collective-permute-start.78 = (bf16[8,24,3456]{2,1,0:T(8,128)(2,1)S(1)}, bf16[8,24,3456]{2,1,0:T(8,128)(2,1)}, u32[]{:S(2)}, u32[]{:S(2)}) collective-permute-start(bf16[8,24,3456]{2,1,0:T(8,128)(2,1)S(1)} %constant_dynamic-update-slice_fusion.56.rest_4_), channel_id=1, source_target_pairs={{0,2},{1,3},{2,0},{3,1},{4,6},{5,7},{6,4},{7,5},{8,10},{9,11},{10,... | collective-permute-start | bytes 3981320 | tf_op jit(solution)/shard_map/ppermute | solution.py:38
  367.2 44.8 %collective-permute-start.91 = (bf16[2,432,768]{2,1,0:T(8,128)(2,1)S(1)}, bf16[2,432,768]{2,1,0:T(8,128)(2,1)S(1)}, u32[]{:S(2)}, u32[]{:S(2)}) collective-permute-start(bf16[2,432,768]{2,1,0:T(8,128)(2,1)S(1)} %slice_bitcast_fusion.3), channel_id=1, source_target_pairs={{0,2},{1,3},{2,0},{3,1},{4,6},{5,7},{6,4},{7,5},{8,10},{9,11},{10,... | collective-permute-start | bytes 3981320 | tf_op jit(solution)/shard_map/ppermute | solution.py:38
  368.0 44.0 %collective-permute-start.92 = (bf16[2,432,768]{2,1,0:T(8,128)(2,1)S(1)}, bf16[2,432,768]{2,1,0:T(8,128)(2,1)S(1)}, u32[]{:S(2)}, u32[]{:S(2)}) collective-permute-start(bf16[2,432,768]{2,1,0:T(8,128)(2,1)S(1)} %slice.705), channel_id=1, source_target_pairs={{0,4},{1,5},{2,6},{3,7},{4,0},{5,1},{6,2},{7,3},{8,12},{9,13},{10,... | collective-permute-start | bytes 3981320 | tf_op jit(solution)/shard_map/ppermute | solution.py:38
  370.9 34.6 %collective-permute-start.88 = (bf16[3,192,256]{2,1,0:T(8,128)(2,1)S(1)}, bf16[3,192,256]{2,1,0:T(8,128)(2,1)S(1)}, u32[]{:S(2)}, u32[]{:S(2)}) collective-permute-start(bf16[3,192,256]{2,1,0:T(8,128)(2,1)S(1)} %pad_maximum_fusion.11), channel_id=1, source_target_pairs={{0,2},{1,3},{2,0},{3,1},{4,6},{5,7},{6,4},{7,5},{8,10},{9,11},{10,... | collective-permute-start | bytes 884744 | tf_op jit(solution)/shard_map/ppermute | solution.py:38
  372.1 38.8 %collective-permute-start.89 = (bf16[3,192,256]{2,1,0:T(8,128)(2,1)S(1)}, bf16[3,192,256]{2,1,0:T(8,128)(2,1)S(1)}, u32[]{:S(2)}, u32[]{:S(2)}) collective-permute-start(bf16[3,192,256]{2,1,0:T(8,128)(2,1)S(1)} %pad_maximum_fusion.12), channel_id=1, source_target_pairs={{0,4},{1,5},{2,6},{3,7},{4,0},{5,1},{6,2},{7,3},{8,12},{9,13},{10,... | collective-permute-start | bytes 884744 | tf_op jit(solution)/shard_map/ppermute | solution.py:38
  373.4 38.6 %collective-permute-start.90 = (bf16[3,192,256]{2,1,0:T(8,128)(2,1)S(1)}, bf16[3,192,256]{2,1,0:T(8,128)(2,1)S(1)}, u32[]{:S(2)}, u32[]{:S(2)}) collective-permute-start(bf16[3,192,256]{2,1,0:T(8,128)(2,1)S(1)} %pad_maximum_fusion.13), channel_id=1, source_target_pairs={{0,6},{1,7},{2,4},{3,5},{4,2},{5,3},{6,0},{7,1},{8,14},{9,15},{10,... | collective-permute-start | bytes 884744 | tf_op jit(solution)/shard_map/ppermute | solution.py:38
  440.8 67.7 %collective-permute-start.104 = (bf16[4,864,768]{2,1,0:T(8,128)(2,1)}, bf16[4,864,768]{2,1,0:T(8,128)(2,1)}, u32[]{:S(2)}, u32[]{:S(2)}) collective-permute-start(bf16[4,864,768]{2,1,0:T(8,128)(2,1)} %get-tuple-element.430), channel_id=1, source_target_pairs={{0,1},{1,0},{2,3},{3,2},{4,5},{5,4},{6,7},{7,6},{8,9},{9,8},{10,11... | collective-permute-start | bytes 15925256 | tf_op jit(solution)/shard_map/ppermute | solution.py:38
  472.6 35.9 %collective-permute-start.102 = (bf16[2,144,768]{2,1,0:T(8,128)(2,1)S(1)}, bf16[2,144,768]{2,1,0:T(8,128)(2,1)}, u32[]{:S(2)}, u32[]{:S(2)}) collective-permute-start(bf16[2,144,768]{2,1,0:T(8,128)(2,1)S(1)} %slice_bitcast_fusion.15), channel_id=1, source_target_pairs={{0,2},{1,3},{2,0},{3,1},{4,6},{5,7},{6,4},{7,5},{8,10},{9,11},{10,... | collective-permute-start | bytes 1327112 | tf_op jit(solution)/shard_map/ppermute | solution.py:38
  474.4 34.2 %collective-permute-start.103 = (bf16[2,144,768]{2,1,0:T(8,128)(2,1)}, bf16[2,144,768]{2,1,0:T(8,128)(2,1)}, u32[]{:S(2)}, u32[]{:S(2)}) collective-permute-start(bf16[2,144,768]{2,1,0:T(8,128)(2,1)} %slice.713), channel_id=1, source_target_pairs={{0,4},{1,5},{2,6},{3,7},{4,0},{5,1},{6,2},{7,3},{8,12},{9,13},{10,... | collective-permute-start | bytes 1327112 | tf_op jit(solution)/shard_map/ppermute | solution.py:38
  509.9 51.5 %collective-permute-start.106 = (bf16[216,768]{1,0:T(8,128)(2,1)S(1)}, bf16[216,768]{1,0:T(8,128)(2,1)}, u32[]{:S(2)}, u32[]{:S(2)}) collective-permute-start(bf16[216,768]{1,0:T(8,128)(2,1)S(1)} %fusion.13), channel_id=1, source_target_pairs={{0,8},{8,0},{16,24},{24,16},{1,9},{9,1},{17,25},{25,17},{2,10},{10... | collective-permute-start | bytes 995336 | tf_op jit(solution)/shard_map/ppermute | solution.py:38
  516.8 44.6 %collective-permute-start.107 = (bf16[216,768]{1,0:T(8,128)(2,1)S(1)}, bf16[216,768]{1,0:T(8,128)(2,1)}, u32[]{:S(2)}, u32[]{:S(2)}) collective-permute-start(bf16[216,768]{1,0:T(8,128)(2,1)S(1)} %fusion.13), channel_id=1, source_target_pairs={{0,16},{8,24},{16,0},{24,8},{1,17},{9,25},{17,1},{25,9},{2,18},{10... | collective-permute-start | bytes 995336 | tf_op jit(solution)/shard_map/ppermute | solution.py:38
  517.5 43.8 %collective-permute-start.108 = (bf16[216,768]{1,0:T(8,128)(2,1)S(1)}, bf16[216,768]{1,0:T(8,128)(2,1)}, u32[]{:S(2)}, u32[]{:S(2)}) collective-permute-start(bf16[216,768]{1,0:T(8,128)(2,1)S(1)} %fusion.13), channel_id=1, source_target_pairs={{0,24},{8,16},{16,8},{24,0},{1,25},{9,17},{17,9},{25,1},{2,26},{10... | collective-permute-start | bytes 995336 | tf_op jit(solution)/shard_map/ppermute | solution.py:38
  553.0 48.8 %collective-permute-start.117 = (bf16[2,432,768]{2,1,0:T(8,128)(2,1)}, bf16[2,432,768]{2,1,0:T(8,128)(2,1)}, u32[]{:S(2)}, u32[]{:S(2)}) collective-permute-start(bf16[2,432,768]{2,1,0:T(8,128)(2,1)} %slice_bitcast_fusion.1), channel_id=1, source_target_pairs={{0,2},{1,3},{2,0},{3,1},{4,6},{5,7},{6,4},{7,5},{8,10},{9,11},{10,... | collective-permute-start | bytes 3981320 | tf_op jit(solution)/shard_map/ppermute | solution.py:38
  559.3 42.5 %collective-permute-start.118 = (bf16[2,432,768]{2,1,0:T(8,128)(2,1)}, bf16[2,432,768]{2,1,0:T(8,128)(2,1)}, u32[]{:S(2)}, u32[]{:S(2)}) collective-permute-start(bf16[2,432,768]{2,1,0:T(8,128)(2,1)} %slice.725), channel_id=1, source_target_pairs={{0,4},{1,5},{2,6},{3,7},{4,0},{5,1},{6,2},{7,3},{8,12},{9,13},{10,... | collective-permute-start | bytes 3981320 | tf_op jit(solution)/shard_map/ppermute | solution.py:38
  634.4 29.6 %collective-permute-start.129 = (bf16[2,144,768]{2,1,0:T(8,128)(2,1)S(1)}, bf16[2,144,768]{2,1,0:T(8,128)(2,1)S(1)}, u32[]{:S(2)}, u32[]{:S(2)}) collective-permute-start(bf16[2,144,768]{2,1,0:T(8,128)(2,1)S(1)} %slice_bitcast_fusion.12), channel_id=1, source_target_pairs={{0,2},{1,3},{2,0},{3,1},{4,6},{5,7},{6,4},{7,5},{8,10},{9,11},{10,... | collective-permute-start | bytes 1327112 | tf_op jit(solution)/shard_map/ppermute | solution.py:38
  (216 other events, 2466.1 us)

commit v2 on v1

--- a/solution.py
+++ b/solution.py
@@ -42,6 +42,28 @@
     return pl.BlockSpec(shape, lambda *unused: (0,) * len(shape))
 
 
+def column_spec(width, first, step=1):
+    return pl.BlockSpec((width, width), lambda j: (0, first + step * j))
+
+
+def down_spec(width, pieces):
+    return pl.BlockSpec((width // pieces, pieces * width), lambda j: (j, 0))
+
+
+def load_down(target, block, pieces, depth):
+    if pieces == 1:
+        target[...] = block[...]
+        return
+    width = target.shape[1]
+    rows = block[...].astype(F32)
+    parts = [
+        rows[d * depth : (d + 1) * depth, t * width : (t + 1) * width]
+        for d in range(rows.shape[0] // depth)
+        for t in range(pieces)
+    ]
+    target[...] = jnp.concatenate(parts, axis=0).astype(BF16)
+
+
 def params(count=1):
     return pltpu.CompilerParams(
         dimension_semantics=("arbitrary",) * count, vmem_limit_bytes=VMEM_LIMIT
@@ -62,6 +84,7 @@
 
 
 def project(order, rows, weight, bias, groups):
+    weight, first = weight
     tokens, width = rows.shape
     span = width // groups
     return pl.pallas_call(
@@ -71,7 +94,7 @@
         in_specs=[
             SMEM_SPEC,
             resident((tokens, width)),
-            pl.BlockSpec((width, width), lambda j: (0, j)),
+            column_spec(width, first),
             pl.BlockSpec((1, 1, width), lambda j: (j, 0, 0)),
         ],
         out_specs=[pl.BlockSpec((1, span, tokens), lambda j: (j, 0, 0))] * groups,
@@ -261,6 +284,7 @@
 
 
 OUT_BIAS, ATT_GAIN, ATT_SHIFT, DOWN_BIAS, FEED_GAIN, FEED_SHIFT = range(6)
+SMALL_ROWS, SMALL_UP, SMALL_PROJECT = 16, 8, 12
 
 
 def normalized(rows):
@@ -277,9 +301,11 @@
     return inverse * (scaled - mean_scaled - normal * mean_both)
 
 
-def feed_body(groups, span, blocks, order, x_ref, wo_ref, wu_ref, wd_ref, vec, ub_ref, *rest):
+def feed_body(
+    groups, span, blocks, pieces, depth, order, x_ref, wo_ref, wu_ref, wd_ref, vec, ub_ref, *rest
+):
     contexts, rest = rest[:groups], rest[groups:]
-    sum_first, hidden_low, sum_second, out, hidden, outward = rest
+    sum_first, hidden_low, sum_second, out, hidden, outward, down = rest
     j = pl.program_id(0)
 
     @pl.when(j == 0)
@@ -297,7 +323,8 @@
 
     inner = nn(hidden_low[...], wu_ref[...]) + ub_ref[0]
     activated = (0.5 * inner * (1.0 + lax.erf(inner * RSQRT2))).astype(BF16)
-    outward[...] += nn(activated, wd_ref[...])
+    load_down(down, wd_ref, pieces, depth)
+    outward[...] += nn(activated, down[...])
 
     @pl.when(j == blocks - 1)
     def _():
@@ -308,26 +335,27 @@
 
 
 def feed(order, rows, w_output, w_up, w_down, vectors, up_bias, contexts):
+    (w_output, at_output), (w_up, at_up), (w_down, pieces, depth) = w_output, w_up, w_down
     tokens, width = rows.shape
     groups, span = len(contexts), contexts[0].shape[0]
-    blocks = w_up.shape[1] // width
+    blocks = up_bias.shape[0]
     full = jax.ShapeDtypeStruct((tokens, width), F32)
     return pl.pallas_call(
-        functools.partial(feed_body, groups, span, blocks),
+        functools.partial(feed_body, groups, span, blocks, pieces, depth),
         out_shape=[full, jax.ShapeDtypeStruct((tokens, width), BF16), full, full],
         grid=(blocks,),
         in_specs=[
             SMEM_SPEC,
             resident((tokens, width)),
-            resident((width, width)),
-            pl.BlockSpec((width, width), lambda j: (0, j)),
-            pl.BlockSpec((width, width), lambda j: (j, 0)),
+            column_spec(width, at_output, 0),
+            column_spec(width, at_up),
+            down_spec(width, pieces),
             resident(vectors.shape),
             pl.BlockSpec((1, 1, width), lambda j: (j, 0, 0)),
         ]
         + [resident((span, tokens))] * groups,
         out_specs=[resident((tokens, width))] * 4,
-        scratch_shapes=[pltpu.VMEM((tokens, width), F32)] * 2,
+        scratch_shapes=[pltpu.VMEM((tokens, width), F32)] * 2 + [pltpu.VMEM((width, width), BF16)],
         compiler_params=params(),
         cost_estimate=pl.CostEstimate(
             flops=(4 * blocks + 2) * tokens * width * width,
@@ -339,15 +367,25 @@
 
 
 def feed_back_body(
-    groups, span, blocks, devices, order, place, grad_ref, first_ref, second_ref, low_ref, *rest
+    groups,
+    span,
+    blocks,
+    devices,
+    pieces,
+    depth,
+    order,
+    grad_ref,
+    first_ref,
+    second_ref,
+    low_ref,
+    *rest
 ):
     wo_ref, wu_ref, wd_ref, vec, ub_ref = rest[:5]
     contexts, rest = rest[5 : 5 + groups], rest[5 + groups :]
-    own, send, grad_first, small = rest[:4]
-    grad_contexts, rest = rest[4 : 4 + groups], rest[4 + groups :]
-    grad_out, grad_hidden, tile = rest
+    shares, grad_first, small = rest[:3]
+    grad_contexts, rest = rest[3 : 3 + groups], rest[3 + groups :]
+    grad_out, grad_hidden, tile, down = rest
     width = vec.shape[-1]
-    me = place[0]
     j = pl.program_id(0)
     share = width // devices
     down_share = blocks * share
@@ -370,30 +408,20 @@
     below = 0.5 * (1.0 + lax.erf(inner * RSQRT2))
     activated = (inner * below).astype(BF16)
     slope = below + inner * (PDF_SCALE * jnp.exp(-0.5 * inner * inner))
-    grad_inner = (nt(grad_out[...], wd_ref[...]) * slope).astype(BF16)
-    small[pl.ds(8 + j, 1), :] = jnp.sum(grad_inner.astype(F32), axis=0, keepdims=True)
+    load_down(down, wd_ref, pieces, depth)
+    grad_inner = (nt(grad_out[...], down[...]) * slope).astype(BF16)
+    small[pl.ds(SMALL_UP + j, 1), :] = jnp.sum(grad_inner.astype(F32), axis=0, keepdims=True)
     grad_hidden[...] += nt(grad_inner, wu_ref[...])
 
-    tile[...] = tn(activated, grad_out[...]).astype(BF16)
+    product = tn(activated, grad_out[...]).astype(BF16)
     for k in range(per_block):
-        owner = (j * per_block + k) ^ me
-        slot = lax.shift_right_logical(owner, 1)
-        rows = pl.ds(k * down_share, down_share)
-
-        @pl.when((owner & 1) == 0)
-        def _():
-            own[slot, pl.ds(0, down_share), :] = tile[rows, :]
-
-        @pl.when((owner & 1) == 1)
-        def _():
-            send[slot, pl.ds(0, down_share), :] = tile[rows, :]
-
-    tile[...] = tn(low_ref[...], grad_inner).astype(BF16)
-    for i in range(devices // 2):
-        for bit, target in ((0, own), (1, send)):
-            start = pl.multiple_of((me ^ (2 * i + bit)) * share, share)
-            base = pl.multiple_of(down_share + j * share, share)
-            target[i, pl.ds(base, share), :] = tile[pl.ds(start, share), :]
+        shares[j * per_block + k, pl.ds(0, down_share), :] = product[
+            k * down_share : (k + 1) * down_share, :
+        ]
+    product = tn(low_ref[...], grad_inner).astype(BF16)
+    base = pl.multiple_of(down_share + j * share, share)
+    for i in range(devices):
+        shares[i, pl.ds(base, share), :] = product[i * share : (i + 1) * share, :]
 
     @pl.when(j == blocks - 1)
     def _():
@@ -409,46 +437,45 @@
             start = pl.multiple_of(order[r] * span, span)
             tile[pl.ds(start, span), :] = nn(contexts[r][...], low).astype(BF16)
             grad_contexts[r][...] = nt(wo_ref[pl.ds(start, span), :], low).astype(BF16)
-        for i in range(devices // 2):
-            for bit, target in ((0, own), (1, send)):
-                start = pl.multiple_of((me ^ (2 * i + bit)) * share, share)
-                base = down_share + blocks * share
-                target[i, base : base + share, :] = tile[pl.ds(start, share), :]
+        last = down_share + blocks * share
+        for i in range(devices):
+            shares[i, last : last + share, :] = tile[i * share : (i + 1) * share, :]
 
 
 def feed_back(
-    order, place, grad, first, second, low, w_output, w_up, w_down, vectors, up_bias, contexts, devices
+    order, grad, first, second, low, w_output, w_up, w_down, vectors, up_bias, contexts, devices
 ):
+    (w_output, at_output), (w_up, at_up), (w_down, pieces, depth) = w_output, w_up, w_down
     tokens, width = grad.shape
     groups, span = len(contexts), contexts[0].shape[0]
-    blocks = w_up.shape[1] // width
+    blocks = up_bias.shape[0]
     share = width // devices
-    kept = (devices // 2, (2 * blocks + 1) * share, width)
+    kept = (devices, (2 * blocks + 1) * share, width)
     return pl.pallas_call(
-        functools.partial(feed_back_body, groups, span, blocks, devices),
+        functools.partial(feed_back_body, groups, span, blocks, devices, pieces, depth),
         out_shape=[
             jax.ShapeDtypeStruct(kept, BF16),
-            jax.ShapeDtypeStruct(kept, BF16),
             jax.ShapeDtypeStruct((tokens, width), F32),
-            jax.ShapeDtypeStruct((16, width), F32),
+            jax.ShapeDtypeStruct((SMALL_ROWS, width), F32),
         ]
         + [jax.ShapeDtypeStruct((span, tokens), BF16)] * groups,
         grid=(blocks,),
-        in_specs=[SMEM_SPEC, SMEM_SPEC]
+        in_specs=[SMEM_SPEC]
         + [resident((tokens, width))] * 4
         + [
-            resident((width, width)),
-            pl.BlockSpec((width, width), lambda j: (0, j)),
-            pl.BlockSpec((width, width), lambda j: (j, 0)),
+            column_spec(width, at_output, 0),
+            column_spec(width, at_up),
+            down_spec(width, pieces),
             resident(vectors.shape),
             pl.BlockSpec((1, 1, width), lambda j: (j, 0, 0)),
         ]
         + [resident((span, tokens))] * groups,
-        out_specs=[resident(kept), resident(kept), resident((tokens, width)), resident((16, width))]
+        out_specs=[resident(kept), resident((tokens, width)), resident((SMALL_ROWS, width))]
         + [resident((span, tokens))] * groups,
         scratch_shapes=[
             pltpu.VMEM((tokens, width), BF16),
             pltpu.VMEM((tokens, width), F32),
+            pltpu.VMEM((width, width), BF16),
             pltpu.VMEM((width, width), BF16),
         ],
         compiler_params=params(),
@@ -460,7 +487,6 @@
         name="feed_back",
     )(
         order,
-        place,
         grad,
         first,
         second,
@@ -474,10 +500,10 @@
     )
 
 
-def project_back_body(groups, span, devices, order, place, x_ref, grad_ref, w_ref, *rest):
+def project_back_body(groups, span, devices, order, place, x_ref, grad_ref, w_ref, small_ref, *rest):
     pieces, rest = rest[:groups], rest[groups:]
     own, send, out, small, joined, tile = rest
-    width = w_ref.shape[0]
+    width = out.shape[1]
     me = place[0]
     j = pl.program_id(0)
     share = width // devices
@@ -485,13 +511,13 @@
     @pl.when(j == 0)
     def _():
         out[...] = grad_ref[...]
-        small[...] = jnp.zeros_like(small)
+        small[...] = small_ref[...]
 
     for r in range(groups):
         start = pl.multiple_of(order[r] * span, span)
         joined[pl.ds(start, span), :] = pieces[r][0]
     grad = joined[...].T
-    small[pl.ds(j, 1), :] = jnp.sum(grad.astype(F32), axis=0, keepdims=True)
+    small[pl.ds(SMALL_PROJECT + j, 1), :] = jnp.sum(grad.astype(F32), axis=0, keepdims=True)
     out[...] += nt(grad, w_ref[...])
     tile[...] = tn(x_ref[...].astype(BF16), grad).astype(BF16)
     for i in range(devices // 2):
@@ -500,18 +526,25 @@
             base = pl.multiple_of(j * share, share)
             target[i, pl.ds(base, share), :] = tile[pl.ds(start, share), :]
 
-
-def project_back(order, place, rows, grad, weight, pieces, devices):
+    @pl.when(j == 2)
+    def _():
+        rows = jnp.concatenate([small[...], jnp.zeros_like(small)], axis=0).astype(BF16)
+        for i in range(devices // 2):
+            for target in (own, send):
+                target[i, 3 * share :, :] = rows
+
+
+def project_back(order, place, rows, grad, weight, small, pieces, devices):
+    weight, first = weight
     tokens, width = rows.shape
     groups, span = len(pieces), pieces[0].shape[1]
-    kept = (devices // 2, 3 * (width // devices), width)
+    kept = (devices // 2, 3 * (width // devices) + 2 * SMALL_ROWS, width)
     return pl.pallas_call(
         functools.partial(project_back_body, groups, span, devices),
         out_shape=[
             jax.ShapeDtypeStruct(kept, BF16),
             jax.ShapeDtypeStruct(kept, BF16),
             jax.ShapeDtypeStruct((tokens, width), F32),
-            jax.ShapeDtypeStruct((8, width), F32),
         ],
         grid=(3,),
         in_specs=[
@@ -519,23 +552,28 @@
             SMEM_SPEC,
             resident((tokens, width)),
             resident((tokens, width)),
-            pl.BlockSpec((width, width), lambda j: (0, j)),
+            column_spec(width, first),
+            resident((SMALL_ROWS, width)),
         ]
         + [pl.BlockSpec((1, span, tokens), lambda j: (j, 0, 0))] * groups,
-        out_specs=[resident(kept), resident(kept), resident((tokens, width)), resident((8, width))],
-        scratch_shapes=[pltpu.VMEM((width, tokens), BF16), pltpu.VMEM((width, width), BF16)],
+        out_specs=[resident(kept), resident(kept), resident((tokens, width))],
+        scratch_shapes=[
+            pltpu.VMEM((SMALL_ROWS, width), F32),
+            pltpu.VMEM((width, tokens), BF16),
+            pltpu.VMEM((width, width), BF16),
+        ],
         compiler_params=params(),
         cost_estimate=pl.CostEstimate(
             flops=12 * tokens * width * width, bytes_accessed=12 * width * width, transcendentals=0
         ),
         name="project_back",
-    )(order, place, rows, grad, weight, *pieces)
+    )(order, place, rows, grad, weight, small, *pieces)
 
 
 class Stream:
     def __init__(self, steps):
-        self.steps, self.result = steps, None
-        self.flying = next(steps)
+        self.steps, self.result, self.flying = steps, None, None
+        self.resume(None)
 
     def resume(self, arrived):
         try:
@@ -550,21 +588,6 @@
     for item, arrived in zip(streams, flying):
         item.resume(arrived)
     return values
-
-
-def gather_steps(shard, devices, dp_size, masks):
-    arrived = yield [exchange(shard, "dp", dp_size, m) for m in range(1, dp_size)]
-    stack = jnp.stack([shard] + list(arrived))
-    offsets = [(m, 0) for m in range(dp_size)]
-    stacks = [stack]
-    for mask in masks:
-        (other,) = yield [exchange(stack, "seq", devices, mask)]
-        offsets += [(d, q ^ mask) for d, q in offsets]
-        stacks = [stack, other]
-        stack = jnp.concatenate(stacks)
-    arrived = yield [exchange(item, "seq", devices, 1) for item in stacks]
-    offsets += [(d, q ^ 1) for d, q in offsets]
-    return stacks + list(arrived), offsets
 
 
 def sum_steps(own, send, devices, dp_size, dp_me):
@@ -592,6 +615,11 @@
         leave = yield leave
         kept = [add_low(a, b) for a, b in zip(stay, leave)]
     total = jnp.concatenate(kept, axis=0)
+    return (yield from dp_steps(total, dp_size, dp_me))
+
+
+def dp_steps(total, dp_size, dp_me):
+    rows, width = total.shape
     if dp_size != 4:
         return lax.psum(total, "dp")
     pieces = total.reshape(dp_size, rows // dp_size, width)
@@ -609,91 +637,8 @@
     return jnp.concatenate(stack, axis=0)
 
 
-def vector_sum_steps(value, devices, dp_size):
-    for axis, size in (("seq", devices), ("dp", dp_size)):
-        for bit in range(int(math.log2(size))):
-            (other,) = yield [exchange(value, axis, size, 1 << bit)]
-            value = value + other
-    return value
-
-
 def add_low(a, b):
     return (a.astype(F32) + b.astype(F32)).astype(BF16)
-
-
-def place_body(sources, layout, outs_count, table, *rest):
-    parts, rest = rest[:sources], rest[sources:]
-    outs, (buffer, in_sems, out_sems) = rest[:outs_count], rest[outs_count:]
-    per = buffer.shape[0] // sources
-
-    def into(a, k):
-        i = a * per + k
-        return pltpu.make_async_copy(parts[a].at[k], buffer.at[i], in_sems.at[i])
-
-    def onward(a, k):
-        i = a * per + k
-        half = a * 2 // sources
-        copies = []
-        for at, (target, index, column, size, first) in enumerate(layout[half]):
-            if index is None:
-                goal = outs[target].at[table[i], :, pl.ds(first, size)]
-            else:
-                goal = outs[target].at[table[i], index]
-            copies.append(
-                pltpu.make_async_copy(
-                    buffer.at[i, :, pl.ds(column, size)], goal, out_sems.at[i, at]
-                )
-            )
-        return copies
-
-    for a in range(sources):
-
-        def begin(k, unused, a=a):
-            into(a, k).start()
-            return unused
-
-        lax.fori_loop(0, per, begin, 0)
-    for a in range(sources):
-
-        def middle(k, unused, a=a):
-            into(a, k).wait()
-            for copy in onward(a, k):
-                copy.start()
-            return unused
-
-        lax.fori_loop(0, per, middle, 0)
-    for a in range(sources):
-
-        def finish(k, unused, a=a):
-            for copy in onward(a, k):
-                copy.wait()
-            return unused
-
-        lax.fori_loop(0, per, finish, 0)
-
-
-def put_in_place(first, second, layout, shapes, me, dp_me, devices):
-    parts = first[0] + second[0]
-    offsets = jnp.array(first[1] + second[1], jnp.int32)
-    table = (dp_me ^ offsets[:, 0]) * devices + (me ^ offsets[:, 1])
-    depth, columns = parts[0].shape[1:]
-    count = len(first[1]) * 2
-    most = max(len(item) for item in layout)
-    size = 4 * count * depth * columns
-    return pl.pallas_call(
-        functools.partial(place_body, len(parts), layout, len(shapes)),
-        out_shape=[jax.ShapeDtypeStruct(shape, BF16) for shape in shapes],
-        in_specs=[SMEM_SPEC] + [ANY_SPEC] * len(parts),
-        out_specs=[ANY_SPEC] * len(shapes),
-        scratch_shapes=[
-            pltpu.VMEM((count, depth, columns), BF16),
-            pltpu.SemaphoreType.DMA((count,)),
-            pltpu.SemaphoreType.DMA((count, most)),
-        ],
-        compiler_params=pltpu.CompilerParams(vmem_limit_bytes=VMEM_LIMIT),
-        cost_estimate=pl.CostEstimate(flops=0, bytes_accessed=size, transcendentals=0),
-        name="put_in_place",
-    )(table, *parts)
 
 
 def per_device(
@@ -750,76 +695,6 @@
     used = flat.shape[0]
     flat = jnp.pad(flat, (0, -used % 1024)).reshape(-1, 128)
 
-    def chunk_project(layer, half):
-        cut = 3 * width // 2
-        return project_weight[layer, :, half * cut : (half + 1) * cut]
-
-    def chunk_rest(layer, half):
-        cut = down_weight.shape[1] // 2
-        down = down_weight[layer, half * cut : (half + 1) * cut]
-        return jnp.concatenate(
-            [
-                output_weight[layer, :, half * (width // 2) : (half + 1) * (width // 2)],
-                up_weight[layer, :, half * (inner_width // 2) : (half + 1) * (inner_width // 2)],
-            ]
-            + [down[t * depth : (t + 1) * depth] for t in range(blocks // 2)],
-            axis=1,
-        )
-
-    masks = [2 << b for b in range(int(math.log2(seq_size)) - 1)]
-
-    def gather(chunk, half=0):
-        return Stream(gather_steps(chunk, seq_size, dp_size, masks[::-1] if half else masks))
-
-    def project_streams(layer):
-        return [gather(chunk_project(layer, half), half) for half in range(2)]
-
-    def rest_streams(layer):
-        return [gather(chunk_rest(layer, half), half) for half in range(2)]
-
-    def placed_project(streams):
-        cut = 3 * width // 2
-        layout = [[(0, None, 0, cut, half * cut)] for half in range(2)]
-        (made,) = put_in_place(
-            streams[0].result,
-            streams[1].result,
-            layout,
-            [(everyone, depth, 3 * width)],
-            me,
-            dp_me,
-            seq_size,
-        )
-        return made.reshape(width, 3 * width)
-
-    def placed_rest(streams):
-        a, b = width // 2, inner_width // 2
-        layout = [
-            [(0, None, 0, a, half * a), (1, None, a, b, half * b)]
-            + [
-                (2, half * (blocks // 2) + t, a + b + t * width, width, 0)
-                for t in range(blocks // 2)
-            ]
-            for half in range(2)
-        ]
-        w_output, w_up, w_down = put_in_place(
-            streams[0].result,
-            streams[1].result,
-            layout,
-            [
-                (everyone, depth, width),
-                (everyone, depth, inner_width),
-                (everyone, blocks, depth, width),
-            ],
-            me,
-            dp_me,
-            seq_size,
-        )
-        return (
-            w_output.reshape(width, width),
-            w_up.reshape(width, inner_width),
-            w_down.reshape(inner_width, width),
-        )
-
     def swap_groups(items):
         return [items[0]] + [
             exchange(items[r], "seq", seq_size, r * members) for r in range(1, groups)
@@ -832,34 +707,39 @@
             items += [exchange(item, "seq", seq_size, j) for item in own]
         return items
 
-    w_project, w_rest = [None] * LAYERS, [None] * LAYERS
+    def gathered(shard):
+        return lax.all_gather(shard, both, axis=0, tiled=True)
+
+    def rest_shard(layer):
+        down = down_weight[layer].reshape(blocks, depth, width)
+        return [down[t] for t in range(blocks)] + [up_weight[layer], output_weight[layer]]
+
+    def rest_of(whole):
+        return (whole, 2 * blocks), (whole, blocks), (whole, blocks, depth)
+
     if plain:
         table = lax.all_gather(flat, both, axis=0, tiled=False)
+        w_project = [(gathered(project_weight[layer]), 0) for layer in range(LAYERS)]
+        w_rest = [
+            (
+                (gathered(output_weight[layer]), 0),
+                (gathered(up_weight[layer]), 0),
+                (gathered(down_weight[layer]), 1, depth),
+            )
+            for layer in range(LAYERS)
+        ]
+    else:
+        extra = jnp.pad(flat.reshape(-1), (0, depth * 128 - flat.size)).reshape(depth, 128)
+        first = gathered(jnp.concatenate([project_weight[0], extra], axis=1))
+        table = first[:, 3 * width :]
+        w_project, w_rest = [(first, 0)], []
         for layer in range(LAYERS):
-            w_project[layer] = lax.all_gather(project_weight[layer], both, axis=0, tiled=True)
-            w_rest[layer] = tuple(
-                lax.all_gather(item[layer], both, axis=0, tiled=True)
-                for item in (output_weight, up_weight, down_weight)
-            )
-        projects = rests = [[]] * LAYERS
-    else:
-        small = gather(flat)
-        projects, rests = [project_streams(0), None], [None, None]
-        first = projects[0] + [small]
-        tick(first)
-        rests[0] = rest_streams(0)
-        tick(first)
-        tick(first)
-        tick(rests[0])
-        tick(first)
-        stacks, offsets = small.result
-        offsets = jnp.array(offsets, jnp.int32)
-        where = {pair: i for i, pair in enumerate(small.result[1])}
-        lookup = jnp.array(
-            [where[(d, q)] for d in range(dp_size) for q in range(seq_size)], jnp.int32
-        )
-        wanted = jnp.arange(everyone, dtype=jnp.int32) ^ (dp_me * seq_size + me)
-        table = jnp.take(jnp.concatenate(stacks), jnp.take(lookup, wanted), axis=0)
+            parts = rest_shard(layer)
+            if layer + 1 < LAYERS:
+                parts.append(project_weight[layer + 1])
+            whole = gathered(jnp.concatenate(parts, axis=1))
+            w_rest.append(rest_of(whole))
+            w_project.append((whole, 2 * blocks + 1))
 
     table = table.reshape(everyone, -1)
     small_rows = LAYERS * 8 * depth
@@ -898,22 +778,10 @@
     current = states[0].astype(F32)
     saved = []
     for layer in range(LAYERS):
-        last = layer == LAYERS - 1
-        if not plain:
-            w_project[layer] = placed_project(projects[layer])
         made = projected(layer, current)
         parts = with_members(swap_groups(made))
-        parts = tick(rests[layer], tuple(parts))
-        if not plain and not last:
-            projects[layer + 1] = project_streams(layer + 1)
-            rests[layer + 1] = rest_streams(layer + 1)
         *mixed, exact, log_total = attend(active, seg_row, seg_col, parts, groups, members)
-        contexts = tuple(swap_groups(mixed))
-        ahead = [] if plain or last else projects[layer + 1]
-        contexts = tick(rests[layer] + ahead, contexts)
-        contexts = tick(rests[layer] + ahead, contexts)
-        if not plain:
-            w_rest[layer] = placed_rest(rests[layer])
+        contexts = swap_groups(mixed)
         w_output, w_up, w_down = w_rest[layer]
         sum_first, low, sum_second, following = feed(
             order,
@@ -927,21 +795,16 @@
         )
         saved.append((current, parts, exact, log_total, contexts, sum_first, low, sum_second))
         current = following
-        if not plain and not last:
-            current = tick(ahead + rests[layer + 1], current)
-            current = tick(ahead, current)
     output = current.astype(BF16)[None]
 
     grad = cotangent[0].astype(F32)
-    smalls = [None] * LAYERS
-    feeds, backs = [None] * LAYERS, [None] * LAYERS
+    shares, feeds, backs = [None] * LAYERS, [None] * LAYERS, [None] * LAYERS
     behind = []
     for layer in reversed(range(LAYERS)):
         w_output, w_up, w_down = w_rest[layer]
         entered, parts, exact, log_total, contexts, sum_first, low, sum_second = saved[layer]
-        own, send, grad_first, small_feed, *grad_mixed = feed_back(
+        terms, grad_first, small, *grad_mixed = feed_back(
             order,
-            place,
             grad,
             sum_first,
             sum_second,
@@ -954,10 +817,12 @@
             contexts,
             seq_size,
         )
+        shares[layer] = lax.psum_scatter(
+            terms.reshape(-1, width), "seq", scatter_dimension=0, tiled=True
+        )
         grad_mixed = tick(behind, tuple(grad_mixed))
-        feeds[layer] = Stream(sum_steps(own, send, seq_size, dp_size, dp_me))
         grads = tuple(swap_groups(grad_mixed))
-        grads = tick(behind + [feeds[layer]], grads)
+        grads = tick(behind, grads)
         grad_query, kept_kv, *sent_kv = attend_back(
             active, seg_row, seg_col, parts, grads, exact, log_total, groups, members
         )
@@ -967,23 +832,27 @@
             jnp.concatenate([grad_query[r][None], kept_kv[r].astype(BF16)], axis=0)
             for r in range(groups)
         ]
+        if layer + 1 < LAYERS:
+            messages, later = lax.optimization_barrier((tuple(messages), shares[layer + 1]))
+            feeds[layer + 1] = Stream(dp_steps(later, dp_size, dp_me))
         messages = tick(behind, tuple(messages))
+        behind += [item for item in feeds if item is not None]
         pieces = tuple(swap_groups(messages))
-        pieces = tick(behind + [feeds[layer]], pieces)
-        own, send, grad, small_project = project_back(
-            order, place, entered, grad_first, w_project[layer], pieces, seq_size
+        pieces = tick(behind, pieces)
+        own, send, grad = project_back(
+            order, place, entered, grad_first, w_project[layer], small, pieces, seq_size
         )
         backs[layer] = Stream(sum_steps(own, send, seq_size, dp_size, dp_me))
-        behind = [feeds[layer], backs[layer]]
-        smalls[layer] = jnp.concatenate(
-            [small_feed[:6], small_feed[8 : 8 + blocks], small_project[0:1], small_project[2:3]],
-            axis=0,
-        )
-    vector_sum = Stream(vector_sum_steps(jnp.stack(smalls), seq_size, dp_size))
-    behind = feeds + backs + [vector_sum]
+        behind = behind + [backs[layer]]
+    tick(behind)
+    tick(behind)
+    feeds[0] = Stream(dp_steps(shares[0], dp_size, dp_me))
+    behind = behind + [feeds[0]]
     while any(item.flying is not None for item in behind):
         tick(behind)
-    small = vector_sum.result
+    small = jnp.stack(
+        [backs[layer].result[3 * share : 3 * share + SMALL_ROWS] for layer in range(LAYERS)]
+    ).astype(F32)
     results = [(feeds[layer].result, backs[layer].result) for layer in range(LAYERS)]
 
     def mine(rows, size):
@@ -997,13 +866,13 @@
     g_up = jnp.stack([columns(item[0], range(blocks, 2 * blocks)) for item in results])
     g_down = jnp.stack([item[0][:down_rows].astype(F32) for item in results])
     g_output = jnp.stack([item[0][down_rows + blocks * share :].astype(F32) for item in results])
-    wide = small[:, 6 : 6 + blocks].reshape(LAYERS, blocks * width)
+    wide = small[:, SMALL_UP : SMALL_UP + blocks].reshape(LAYERS, blocks * width)
     return (
         output,
         grad[None],
         g_project,
-        mine(small[:, 6 + blocks], share),
-        mine(small[:, 7 + blocks], share),
+        mine(small[:, SMALL_PROJECT], share),
+        mine(small[:, SMALL_PROJECT + 2], share),
         g_output,
         mine(small[:, OUT_BIAS], share),
         mine(small[:, ATT_GAIN], share),

time: 751 us -> 666 us (0.89); the launches traced: 739 us -> 665 us
  starting transfers between devices: 170 us -> 87.4 us
  waiting for transfers between devices: 246 us -> 328 us
  local copies, waits for them, and re-layouts: 69 us -> 33.2 us
  other arithmetic: 59.3 us -> 26.4 us
  Pallas kernels: 192 us -> 175 us
  between operations: 2.83 us -> 14.7 us
    all_gather x0 -> x3, waiting for transfers between devices: none -> 138 us  [gathered(): return lax.all_gather(shard, both, axis=0, tiled=True)]
    ppermute x146 -> x68, starting transfers between devices: 170 us -> 87.2 us  [exchange(): return lax.ppermute(value, axis, [(i, i ^ mask) for i in range(size)])]
    ppermute x146 -> x68, waiting for transfers between devices: 246 us -> 189 us  [exchange(): return lax.ppermute(value, axis, [(i, i ^ mask) for i in range(size)])]
    pallas_call x6 -> x2, Pallas kernels: 54.2 us -> 20 us  [feed(): pl.pallas_call(functools.partial(feed_body, groups, span, blocks, pieces,...]
    convert_element_type x20 -> x10, other arithmetic: 24.9 us -> 5.74 us  [add_low(): return (a.astype(F32) + b.astype(F32)).astype(BF16)]
    unnamed x225 -> x116, local copies, waits for them, and re-layouts: 30.7 us -> 17.3 us
    pallas_call x2, Pallas kernels: 40.5 us -> 52.6 us  [attend_back(): pl.pallas_call(functools.partial(attend_back_body, groups, members, heads...]
    pallas_call x2, Pallas kernels: 34.3 us -> 43.1 us  [attend(): pl.pallas_call(functools.partial(attend_body, groups, members, heads), ou...]
  transfers between devices with their start and end apart: 146 -> 73, of which waited for: 46 -> 33; matrix products, arithmetic and copies ran while one was open for 14% -> 6% of each run, Pallas kernels for 14% -> 22%
where the time goes in v2:
time: 666 us; the launch traced here: 665 us
  waiting for transfers between devices  328 us (49%)
  Pallas kernels  175 us (26%)
  starting transfers between devices  87.4 us (13%)
  local copies, waits for them, and re-layouts  33.2 us (5%)
  other arithmetic  26.4 us (4%)
  between operations  14.7 us (2%)
    ppermute x68, waiting for transfers between devices, exchange(): return lax.ppermute(value, axis, [(i, i ^ mask) for i in range(size)])  189 us
    all_gather x3, waiting for transfers between devices, gathered(): return lax.all_gather(shard, both, axis=0, tiled=True)  138 us
    ppermute x68, starting transfers between devices, exchange(): return lax.ppermute(value, axis, [(i, i ^ mask) for i in range(size)])  87.2 us
    pallas_call x2, Pallas kernels, attend_back(): pl.pallas_call(functools.partial(attend_back_body, groups, members, heads...  52.6 us
    pallas_call x2, Pallas kernels, attend(): pl.pallas_call(functools.partial(attend_body, groups, members, heads), ou...  43.1 us
    pallas_call x2, Pallas kernels, feed_back(): pl.pallas_call(functools.partial(feed_back_body, groups, span, blocks, de...  34.7 us
    pallas_call x2, Pallas kernels, feed(): pl.pallas_call(functools.partial(feed_body, groups, span, blocks, pieces,...  20 us
    unnamed x116, local copies, waits for them, and re-layouts  17.3 us
  transfers between devices with their start and end apart: 73, of which 33 were waited for; matrix products, arithmetic and copies ran while one was open for 6% of the time, Pallas kernels for 22%

profile of v2, /device:TPU:0, one launch (start us, length us, event | category | flops | bytes accessed | tf_op | source)
XLA Modules:
  0.0 664.8 jit_solution(11480404097771081893)
XLA Ops:
  24.1 55.2 %all-gather.6.cloned.1.call-done.w_ref = bf16[768,2432]{1,0:T(8,128)(2,1)} async-done(((bf16[24,2432]{1,0:T(8,128)(2,1)}), bf16[768,2432]{1,0:T(8,128)(2,1)}) %all-gather.6.cloned.1.call-update) | async-done | bytes 3735568 | tf_op jit(solution)/shard_map/all_gather | solution.py:711
  90.9 8.7 %collective-permute-done.rest_1_ = bf16[3,192,256]{2,1,0:T(8,128)(2,1)S(1)} collective-permute-done((bf16[3,192,256]{2,1,0:T(8,128)(2,1)}, bf16[3,192,256]{2,1,0:T(8,128)(2,1)S(1)}, u32[]{:S(2)}, u32[]{:S(2)}) %collective-permute-start) | collective-permute-done | bytes 294944 | tf_op jit(solution)/shard_map/ppermute | solution.py:38
  111.4 21.6 %attend.2 = (bf16[192,256]{1,0:T(8,128)(2,1)}, bf16[192,256]{1,0:T(8,128)(2,1)}, bf16[192,256]{1,0:T(8,128)(2,1)}, bf16[192,256]{1,0:T(8,128)(2,1)}, f32[4,192,256]{2,1,0:T(8,128)}, /*index=5*/f32[4,3,1,256]{3,2,1,0:T(1,128)}) custom-call(s32[4,8]{1,0:T(4,128)} %and_convert_fusion.active, s32[4,1,256]{2,1,0:T(1,128)} %broadcast_in_dim.37.seg_row, ...), custom_call_target="tpu_custom_call" | custom-call | flops 805306368 | bytes 3932160 | tf_op jit(solution)/shard_map/attend/pallas_call | solution.py:168
  140.9 52.7 %all-gather.4.cloned.1.call-done.wo_ref.wu_ref.wd_ref.w_ref.rest_0_.rest_1_.rest_2_ = bf16[768,9216]{1,0:T(8,128)(2,1)} async-done(((bf16[24,9216]{1,0:T(8,128)(2,1)}), bf16[768,9216]{1,0:T(8,128)(2,1)}) %all-gather.4.cloned.1.call-update) | async-done | bytes 14155792 | tf_op jit(solution)/shard_map/all_gather | solution.py:711
  193.5 10.0 %feed.2 = (f32[256,768]{1,0:T(8,128)}, bf16[256,768]{1,0:T(8,128)(2,1)}, f32[256,768]{1,0:T(8,128)}, f32[256,768]{1,0:T(8,128)}) custom-call(s32[4]{0:T(128)} %iota_xor_fusion.order, f32[256,768]{1,0:T(8,128)} %bitcast_convert_fusion.1.x_ref, bf16[768,9216]{1,0:T(8,128)(2,1)} %all-gather.4.cloned.1.call-done.wo_ref.wu_ref.wd_ref.w_ref.rest_0_.rest_1_.rest_2_, ...), custom_call_target="tpu_custom_call" | custom-call | flops 2717908992 | bytes 10616832 | tf_op jit(solution)/shard_map/feed/pallas_call | solution.py:343
  228.6 21.6 %attend.3 = (bf16[192,256]{1,0:T(8,128)(2,1)}, bf16[192,256]{1,0:T(8,128)(2,1)}, bf16[192,256]{1,0:T(8,128)(2,1)}, bf16[192,256]{1,0:T(8,128)(2,1)}, f32[4,192,256]{2,1,0:T(8,128)}, /*index=5*/f32[4,3,1,256]{3,2,1,0:T(1,128)}) custom-call(s32[4,8]{1,0:T(4,128)} %and_convert_fusion.active, s32[4,1,256]{2,1,0:T(1,128)} %broadcast_in_dim.37.seg_row, ...), custom_call_target="tpu_custom_call" | custom-call | flops 805306368 | bytes 3932160 | tf_op jit(solution)/shard_map/attend/pallas_call | solution.py:168
  256.2 30.3 %all-gather.8.cloned.1.call-done.wo_ref.wu_ref.wd_ref.rest_0_.rest_1_.rest_2_ = bf16[768,6912]{1,0:T(8,128)(2,1)} async-done(((bf16[24,6912]{1,0:T(8,128)(2,1)}), bf16[768,6912]{1,0:T(8,128)(2,1)}) %all-gather.8.cloned.1.call-update) | async-done | bytes 10616848 | tf_op jit(solution)/shard_map/all_gather | solution.py:711
  287.2 10.0 %feed.3 = (f32[256,768]{1,0:T(8,128)}, bf16[256,768]{1,0:T(8,128)(2,1)}, f32[256,768]{1,0:T(8,128)}, f32[256,768]{1,0:T(8,128)}) custom-call(s32[4]{0:T(128)} %iota_xor_fusion.order, f32[256,768]{1,0:T(8,128)} %get-tuple-element.148.x_ref, bf16[768,6912]{1,0:T(8,128)(2,1)} %all-gather.8.cloned.1.call-done.wo_ref.wu_ref.wd_ref.rest_0_.rest_1_.rest_2_, ...), custom_call_target="tpu_custom_call" | custom-call | flops 2717908992 | bytes 10616832 | tf_op jit(solution)/shard_map/feed/pallas_call | solution.py:343
  297.2 17.4 %feed_back.2 = (bf16[8,864,768]{2,1,0:T(8,128)(2,1)}, f32[256,768]{1,0:T(8,128)}, f32[16,768]{1,0:T(8,128)}, bf16[192,256]{1,0:T(8,128)(2,1)}, bf16[192,256]{1,0...) custom-call(s32[4]{0:T(128)} %iota_xor_fusion.order, f32[256,768]{1,0:T(8,128)} %bitcast_convert_fusion.grad_ref, ...), custom_call_target="tpu_custom_call" | custom-call | flops 6643777536 | bytes 21233664 | tf_op jit(solution)/shard_map/feed_back/pallas_call | solution.py:454
  324.3 26.6 %attend_back.2 = (bf16[4,192,256]{2,1,0:T(8,128)(2,1)}, f32[4,2,192,256]{3,2,1,0:T(8,128)}, bf16[4,2,192,256]{3,2,1,0:T(8,128)(2,1)}) custom-call(s32[4,8]{1,0:T(4,128)} %and_convert_fusion.active, s32[4,1,256]{2,1,0:T(1,128)} %broadcast_in_dim.37.seg_row, s32[8,256,1]{2,1,0:T(8,128)} %select_convert_fusion.seg_col, ...), custom_call_target="tpu_custom_call" | custom-call | flops 2013265920 | bytes 7864320 | tf_op jit(solution)/shard_map/attend_back/pallas_call | solution.py:254
  359.5 12.7 %collective-permute-done.24.rest_1_ = bf16[3,192,256]{2,1,0:T(8,128)(2,1)S(1)} collective-permute-done((bf16[3,192,256]{2,1,0:T(8,128)(2,1)S(1)}, bf16[3,192,256]{2,1,0:T(8,128)(2,1)S(1)}, u32[]{:S(2)}, u32[]{:S(2)}) %collective-permute-start.24) | collective-permute-done | bytes 294944 | tf_op jit(solution)/shard_map/ppermute | solution.py:38
  373.1 11.1 %collective-permute-done.26.rest_3_ = bf16[3,192,256]{2,1,0:T(8,128)(2,1)S(1)} collective-permute-done((bf16[3,192,256]{2,1,0:T(8,128)(2,1)S(1)}, bf16[3,192,256]{2,1,0:T(8,128)(2,1)S(1)}, u32[]{:S(2)}, u32[]{:S(2)}) %collective-permute-start.26) | collective-permute-done | bytes 294944 | tf_op jit(solution)/shard_map/ppermute | solution.py:38
  385.0 7.5 %project_back.2 = (bf16[4,320,768]{2,1,0:T(8,128)(2,1)}, bf16[4,320,768]{2,1,0:T(8,128)(2,1)}, f32[256,768]{1,0:T(8,128)}) custom-call(s32[4]{0:T(128)} %iota_xor_fusion.order, s32[1]{0:T(128)} %bitcast.34.place, f32[256,768]{1,0:T(8,128)} %get-tuple-element.148.x_ref, f32[256,768]{1,0:T(8,128)} %get-tuple-element.161.grad_ref, ...), custom_call_target="tpu_custom_call" | custom-call | flops 1811939328 | bytes 7077888 | tf_op jit(solution)/shard_map/project_back/pallas_call | solution.py:542
  392.5 17.3 %feed_back.3 = (bf16[8,864,768]{2,1,0:T(8,128)(2,1)}, f32[256,768]{1,0:T(8,128)}, f32[16,768]{1,0:T(8,128)}, bf16[192,256]{1,0:T(8,128)(2,1)}, bf16[192,256]{1,0...) custom-call(s32[4]{0:T(128)} %iota_xor_fusion.order, f32[256,768]{1,0:T(8,128)} %get-tuple-element.188.grad_ref, ...), custom_call_target="tpu_custom_call" | custom-call | flops 6643777536 | bytes 21233664 | tf_op jit(solution)/shard_map/feed_back/pallas_call | solution.py:454
  423.1 10.6 %collective-permute-done.28.rest_9_ = bf16[192,256]{1,0:T(8,128)(2,1)} collective-permute-done((bf16[192,256]{1,0:T(8,128)(2,1)}, bf16[192,256]{1,0:T(8,128)(2,1)}, u32[]{:S(2)}, u32[]{:S(2)}) %collective-permute-start.28) | collective-permute-done | bytes 98336 | tf_op jit(solution)/shard_map/ppermute | solution.py:38
  436.8 26.0 %attend_back.3 = (bf16[4,192,256]{2,1,0:T(8,128)(2,1)}, f32[4,2,192,256]{3,2,1,0:T(8,128)}, bf16[4,2,192,256]{3,2,1,0:T(8,128)(2,1)}) custom-call(s32[4,8]{1,0:T(4,128)} %and_convert_fusion.active, s32[4,1,256]{2,1,0:T(1,128)} %broadcast_in_dim.37.seg_row, s32[8,256,1]{2,1,0:T(8,128)} %select_convert_fusion.seg_col, ...), custom_call_target="tpu_custom_call" | custom-call | flops 2013265920 | bytes 7864320 | tf_op jit(solution)/shard_map/attend_back/pallas_call | solution.py:254
  466.7 8.1 %collective-permute-done.34 = bf16[160,768]{1,0:T(8,128)(2,1)} collective-permute-done((bf16[160,768]{1,0:T(8,128)(2,1)}, bf16[160,768]{1,0:T(8,128)(2,1)}, u32[]{:S(2)}, u32[]{:S(2)}) %collective-permute-start.34) | collective-permute-done | bytes 245792 | tf_op jit(solution)/shard_map/ppermute | solution.py:38
  493.4 17.4 %collective-permute-done.37.rest_2_ = bf16[3,192,256]{2,1,0:T(8,128)(2,1)S(1)} collective-permute-done((bf16[3,192,256]{2,1,0:T(8,128)(2,1)S(1)}, bf16[3,192,256]{2,1,0:T(8,128)(2,1)S(1)}, u32[]{:S(2)}, u32[]{:S(2)}) %collective-permute-start.37) | collective-permute-done | bytes 294944 | tf_op jit(solution)/shard_map/ppermute | solution.py:38
  513.9 7.7 %project_back.3 = (bf16[4,320,768]{2,1,0:T(8,128)(2,1)}, bf16[4,320,768]{2,1,0:T(8,128)(2,1)}, f32[256,768]{1,0:T(8,128)}) custom-call(s32[4]{0:T(128)} %iota_xor_fusion.order, s32[1]{0:T(128)} %bitcast.34.place, f32[256,768]{1,0:T(8,128)} %bitcast_convert_fusion.1.x_ref, f32[256,768]{1,0:T(8,128)} %get-tuple-element.192.grad_ref, ...), custom_call_target="tpu_custom_call" | custom-call | flops 1811939328 | bytes 7077888 | tf_op jit(solution)/shard_map/project_back/pallas_call | solution.py:542
  540.3 19.6 %collective-permute-done.47 = bf16[80,768]{1,0:T(8,128)(2,1)S(1)} collective-permute-done((bf16[80,768]{1,0:T(8,128)(2,1)S(1)}, bf16[80,768]{1,0:T(8,128)(2,1)S(1)}, u32[]{:S(2)}, u32[]{:S(2)}) %collective-permute-start.47) | collective-permute-done | bytes 122912 | tf_op jit(solution)/shard_map/ppermute | solution.py:38
  559.9 11.5 %collective-permute-start.56 = (bf16[216,768]{1,0:T(8,128)(2,1)S(1)}, bf16[216,768]{1,0:T(8,128)(2,1)S(1)}, u32[]{:S(2)}, u32[]{:S(2)}) collective-permute-start(bf16[216,768]{1,0:T(8,128)(2,1)S(1)} %get-tuple-element.285), channel_id=1, source_target_pairs={{0,8},{8,0},{16,24},{24,16},{1,9},{9,1},{17,25},{25,17},{2,10},{10... | collective-permute-start | bytes 995336 | tf_op jit(solution)/shard_map/ppermute | solution.py:38
  579.3 8.7 %collective-permute-done.52 = bf16[2,160,768]{2,1,0:T(8,128)(2,1)S(1)} collective-permute-done((bf16[2,160,768]{2,1,0:T(8,128)(2,1)S(1)}, bf16[2,160,768]{2,1,0:T(8,128)(2,1)S(1)}, u32[]{:S(2)}, u32[]{:S(2)}) %collective-permute-start.52) | collective-permute-done | bytes 491552 | tf_op jit(solution)/shard_map/ppermute | solution.py:38
  609.7 18.7 %collective-permute-done.59 = bf16[80,768]{1,0:T(8,128)(2,1)S(1)} collective-permute-done((bf16[80,768]{1,0:T(8,128)(2,1)S(1)}, bf16[80,768]{1,0:T(8,128)(2,1)S(1)}, u32[]{:S(2)}, u32[]{:S(2)}) %collective-permute-start.59) | collective-permute-done | bytes 122912 | tf_op jit(solution)/shard_map/ppermute | solution.py:38
  631.5 12.0 %collective-permute-done.60 = bf16[80,768]{1,0:T(8,128)(2,1)S(1)} collective-permute-done((bf16[80,768]{1,0:T(8,128)(2,1)S(1)}, bf16[80,768]{1,0:T(8,128)(2,1)S(1)}, u32[]{:S(2)}, u32[]{:S(2)}) %collective-permute-start.60) | collective-permute-done | bytes 122912 | tf_op jit(solution)/shard_map/ppermute | solution.py:38
  (363 shorter events, 207.0 us)
Async XLA Ops:
  7.2 72.1 %all-gather.6.cloned.1.call-start = ((), (), s32[]{:S(2)}) async-start(), calls=%async_computation.3 | async-start | bytes 3852288 | tf_op jit(solution)/shard_map/all_gather | solution.py:711
  15.8 177.7 %all-gather.4.cloned.1.call-start = ((), (), s32[]{:S(2)}) async-start(), calls=%async_computation.2 | async-start | bytes 14598144 | tf_op jit(solution)/shard_map/all_gather | solution.py:711
  21.7 264.7 %all-gather.8.cloned.1.call-start = ((), (), s32[]{:S(2)}) async-start(), calls=%async_computation.4 | async-start | bytes 10948608 | tf_op jit(solution)/shard_map/all_gather | solution.py:711
  22.4 444.2 %reduce-scatter.3.cloned.1.call-start = ((), (), s32[]{:S(2)}) async-start(), calls=%async_computation.5 | async-start | bytes 11943936 | tf_op jit(solution)/shard_map/reduce_scatter | solution.py:820
  250.2 36.2 %collective-permute-start.17 = (bf16[192,256]{1,0:T(8,128)(2,1)}, bf16[192,256]{1,0:T(8,128)(2,1)S(1)}, u32[]{:S(2)}, u32[]{:S(2)}) collective-permute-start(bf16[192,256]{1,0:T(8,128)(2,1)} %get-tuple-element.154), channel_id=1, source_target_pairs={{0,2},{1,3},{2,0},{3,1},{4,6},{5,7},{6,4},{7,5},{8,10},{9,11},{10,... | collective-permute-start | bytes 294920 | tf_op jit(solution)/shard_map/ppermute | solution.py:38
  250.5 35.9 %collective-permute-start.18 = (bf16[192,256]{1,0:T(8,128)(2,1)}, bf16[192,256]{1,0:T(8,128)(2,1)S(1)}, u32[]{:S(2)}, u32[]{:S(2)}) collective-permute-start(bf16[192,256]{1,0:T(8,128)(2,1)} %get-tuple-element.155), channel_id=1, source_target_pairs={{0,4},{1,5},{2,6},{3,7},{4,0},{5,1},{6,2},{7,3},{8,12},{9,13},{10,... | collective-permute-start | bytes 294920 | tf_op jit(solution)/shard_map/ppermute | solution.py:38
  252.4 34.1 %collective-permute-start.19 = (bf16[192,256]{1,0:T(8,128)(2,1)}, bf16[192,256]{1,0:T(8,128)(2,1)S(1)}, u32[]{:S(2)}, u32[]{:S(2)}) collective-permute-start(bf16[192,256]{1,0:T(8,128)(2,1)} %get-tuple-element.156), channel_id=1, source_target_pairs={{0,6},{1,7},{2,4},{3,5},{4,2},{5,3},{6,0},{7,1},{8,14},{9,15},{10,... | collective-permute-start | bytes 294920 | tf_op jit(solution)/shard_map/ppermute | solution.py:38
  314.6 224.5 %reduce-scatter.5.cloned.1.call-start = ((), (), s32[]{:S(2)}) async-start(), calls=%async_computation.6 | async-start | bytes 11943936 | tf_op jit(solution)/shard_map/reduce_scatter | solution.py:820
  357.8 26.5 %collective-permute-start.26 = (bf16[3,192,256]{2,1,0:T(8,128)(2,1)S(1)}, bf16[3,192,256]{2,1,0:T(8,128)(2,1)S(1)}, u32[]{:S(2)}, u32[]{:S(2)}) collective-permute-start(bf16[3,192,256]{2,1,0:T(8,128)(2,1)S(1)} %get-tuple-element.183), channel_id=1, source_target_pairs={{0,6},{1,7},{2,4},{3,5},{4,2},{5,3},{6,0},{7,1},{8,14},{9,15},{10,... | collective-permute-start | bytes 884744 | tf_op jit(solution)/shard_map/ppermute | solution.py:38
  482.0 28.8 %collective-permute-start.42 = (bf16[216,768]{1,0:T(8,128)(2,1)S(1)}, bf16[216,768]{1,0:T(8,128)(2,1)S(1)}, u32[]{:S(2)}, u32[]{:S(2)}) collective-permute-start(bf16[216,768]{1,0:T(8,128)(2,1)S(1)} %get-tuple-element.288), channel_id=1, source_target_pairs={{0,8},{8,0},{16,24},{24,16},{1,9},{9,1},{17,25},{25,17},{2,10},{10... | collective-permute-start | bytes 995336 | tf_op jit(solution)/shard_map/ppermute | solution.py:38
  484.5 29.4 %collective-permute-start.43 = (bf16[216,768]{1,0:T(8,128)(2,1)S(1)}, bf16[216,768]{1,0:T(8,128)(2,1)S(1)}, u32[]{:S(2)}, u32[]{:S(2)}) collective-permute-start(bf16[216,768]{1,0:T(8,128)(2,1)S(1)} %get-tuple-element.287), channel_id=1, source_target_pairs={{0,16},{8,24},{16,0},{24,8},{1,17},{9,25},{17,1},{25,9},{2,18},{10... | collective-permute-start | bytes 995336 | tf_op jit(solution)/shard_map/ppermute | solution.py:38
  489.9 24.0 %collective-permute-start.44 = (bf16[216,768]{1,0:T(8,128)(2,1)S(1)}, bf16[216,768]{1,0:T(8,128)(2,1)S(1)}, u32[]{:S(2)}, u32[]{:S(2)}) collective-permute-start(bf16[216,768]{1,0:T(8,128)(2,1)S(1)} %get-tuple-element.286), channel_id=1, source_target_pairs={{0,24},{8,16},{16,8},{24,0},{1,25},{9,17},{17,9},{25,1},{2,26},{10... | collective-permute-start | bytes 995336 | tf_op jit(solution)/shard_map/ppermute | solution.py:38
  521.6 52.3 %collective-permute-start.51 = (bf16[4,320,768]{2,1,0:T(8,128)(2,1)}, bf16[4,320,768]{2,1,0:T(8,128)(2,1)}, u32[]{:S(2)}, u32[]{:S(2)}) collective-permute-start(bf16[4,320,768]{2,1,0:T(8,128)(2,1)} %get-tuple-element.240), channel_id=1, source_target_pairs={{0,1},{1,0},{2,3},{3,2},{4,5},{5,4},{6,7},{7,6},{8,9},{9,8},{10,11... | collective-permute-start | bytes 5898248 | tf_op jit(solution)/shard_map/ppermute | solution.py:38
  529.4 42.1 %collective-permute-start.48 = (bf16[216,768]{1,0:T(8,128)(2,1)S(1)}, bf16[216,768]{1,0:T(8,128)(2,1)S(1)}, u32[]{:S(2)}, u32[]{:S(2)}) collective-permute-start(bf16[216,768]{1,0:T(8,128)(2,1)S(1)} %fusion.7), channel_id=1, source_target_pairs={{0,8},{8,0},{16,24},{24,16},{1,9},{9,1},{17,25},{25,17},{2,10},{10... | collective-permute-start | bytes 995336 | tf_op jit(solution)/shard_map/ppermute | solution.py:38
  531.3 40.2 %collective-permute-start.49 = (bf16[216,768]{1,0:T(8,128)(2,1)S(1)}, bf16[216,768]{1,0:T(8,128)(2,1)}, u32[]{:S(2)}, u32[]{:S(2)}) collective-permute-start(bf16[216,768]{1,0:T(8,128)(2,1)S(1)} %fusion.7), channel_id=1, source_target_pairs={{0,16},{8,24},{16,0},{24,8},{1,17},{9,25},{17,1},{25,9},{2,18},{10... | collective-permute-start | bytes 995336 | tf_op jit(solution)/shard_map/ppermute | solution.py:38
  533.6 40.3 %collective-permute-start.50 = (bf16[216,768]{1,0:T(8,128)(2,1)S(1)}, bf16[216,768]{1,0:T(8,128)(2,1)}, u32[]{:S(2)}, u32[]{:S(2)}) collective-permute-start(bf16[216,768]{1,0:T(8,128)(2,1)S(1)} %fusion.7), channel_id=1, source_target_pairs={{0,24},{8,16},{16,8},{24,0},{1,25},{9,17},{17,9},{25,1},{2,26},{10... | collective-permute-start | bytes 995336 | tf_op jit(solution)/shard_map/ppermute | solution.py:38
  559.9 31.0 %collective-permute-start.56 = (bf16[216,768]{1,0:T(8,128)(2,1)S(1)}, bf16[216,768]{1,0:T(8,128)(2,1)S(1)}, u32[]{:S(2)}, u32[]{:S(2)}) collective-permute-start(bf16[216,768]{1,0:T(8,128)(2,1)S(1)} %get-tuple-element.285), channel_id=1, source_target_pairs={{0,8},{8,0},{16,24},{24,16},{1,9},{9,1},{17,25},{25,17},{2,10},{10... | collective-permute-start | bytes 995336 | tf_op jit(solution)/shard_map/ppermute | solution.py:38
  571.5 25.8 %collective-permute-start.57 = (bf16[216,768]{1,0:T(8,128)(2,1)S(1)}, bf16[216,768]{1,0:T(8,128)(2,1)S(1)}, u32[]{:S(2)}, u32[]{:S(2)}) collective-permute-start(bf16[216,768]{1,0:T(8,128)(2,1)S(1)} %get-tuple-element.284), channel_id=1, source_target_pairs={{0,16},{8,24},{16,0},{24,8},{1,17},{9,25},{17,1},{25,9},{2,18},{10... | collective-permute-start | bytes 995336 | tf_op jit(solution)/shard_map/ppermute | solution.py:38
  571.5 25.8 %collective-permute-start.58 = (bf16[216,768]{1,0:T(8,128)(2,1)S(1)}, bf16[216,768]{1,0:T(8,128)(2,1)S(1)}, u32[]{:S(2)}, u32[]{:S(2)}) collective-permute-start(bf16[216,768]{1,0:T(8,128)(2,1)S(1)} %get-tuple-element.283), channel_id=1, source_target_pairs={{0,24},{8,16},{16,8},{24,0},{1,25},{9,17},{17,9},{25,1},{2,26},{10... | collective-permute-start | bytes 995336 | tf_op jit(solution)/shard_map/ppermute | solution.py:38
  598.4 45.1 %collective-permute-start.62 = (bf16[216,768]{1,0:T(8,128)(2,1)S(1)}, bf16[216,768]{1,0:T(8,128)(2,1)S(1)}, u32[]{:S(2)}, u32[]{:S(2)}) collective-permute-start(bf16[216,768]{1,0:T(8,128)(2,1)S(1)} %fusion.4), channel_id=1, source_target_pairs={{0,8},{8,0},{16,24},{24,16},{1,9},{9,1},{17,25},{25,17},{2,10},{10... | collective-permute-start | bytes 995336 | tf_op jit(solution)/shard_map/ppermute | solution.py:38
  604.3 39.2 %collective-permute-start.63 = (bf16[216,768]{1,0:T(8,128)(2,1)S(1)}, bf16[216,768]{1,0:T(8,128)(2,1)S(1)}, u32[]{:S(2)}, u32[]{:S(2)}) collective-permute-start(bf16[216,768]{1,0:T(8,128)(2,1)S(1)} %fusion.4), channel_id=1, source_target_pairs={{0,16},{8,24},{16,0},{24,8},{1,17},{9,25},{17,1},{25,9},{2,18},{10... | collective-permute-start | bytes 995336 | tf_op jit(solution)/shard_map/ppermute | solution.py:38
  605.0 38.5 %collective-permute-start.64 = (bf16[216,768]{1,0:T(8,128)(2,1)S(1)}, bf16[216,768]{1,0:T(8,128)(2,1)S(1)}, u32[]{:S(2)}, u32[]{:S(2)}) collective-permute-start(bf16[216,768]{1,0:T(8,128)(2,1)S(1)} %fusion.4), channel_id=1, source_target_pairs={{0,24},{8,16},{16,8},{24,0},{1,25},{9,17},{17,9},{25,1},{2,26},{10... | collective-permute-start | bytes 995336 | tf_op jit(solution)/shard_map/ppermute | solution.py:38
  607.0 21.5 %collective-permute-start.59 = (bf16[80,768]{1,0:T(8,128)(2,1)S(1)}, bf16[80,768]{1,0:T(8,128)(2,1)S(1)}, u32[]{:S(2)}, u32[]{:S(2)}) collective-permute-start(bf16[80,768]{1,0:T(8,128)(2,1)S(1)} %get-tuple-element.303), channel_id=1, source_target_pairs={{0,8},{8,0},{16,24},{24,16},{1,9},{9,1},{17,25},{25,17},{2,10},{10... | collective-permute-start | bytes 368648 | tf_op jit(solution)/shard_map/ppermute | solution.py:38
  608.1 35.4 %collective-permute-start.60 = (bf16[80,768]{1,0:T(8,128)(2,1)S(1)}, bf16[80,768]{1,0:T(8,128)(2,1)S(1)}, u32[]{:S(2)}, u32[]{:S(2)}) collective-permute-start(bf16[80,768]{1,0:T(8,128)(2,1)S(1)} %get-tuple-element.302), channel_id=1, source_target_pairs={{0,16},{8,24},{16,0},{24,8},{1,17},{9,25},{17,1},{25,9},{2,18},{10... | collective-permute-start | bytes 368648 | tf_op jit(solution)/shard_map/ppermute | solution.py:38
  (100 other events, 1010.9 us)
Sparse Core Ops, SparseCore 0:
  15.9 63.3 all-gather.5
  82.8 110.7 all-gather.3
  197.0 89.3 all-gather.7
  314.7 93.5 reduce-scatter.2
  411.7 106.0 reduce-scatter.4

commit v3 on v2

--- a/solution.py
+++ b/solution.py
@@ -72,6 +72,36 @@
 
 SMEM_SPEC = pl.BlockSpec(memory_space=pltpu.SMEM)
 ANY_SPEC = pl.BlockSpec(memory_space=pl.ANY)
+
+
+def pack_body(weight, *rest):
+    items, (out, extra) = rest[:-2], rest[-2:]
+    width = weight.shape[2]
+    extra[...] = jnp.zeros_like(extra)
+    at = 0
+    for item in items:
+        rows = item[...].astype(F32)
+        for first in range(0, rows.shape[1], 128):
+            part = rows[:, first : first + 128]
+            extra[at : at + part.shape[0], : part.shape[1]] = part
+            at += part.shape[0]
+    out[:, :width] = weight[0]
+    out[:, width:] = extra[...].astype(BF16)
+
+
+def pack(weights, items):
+    depth, width = weights.shape[1:]
+    return pl.pallas_call(
+        pack_body,
+        out_shape=jax.ShapeDtypeStruct((depth, width + 128), BF16),
+        grid=(1,),
+        in_specs=[pl.BlockSpec((1, depth, width), lambda j: (0, 0, 0))]
+        + [resident(item.shape) for item in items],
+        out_specs=resident((depth, width + 128)),
+        scratch_shapes=[pltpu.VMEM((depth, 128), F32)],
+        compiler_params=params(),
+        name="pack",
+    )(weights, *items)
 
 
 def project_body(groups, span, order, x_ref, w_ref, b_ref, *rest):
@@ -622,19 +652,25 @@
     rows, width = total.shape
     if dp_size != 4:
         return lax.psum(total, "dp")
-    pieces = total.reshape(dp_size, rows // dp_size, width)
-
-    def piece(m):
-        return lax.dynamic_index_in_dim(pieces, dp_me ^ m, 0, keepdims=False)
-
-    arrived = yield [exchange(piece(m), "dp", dp_size, m) for m in range(1, dp_size)]
-    mine = sum((item.astype(F32) for item in arrived), piece(0).astype(F32)).astype(BF16)
-    arrived = yield [exchange(mine, "dp", dp_size, m) for m in range(1, dp_size)]
-    stack = [mine] + list(arrived)
+    bits = [(dp_me >> b) & 1 for b in range(2)]
+    for b in range(2):
+        halves = total.reshape(2, -1, width)
+        leave = lax.dynamic_index_in_dim(halves, 1 - bits[b], 0, keepdims=False)
+        (arrived,) = yield [exchange(leave, "dp", dp_size, 1 << b)]
+        total = add_low(lax.dynamic_index_in_dim(halves, bits[b], 0, keepdims=False), arrived)
+    for b in (1, 0):
+        (arrived,) = yield [exchange(total, "dp", dp_size, 1 << b)]
+        flip = bits[b] != 0
+        pair = [jnp.where(flip, arrived, total), jnp.where(flip, total, arrived)]
+        total = jnp.concatenate(pair, axis=0)
+    return total
+
+
+def in_order(stack, place):
     for bit in (1, 2):
-        flip = (dp_me & bit) != 0
-        stack = [jnp.where(flip, stack[i ^ bit], stack[i]) for i in range(dp_size)]
-    return jnp.concatenate(stack, axis=0)
+        flip = (place & bit) != 0
+        stack = [jnp.where(flip, stack[i ^ bit], stack[i]) for i in range(4)]
+    return stack
 
 
 def add_low(a, b):
@@ -674,26 +710,23 @@
     order = (me // members) ^ jnp.arange(groups, dtype=jnp.int32)
     place = me.reshape(1).astype(jnp.int32)
     both = ("dp", "seq")
-    plain = depth % 8 != 0 or dp_size != 4
-
-    vectors = jnp.stack(
-        [
-            output_bias,
-            attention_gain,
-            attention_shift,
-            down_bias,
-            feed_gain,
-            feed_shift,
-            query_bias,
-            value_bias,
-        ],
-        axis=1,
-    )
-    flat = jnp.concatenate(
-        [vectors.reshape(-1), up_bias.reshape(-1), segment_ids.astype(BF16).reshape(-1)]
-    )
-    used = flat.shape[0]
-    flat = jnp.pad(flat, (0, -used % 1024)).reshape(-1, 128)
+    def lines(value):
+        return jnp.pad(value, ((0, 0), (0, 128 - value.shape[1])))
+
+    id_rows = -(-tokens // 128)
+    shards = [
+        output_bias,
+        attention_gain,
+        attention_shift,
+        down_bias,
+        feed_gain,
+        feed_shift,
+        query_bias,
+        value_bias,
+        up_bias,
+    ]
+    extra_rows = LAYERS * 9 + id_rows
+    plain = depth % 8 != 0 or dp_size != 4 or extra_rows > depth
 
     def swap_groups(items):
         return [items[0]] + [
@@ -710,6 +743,13 @@
     def gathered(shard):
         return lax.all_gather(shard, both, axis=0, tiled=True)
 
+    def over_dp(shard):
+        return [exchange(shard, "dp", dp_size, m) for m in range(1, dp_size)]
+
+    def over_seq(shard, arrived):
+        stack = jnp.stack(in_order([shard] + list(arrived), dp_me))
+        return lax.all_gather(stack, "seq", axis=1, tiled=True).reshape(width, -1)
+
     def rest_shard(layer):
         down = down_weight[layer].reshape(blocks, depth, width)
         return [down[t] for t in range(blocks)] + [up_weight[layer], output_weight[layer]]
@@ -718,7 +758,10 @@
         return (whole, 2 * blocks), (whole, blocks), (whole, blocks, depth)
 
     if plain:
-        table = lax.all_gather(flat, both, axis=0, tiled=False)
+        ids = jnp.pad(segment_ids.astype(BF16), ((0, 0), (0, id_rows * 128 - tokens)))
+        extra = [lines(item) for item in shards] + [ids.reshape(id_rows, 128)]
+        extra = jnp.concatenate(extra, axis=0)
+        table = lax.all_gather(extra, both, axis=0, tiled=False)
         w_project = [(gathered(project_weight[layer]), 0) for layer in range(LAYERS)]
         w_rest = [
             (
@@ -729,39 +772,35 @@
             for layer in range(LAYERS)
         ]
     else:
-        extra = jnp.pad(flat.reshape(-1), (0, depth * 128 - flat.size)).reshape(depth, 128)
-        first = gathered(jnp.concatenate([project_weight[0], extra], axis=1))
-        table = first[:, 3 * width :]
-        w_project, w_rest = [(first, 0)], []
+        starting = pack(project_weight, shards + [segment_ids])
+        shards = []
         for layer in range(LAYERS):
             parts = rest_shard(layer)
             if layer + 1 < LAYERS:
                 parts.append(project_weight[layer + 1])
-            whole = gathered(jnp.concatenate(parts, axis=1))
-            w_rest.append(rest_of(whole))
-            w_project.append((whole, 2 * blocks + 1))
-
-    table = table.reshape(everyone, -1)
-    small_rows = LAYERS * 8 * depth
-    up_share = inner_width // everyone
+            shards.append(jnp.concatenate(parts, axis=1))
+        arrived, shards[0] = lax.optimization_barrier((over_dp(starting), shards[0]))
+        ahead = over_dp(shards[0])
+        whole = over_seq(starting, arrived)
+        table = whole[:, 3 * width :].reshape(everyone, depth, 128)
+        w_project, w_rest = [(whole, 0)], []
+
     vectors = (
-        table[:, :small_rows]
-        .reshape(everyone, LAYERS, 8, depth)
-        .transpose(1, 2, 0, 3)
-        .reshape(LAYERS, 8, width)
+        table[:, : LAYERS * 8, :depth]
+        .transpose(1, 0, 2)
+        .reshape(8, LAYERS, width)
+        .transpose(1, 0, 2)
         .astype(F32)
     )
     up_biases = (
-        table[:, small_rows : small_rows + LAYERS * up_share]
-        .reshape(everyone, LAYERS, up_share)
+        table[:, LAYERS * 8 : LAYERS * 9, : inner_width // everyone]
         .transpose(1, 0, 2)
         .reshape(LAYERS, blocks, 1, width)
         .astype(F32)
     )
+    ids = table[:, LAYERS * 9 : LAYERS * 9 + id_rows].reshape(everyone, -1)[:, :tokens]
     relative = jnp.array([r * members + j for j in range(members) for r in range(groups)], jnp.int32)
-    segments = jnp.take(
-        table[:, used - tokens : used], dp_me * seq_size + (me ^ relative), axis=0
-    ).astype(jnp.int32)
+    segments = jnp.take(ids, dp_me * seq_size + (me ^ relative), axis=0).astype(jnp.int32)
     first_id, last_id = segments[:, 0], segments[:, -1]
     active = (
         (first_id[:groups, None] <= last_id[None, :])
@@ -778,10 +817,20 @@
     current = states[0].astype(F32)
     saved = []
     for layer in range(LAYERS):
+        if not plain:
+            whole = after if layer else over_seq(shards[0], ahead)
+            w_rest.append(rest_of(whole))
+            w_project.append((whole, 2 * blocks + 1))
         made = projected(layer, current)
-        parts = with_members(swap_groups(made))
+        parts = tuple(with_members(swap_groups(made)))
+        if not plain and layer + 1 < LAYERS:
+            parts, shards[layer + 1] = lax.optimization_barrier((parts, shards[layer + 1]))
+            ahead = over_dp(shards[layer + 1])
         *mixed, exact, log_total = attend(active, seg_row, seg_col, parts, groups, members)
         contexts = swap_groups(mixed)
+        if not plain and layer + 1 < LAYERS:
+            contexts, ahead = lax.optimization_barrier((contexts, ahead))
+            after = over_seq(shards[layer + 1], ahead)
         w_output, w_up, w_down = w_rest[layer]
         sum_first, low, sum_second, following = feed(
             order,
@@ -823,25 +872,27 @@
         grad_mixed = tick(behind, tuple(grad_mixed))
         grads = tuple(swap_groups(grad_mixed))
         grads = tick(behind, grads)
+        if layer + 1 < LAYERS:
+            grads, later = lax.optimization_barrier((grads, shares[layer + 1]))
+            feeds[layer + 1] = Stream(dp_steps(later, dp_size, dp_me))
+            behind = behind + [feeds[layer + 1]]
         grad_query, kept_kv, *sent_kv = attend_back(
             active, seg_row, seg_col, parts, grads, exact, log_total, groups, members
         )
         for j in range(1, members):
             kept_kv = kept_kv + exchange(sent_kv[j - 1], "seq", seq_size, j).astype(F32)
-        messages = [
+        messages = tuple(
             jnp.concatenate([grad_query[r][None], kept_kv[r].astype(BF16)], axis=0)
             for r in range(groups)
-        ]
-        if layer + 1 < LAYERS:
-            messages, later = lax.optimization_barrier((tuple(messages), shares[layer + 1]))
-            feeds[layer + 1] = Stream(dp_steps(later, dp_size, dp_me))
-        messages = tick(behind, tuple(messages))
-        behind += [item for item in feeds if item is not None]
+        )
+        messages = tick(behind, messages)
         pieces = tuple(swap_groups(messages))
         pieces = tick(behind, pieces)
         own, send, grad = project_back(
             order, place, entered, grad_first, w_project[layer], small, pieces, seq_size
         )
+        if layer + 1 < LAYERS:
+            own, send = tick(behind, (own, send))
         backs[layer] = Stream(sum_steps(own, send, seq_size, dp_size, dp_me))
         behind = behind + [backs[layer]]
     tick(behind)

time: 666 us -> 602 us (0.904)
  waiting for transfers between devices: 328 us -> 300 us
  Pallas kernels: 175 us -> 157 us
  starting transfers between devices: 87.4 us -> 70.9 us
  local copies, waits for them, and re-layouts: 33.2 us -> 21.7 us
    all_gather x3, waiting for transfers between devices: 138 us -> 23.9 us  [over_seq(): return lax.all_gather(stack, 'seq', axis=1, tiled=True).reshape(width, -1)]
    ppermute x68 -> x69, waiting for transfers between devices: 189 us -> 276 us  [exchange(): return lax.ppermute(value, axis, [(i, i ^ mask) for i in range(size)])]
    ppermute x68 -> x69, starting transfers between devices: 87.2 us -> 70.3 us  [exchange(): return lax.ppermute(value, axis, [(i, i ^ mask) for i in range(size)])]
    pallas_call x2, Pallas kernels: 52.6 us -> 41.7 us  [attend_back(): pl.pallas_call(functools.partial(attend_back_body, groups, members, heads...]
    pallas_call x2, Pallas kernels: 43.1 us -> 34 us  [attend(): pl.pallas_call(functools.partial(attend_body, groups, members, heads), ou...]
    unnamed x116 -> x90, local copies, waits for them, and re-layouts: 17.3 us -> 9.39 us
  transfers between devices with their start and end apart: 73 -> 74, of which waited for: 33 -> 43; matrix products, arithmetic and copies ran while one was open for 6% -> 7% of each run, Pallas kernels for 22% -> 22%
where the time goes in v3:
time: 602 us; the launch traced here: 596 us
  waiting for transfers between devices  300 us (50%)
  Pallas kernels  157 us (26%)
  starting transfers between devices  70.9 us (12%)
  other arithmetic  31.3 us (5%)
  local copies, waits for them, and re-layouts  21.7 us (4%)
  between operations  14.8 us (2%)
    ppermute x69, waiting for transfers between devices, exchange(): return lax.ppermute(value, axis, [(i, i ^ mask) for i in range(size)])  276 us
    ppermute x69, starting transfers between devices, exchange(): return lax.ppermute(value, axis, [(i, i ^ mask) for i in range(size)])  70.3 us
    pallas_call x2, Pallas kernels, attend_back(): pl.pallas_call(functools.partial(attend_back_body, groups, members, heads...  41.7 us
    pallas_call x2, Pallas kernels, feed_back(): pl.pallas_call(functools.partial(feed_back_body, groups, span, blocks, de...  34.5 us
    pallas_call x2, Pallas kernels, attend(): pl.pallas_call(functools.partial(attend_body, groups, members, heads), ou...  34 us
    all_gather x3, waiting for transfers between devices, over_seq(): return lax.all_gather(stack, 'seq', axis=1, tiled=True).reshape(width, -1)  23.9 us
    pallas_call x2, Pallas kernels, feed(): pl.pallas_call(functools.partial(feed_body, groups, span, blocks, pieces,...  20 us
    pallas_call x2, Pallas kernels, project_back(): pl.pallas_call(functools.partial(project_back_body, groups, span, devices...  15.1 us
  transfers between devices with their start and end apart: 74, of which 43 were waited for; matrix products, arithmetic and copies ran while one was open for 7% of the time, Pallas kernels for 22%

profile of v3, /device:TPU:0, one launch (start us, length us, event | category | flops | bytes accessed | tf_op | source)
XLA Modules:
  0.0 595.8 jit_solution(8652599405436445421)
XLA Ops:
  30.3 10.5 %collective-permute-done.3 = bf16[24,9216]{1,0:T(8,128)(2,1)S(1)} collective-permute-done((bf16[24,9216]{1,0:T(8,128)(2,1)S(1)}, bf16[24,9216]{1,0:T(8,128)(2,1)S(1)}, u32[]{:S(2)}, u32[]{:S(2)}) %collective-permute-start.3) | collective-permute-done | bytes 442400 | tf_op jit(solution)/shard_map/ppermute | solution.py:38
  40.9 24.9 %collective-permute-done.4 = bf16[24,9216]{1,0:T(8,128)(2,1)S(1)} collective-permute-done((bf16[24,9216]{1,0:T(8,128)(2,1)S(1)}, bf16[24,9216]{1,0:T(8,128)(2,1)S(1)}, u32[]{:S(2)}, u32[]{:S(2)}) %collective-permute-start.4) | collective-permute-done | bytes 442400 | tf_op jit(solution)/shard_map/ppermute | solution.py:38
  80.8 11.9 %collective-permute-done.6.rest_1_ = bf16[3,192,256]{2,1,0:T(8,128)(2,1)S(1)} collective-permute-done((bf16[3,192,256]{2,1,0:T(8,128)(2,1)}, bf16[3,192,256]{2,1,0:T(8,128)(2,1)S(1)}, u32[]{:S(2)}, u32[]{:S(2)}) %collective-permute-start.6) | collective-permute-done | bytes 294944 | tf_op jit(solution)/shard_map/ppermute | solution.py:38
  94.6 11.2 %collective-permute-done.8.rest_3_ = bf16[3,192,256]{2,1,0:T(8,128)(2,1)S(1)} collective-permute-done((bf16[3,192,256]{2,1,0:T(8,128)(2,1)}, bf16[3,192,256]{2,1,0:T(8,128)(2,1)S(1)}, u32[]{:S(2)}, u32[]{:S(2)}) %collective-permute-start.8) | collective-permute-done | bytes 294944 | tf_op jit(solution)/shard_map/ppermute | solution.py:38
  113.4 17.0 %attend.2 = (bf16[192,256]{1,0:T(8,128)(2,1)}, bf16[192,256]{1,0:T(8,128)(2,1)}, bf16[192,256]{1,0:T(8,128)(2,1)}, bf16[192,256]{1,0:T(8,128)(2,1)}, f32[4,192,256]{2,1,0:T(8,128)}, /*index=5*/f32[4,3,1,256]{3,2,1,0:T(1,128)}) custom-call(s32[4,8]{1,0:T(4,128)} %and_convert_fusion.active, s32[4,1,256]{2,1,0:T(1,128)} %broadcast_in_dim.37.seg_row, ...), custom_call_target="tpu_custom_call" | custom-call | flops 805306368 | bytes 3932160 | tf_op jit(solution)/shard_map/attend/pallas_call | solution.py:198
  150.0 13.2 %all-gather.4.cloned.1.call-done = bf16[4,192,9216]{2,1,0:T(8,128)(2,1)} async-done(((bf16[4,24,9216]{2,1,0:T(8,128)(2,1)}), bf16[4,192,9216]{2,1,0:T(8,128)(2,1)}) %all-gather.4.cloned.1.call-update) | async-done | bytes 14155792 | tf_op jit(solution)/shard_map/all_gather | solution.py:751
  163.2 10.0 %feed.2 = (f32[256,768]{1,0:T(8,128)}, bf16[256,768]{1,0:T(8,128)(2,1)}, f32[256,768]{1,0:T(8,128)}, f32[256,768]{1,0:T(8,128)}) custom-call(s32[4]{0:T(128)} %iota_xor_fusion.order, f32[256,768]{1,0:T(8,128)} %bitcast_convert_fusion.1.x_ref, bf16[768,9216]{1,0:T(8,128)(2,1)} %bitcast.260, bf16[768,9216]{1,0:T(8,128)(2,1)} %bitcast.261, ...), custom_call_target="tpu_custom_call" | custom-call | flops 2717908992 | bytes 10616832 | tf_op jit(solution)/shard_map/feed/pallas_call | solution.py:373
  181.8 12.9 %collective-permute-done.19.rest_1_ = bf16[3,192,256]{2,1,0:T(8,128)(2,1)S(1)} collective-permute-done((bf16[3,192,256]{2,1,0:T(8,128)(2,1)}, bf16[3,192,256]{2,1,0:T(8,128)(2,1)S(1)}, u32[]{:S(2)}, u32[]{:S(2)}) %collective-permute-start.19) | collective-permute-done | bytes 294944 | tf_op jit(solution)/shard_map/ppermute | solution.py:38
  206.6 17.0 %attend.3 = (bf16[192,256]{1,0:T(8,128)(2,1)}, bf16[192,256]{1,0:T(8,128)(2,1)}, bf16[192,256]{1,0:T(8,128)(2,1)}, bf16[192,256]{1,0:T(8,128)(2,1)}, f32[4,192,256]{2,1,0:T(8,128)}, /*index=5*/f32[4,3,1,256]{3,2,1,0:T(1,128)}) custom-call(s32[4,8]{1,0:T(4,128)} %and_convert_fusion.active, s32[4,1,256]{2,1,0:T(1,128)} %broadcast_in_dim.37.seg_row, ...), custom_call_target="tpu_custom_call" | custom-call | flops 805306368 | bytes 3932160 | tf_op jit(solution)/shard_map/attend/pallas_call | solution.py:198
  235.7 10.6 %all-gather.8.cloned.1.call-done = bf16[4,192,6912]{2,1,0:T(8,128)(2,1)} async-done(((bf16[4,24,6912]{2,1,0:T(8,128)(2,1)}), bf16[4,192,6912]{2,1,0:T(8,128)(2,1)}) %all-gather.8.cloned.1.call-update) | async-done | bytes 10616848 | tf_op jit(solution)/shard_map/all_gather | solution.py:751
  246.3 10.0 %feed.3 = (f32[256,768]{1,0:T(8,128)}, bf16[256,768]{1,0:T(8,128)(2,1)}, f32[256,768]{1,0:T(8,128)}, f32[256,768]{1,0:T(8,128)}) custom-call(s32[4]{0:T(128)} %iota_xor_fusion.order, f32[256,768]{1,0:T(8,128)} %get-tuple-element.178.x_ref, bf16[768,6912]{1,0:T(8,128)(2,1)} %bitcast.268, bf16[768,6912]{1,0:T(8,128)(2,1)} %bitcast.269, ...), custom_call_target="tpu_custom_call" | custom-call | flops 2717908992 | bytes 10616832 | tf_op jit(solution)/shard_map/feed/pallas_call | solution.py:373
  256.3 17.2 %feed_back.2 = (bf16[8,864,768]{2,1,0:T(8,128)(2,1)}, f32[256,768]{1,0:T(8,128)}, f32[16,768]{1,0:T(8,128)}, bf16[192,256]{1,0:T(8,128)(2,1)}, bf16[192,256]{1,0...) custom-call(s32[4]{0:T(128)} %iota_xor_fusion.order, f32[256,768]{1,0:T(8,128)} %bitcast_convert_fusion.grad_ref, ...), custom_call_target="tpu_custom_call" | custom-call | flops 6643777536 | bytes 21233664 | tf_op jit(solution)/shard_map/feed_back/pallas_call | solution.py:484
  283.4 21.4 %attend_back.2 = (bf16[4,192,256]{2,1,0:T(8,128)(2,1)}, f32[4,2,192,256]{3,2,1,0:T(8,128)}, bf16[4,2,192,256]{3,2,1,0:T(8,128)(2,1)}) custom-call(s32[4,8]{1,0:T(4,128)} %and_convert_fusion.active, s32[4,1,256]{2,1,0:T(1,128)} %broadcast_in_dim.37.seg_row, s32[8,256,1]{2,1,0:T(8,128)} %select_convert_fusion.seg_col, ...), custom_call_target="tpu_custom_call" | custom-call | flops 2013265920 | bytes 7864320 | tf_op jit(solution)/shard_map/attend_back/pallas_call | solution.py:284
  313.6 12.7 %collective-permute-done.33.rest_1_ = bf16[3,192,256]{2,1,0:T(8,128)(2,1)S(1)} collective-permute-done((bf16[3,192,256]{2,1,0:T(8,128)(2,1)S(1)}, bf16[3,192,256]{2,1,0:T(8,128)(2,1)S(1)}, u32[]{:S(2)}, u32[]{:S(2)}) %collective-permute-start.33) | collective-permute-done | bytes 294944 | tf_op jit(solution)/shard_map/ppermute | solution.py:38
  326.9 11.6 %collective-permute-done.35.rest_3_ = bf16[3,192,256]{2,1,0:T(8,128)(2,1)S(1)} collective-permute-done((bf16[3,192,256]{2,1,0:T(8,128)(2,1)S(1)}, bf16[3,192,256]{2,1,0:T(8,128)(2,1)S(1)}, u32[]{:S(2)}, u32[]{:S(2)}) %collective-permute-start.35) | collective-permute-done | bytes 294944 | tf_op jit(solution)/shard_map/ppermute | solution.py:38
  346.8 17.3 %feed_back.3 = (bf16[8,864,768]{2,1,0:T(8,128)(2,1)}, f32[256,768]{1,0:T(8,128)}, f32[16,768]{1,0:T(8,128)}, bf16[192,256]{1,0:T(8,128)(2,1)}, bf16[192,256]{1,0...) custom-call(s32[4]{0:T(128)} %iota_xor_fusion.order, f32[256,768]{1,0:T(8,128)} %get-tuple-element.221.grad_ref, ...), custom_call_target="tpu_custom_call" | custom-call | flops 6643777536 | bytes 21233664 | tf_op jit(solution)/shard_map/feed_back/pallas_call | solution.py:484
  378.0 10.0 %collective-permute-done.37.rest_9_ = bf16[192,256]{1,0:T(8,128)(2,1)} collective-permute-done((bf16[192,256]{1,0:T(8,128)(2,1)}, bf16[192,256]{1,0:T(8,128)(2,1)}, u32[]{:S(2)}, u32[]{:S(2)}) %collective-permute-start.37) | collective-permute-done | bytes 98336 | tf_op jit(solution)/shard_map/ppermute | solution.py:38
  392.3 20.2 %attend_back.3 = (bf16[4,192,256]{2,1,0:T(8,128)(2,1)}, f32[4,2,192,256]{3,2,1,0:T(8,128)}, bf16[4,2,192,256]{3,2,1,0:T(8,128)(2,1)}) custom-call(s32[4,8]{1,0:T(4,128)} %and_convert_fusion.active, s32[4,1,256]{2,1,0:T(1,128)} %broadcast_in_dim.37.seg_row, s32[8,256,1]{2,1,0:T(8,128)} %select_convert_fusion.seg_col, ...), custom_call_target="tpu_custom_call" | custom-call | flops 2013265920 | bytes 7864320 | tf_op jit(solution)/shard_map/attend_back/pallas_call | solution.py:284
  417.0 9.8 %collective-permute-done.44 = bf16[160,768]{1,0:T(8,128)(2,1)S(1)} collective-permute-done((bf16[160,768]{1,0:T(8,128)(2,1)S(1)}, bf16[160,768]{1,0:T(8,128)(2,1)S(1)}, u32[]{:S(2)}, u32[]{:S(2)}) %collective-permute-start.44) | collective-permute-done | bytes 245792 | tf_op jit(solution)/shard_map/ppermute | solution.py:38
  462.7 11.7 %collective-permute-done.51 = bf16[80,768]{1,0:T(8,128)(2,1)S(1)} collective-permute-done((bf16[80,768]{1,0:T(8,128)(2,1)S(1)}, bf16[80,768]{1,0:T(8,128)(2,1)S(1)}, u32[]{:S(2)}, u32[]{:S(2)}) %collective-permute-start.51) | collective-permute-done | bytes 122912 | tf_op jit(solution)/shard_map/ppermute | solution.py:38
  481.8 11.3 %collective-permute-done.53 = bf16[80,768]{1,0:T(8,128)(2,1)S(1)} collective-permute-done((bf16[80,768]{1,0:T(8,128)(2,1)}, bf16[80,768]{1,0:T(8,128)(2,1)S(1)}, u32[]{:S(2)}, u32[]{:S(2)}) %collective-permute-start.53) | collective-permute-done | bytes 122912 | tf_op jit(solution)/shard_map/ppermute | solution.py:38
  501.7 12.3 %collective-permute-done.56 = bf16[160,768]{1,0:T(8,128)(2,1)S(1)} collective-permute-done((bf16[160,768]{1,0:T(8,128)(2,1)S(1)}, bf16[160,768]{1,0:T(8,128)(2,1)S(1)}, u32[]{:S(2)}, u32[]{:S(2)}) %collective-permute-start.56) | collective-permute-done | bytes 245792 | tf_op jit(solution)/shard_map/ppermute | solution.py:38
  541.1 18.6 %collective-permute-done.64 = bf16[80,768]{1,0:T(8,128)(2,1)S(1)} collective-permute-done((bf16[80,768]{1,0:T(8,128)(2,1)S(1)}, bf16[80,768]{1,0:T(8,128)(2,1)S(1)}, u32[]{:S(2)}, u32[]{:S(2)}) %collective-permute-start.64) | collective-permute-done | bytes 122912 | tf_op jit(solution)/shard_map/ppermute | solution.py:38
  562.7 14.4 %collective-permute-done.66 = bf16[80,768]{1,0:T(8,128)(2,1)S(1)} collective-permute-done((bf16[80,768]{1,0:T(8,128)(2,1)S(1)}, bf16[80,768]{1,0:T(8,128)(2,1)S(1)}, u32[]{:S(2)}, u32[]{:S(2)}) %collective-permute-start.66) | collective-permute-done | bytes 122912 | tf_op jit(solution)/shard_map/ppermute | solution.py:38
  (346 shorter events, 243.0 us)
Async XLA Ops:
  7.2 62.2 %all-gather.6.cloned.1.call-start = ((), (), s32[]{:S(2)}) async-start(), calls=%async_computation.3 | async-start | bytes 4202496 | tf_op jit(solution)/shard_map/all_gather | solution.py:751
  25.8 137.4 %all-gather.4.cloned.1.call-start = ((), (), s32[]{:S(2)}) async-start(), calls=%async_computation.2 | async-start | bytes 15925248 | tf_op jit(solution)/shard_map/all_gather | solution.py:751
  28.3 37.5 %collective-permute-start.4 = (bf16[24,9216]{1,0:T(8,128)(2,1)S(1)}, bf16[24,9216]{1,0:T(8,128)(2,1)S(1)}, u32[]{:S(2)}, u32[]{:S(2)}) collective-permute-start(bf16[24,9216]{1,0:T(8,128)(2,1)S(1)} %bitcast_dynamic-update-slice_fusion.2), channel_id=1, source_target_pairs={{0,16},{8,24},{16,0},{24,8},{1,17},{9,25},{17,1},{25,9},{2,18},{10... | collective-permute-start | bytes 1327112 | tf_op jit(solution)/shard_map/ppermute | solution.py:38
  29.2 36.6 %collective-permute-start.5 = (bf16[24,9216]{1,0:T(8,128)(2,1)S(1)}, bf16[24,9216]{1,0:T(8,128)(2,1)S(1)}, u32[]{:S(2)}, u32[]{:S(2)}) collective-permute-start(bf16[24,9216]{1,0:T(8,128)(2,1)S(1)} %bitcast_dynamic-update-slice_fusion.2), channel_id=1, source_target_pairs={{0,8},{8,0},{16,24},{24,16},{1,9},{9,1},{17,25},{25,17},{2,10},{10... | collective-permute-start | bytes 1327112 | tf_op jit(solution)/shard_map/ppermute | solution.py:38
  67.5 178.8 %all-gather.8.cloned.1.call-start = ((), (), s32[]{:S(2)}) async-start(), calls=%async_computation.4 | async-start | bytes 11943936 | tf_op jit(solution)/shard_map/all_gather | solution.py:751
  79.4 26.4 %collective-permute-start.8 = (bf16[3,192,256]{2,1,0:T(8,128)(2,1)}, bf16[3,192,256]{2,1,0:T(8,128)(2,1)S(1)}, u32[]{:S(2)}, u32[]{:S(2)}) collective-permute-start(bf16[3,192,256]{2,1,0:T(8,128)(2,1)} %get-tuple-element.160), channel_id=1, source_target_pairs={{0,6},{1,7},{2,4},{3,5},{4,2},{5,3},{6,0},{7,1},{8,14},{9,15},{10,... | collective-permute-start | bytes 884744 | tf_op jit(solution)/shard_map/ppermute | solution.py:38
  79.9 27.6 %collective-permute-start.9 = (bf16[3,192,256]{2,1,0:T(8,128)(2,1)}, bf16[3,192,256]{2,1,0:T(8,128)(2,1)S(1)}, u32[]{:S(2)}, u32[]{:S(2)}) collective-permute-start(bf16[3,192,256]{2,1,0:T(8,128)(2,1)} %get-tuple-element.161.rest_0_), channel_id=1, source_target_pairs={{0,1},{1,0},{2,3},{3,2},{4,5},{5,4},{6,7},{7,6},{8,9},{9,8},{10,11... | collective-permute-start | bytes 884744 | tf_op jit(solution)/shard_map/ppermute | solution.py:38
  107.6 38.7 %collective-permute-start.16 = (bf16[24,6912]{1,0:T(8,128)(2,1)S(1)}, bf16[24,6912]{1,0:T(8,128)(2,1)S(1)}, u32[]{:S(2)}, u32[]{:S(2)}) collective-permute-start(bf16[24,6912]{1,0:T(8,128)(2,1)S(1)} %get-tuple-element.173), channel_id=1, source_target_pairs={{0,8},{8,0},{16,24},{24,16},{1,9},{9,1},{17,25},{25,17},{2,10},{10... | collective-permute-start | bytes 995336 | tf_op jit(solution)/shard_map/ppermute | solution.py:38
  107.7 38.6 %collective-permute-start.17 = (bf16[24,6912]{1,0:T(8,128)(2,1)S(1)}, bf16[24,6912]{1,0:T(8,128)(2,1)S(1)}, u32[]{:S(2)}, u32[]{:S(2)}) collective-permute-start(bf16[24,6912]{1,0:T(8,128)(2,1)S(1)} %get-tuple-element.173), channel_id=1, source_target_pairs={{0,16},{8,24},{16,0},{24,8},{1,17},{9,25},{17,1},{25,9},{2,18},{10... | collective-permute-start | bytes 995336 | tf_op jit(solution)/shard_map/ppermute | solution.py:38
  110.2 36.1 %collective-permute-start.18 = (bf16[24,6912]{1,0:T(8,128)(2,1)S(1)}, bf16[24,6912]{1,0:T(8,128)(2,1)S(1)}, u32[]{:S(2)}, u32[]{:S(2)}) collective-permute-start(bf16[24,6912]{1,0:T(8,128)(2,1)S(1)} %get-tuple-element.173), channel_id=1, source_target_pairs={{0,24},{8,16},{16,8},{24,0},{1,25},{9,17},{17,9},{25,1},{2,26},{10... | collective-permute-start | bytes 995336 | tf_op jit(solution)/shard_map/ppermute | solution.py:38
  147.7 244.5 %reduce-scatter.3.cloned.1.call-start = ((), (), s32[]{:S(2)}) async-start(), calls=%async_computation.5 | async-start | bytes 11943936 | tf_op jit(solution)/shard_map/reduce_scatter | solution.py:869
  180.6 23.7 %collective-permute-start.21 = (bf16[3,192,256]{2,1,0:T(8,128)(2,1)}, bf16[3,192,256]{2,1,0:T(8,128)(2,1)S(1)}, u32[]{:S(2)}, u32[]{:S(2)}) collective-permute-start(bf16[3,192,256]{2,1,0:T(8,128)(2,1)} %get-tuple-element.185), channel_id=1, source_target_pairs={{0,6},{1,7},{2,4},{3,5},{4,2},{5,3},{6,0},{7,1},{8,14},{9,15},{10,... | collective-permute-start | bytes 884744 | tf_op jit(solution)/shard_map/ppermute | solution.py:38
  181.8 22.5 %collective-permute-start.22 = (bf16[3,192,256]{2,1,0:T(8,128)(2,1)}, bf16[3,192,256]{2,1,0:T(8,128)(2,1)S(1)}, u32[]{:S(2)}, u32[]{:S(2)}) collective-permute-start(bf16[3,192,256]{2,1,0:T(8,128)(2,1)} %get-tuple-element.182.rest_0_), channel_id=1, source_target_pairs={{0,1},{1,0},{2,3},{3,2},{4,5},{5,4},{6,7},{7,6},{8,9},{9,8},{10,11... | collective-permute-start | bytes 884744 | tf_op jit(solution)/shard_map/ppermute | solution.py:38
  273.6 206.8 %reduce-scatter.5.cloned.1.call-start = ((), (), s32[]{:S(2)}) async-start(), calls=%async_computation.6 | async-start | bytes 11943936 | tf_op jit(solution)/shard_map/reduce_scatter | solution.py:869
  311.8 26.8 %collective-permute-start.35 = (bf16[3,192,256]{2,1,0:T(8,128)(2,1)S(1)}, bf16[3,192,256]{2,1,0:T(8,128)(2,1)S(1)}, u32[]{:S(2)}, u32[]{:S(2)}) collective-permute-start(bf16[3,192,256]{2,1,0:T(8,128)(2,1)S(1)} %get-tuple-element.216), channel_id=1, source_target_pairs={{0,6},{1,7},{2,4},{3,5},{4,2},{5,3},{6,0},{7,1},{8,14},{9,15},{10,... | collective-permute-start | bytes 884744 | tf_op jit(solution)/shard_map/ppermute | solution.py:38
  371.7 19.7 %collective-permute-start.40 = (bf16[2,160,768]{2,1,0:T(8,128)(2,1)S(1)}, bf16[2,160,768]{2,1,0:T(8,128)(2,1)S(1)}, u32[]{:S(2)}, u32[]{:S(2)}) collective-permute-start(bf16[2,160,768]{2,1,0:T(8,128)(2,1)S(1)} %slice_bitcast_fusion.5), channel_id=1, source_target_pairs={{0,2},{1,3},{2,0},{3,1},{4,6},{5,7},{6,4},{7,5},{8,10},{9,11},{10,... | collective-permute-start | bytes 1474568 | tf_op jit(solution)/shard_map/ppermute | solution.py:38
  391.6 25.4 %collective-permute-start.43 = (bf16[160,768]{1,0:T(8,128)(2,1)S(1)}, bf16[160,768]{1,0:T(8,128)(2,1)S(1)}, u32[]{:S(2)}, u32[]{:S(2)}) collective-permute-start(bf16[160,768]{1,0:T(8,128)(2,1)S(1)} %slice_bitcast_fusion.13), channel_id=1, source_target_pairs={{0,4},{1,5},{2,6},{3,7},{4,0},{5,1},{6,2},{7,3},{8,12},{9,13},{10,... | collective-permute-start | bytes 737288 | tf_op jit(solution)/shard_map/ppermute | solution.py:38
  451.9 22.5 %collective-permute-start.52 = (bf16[216,768]{1,0:T(8,128)(2,1)S(1)}, bf16[216,768]{1,0:T(8,128)(2,1)S(1)}, u32[]{:S(2)}, u32[]{:S(2)}) collective-permute-start(bf16[216,768]{1,0:T(8,128)(2,1)S(1)} %fusion.5), channel_id=1, source_target_pairs={{0,16},{8,24},{16,0},{24,8},{1,17},{9,25},{17,1},{25,9},{2,18},{10... | collective-permute-start | bytes 995336 | tf_op jit(solution)/shard_map/ppermute | solution.py:38
  453.3 21.1 %collective-permute-start.51 = (bf16[80,768]{1,0:T(8,128)(2,1)S(1)}, bf16[80,768]{1,0:T(8,128)(2,1)S(1)}, u32[]{:S(2)}, u32[]{:S(2)}) collective-permute-start(bf16[80,768]{1,0:T(8,128)(2,1)S(1)} %dynamic-slice_bitcast_fusion.7), channel_id=1, source_target_pairs={{0,16},{8,24},{16,0},{24,8},{1,17},{9,25},{17,1},{25,9},{2,18},{10... | collective-permute-start | bytes 368648 | tf_op jit(solution)/shard_map/ppermute | solution.py:38
  474.3 21.3 %collective-permute-start.55 = (bf16[4,320,768]{2,1,0:T(8,128)(2,1)}, bf16[4,320,768]{2,1,0:T(8,128)(2,1)}, u32[]{:S(2)}, u32[]{:S(2)}) collective-permute-start(bf16[4,320,768]{2,1,0:T(8,128)(2,1)} %get-tuple-element.274), channel_id=1, source_target_pairs={{0,1},{1,0},{2,3},{3,2},{4,5},{5,4},{6,7},{7,6},{8,9},{9,8},{10,11... | collective-permute-start | bytes 5898248 | tf_op jit(solution)/shard_map/ppermute | solution.py:38
  475.0 20.6 %collective-permute-start.54 = (bf16[432,768]{1,0:T(8,128)(2,1)S(1)}, bf16[432,768]{1,0:T(8,128)(2,1)}, u32[]{:S(2)}, u32[]{:S(2)}) collective-permute-start(bf16[432,768]{1,0:T(8,128)(2,1)S(1)} %pad_maximum_fusion.2), channel_id=1, source_target_pairs={{0,8},{8,0},{16,24},{24,16},{1,9},{9,1},{17,25},{25,17},{2,10},{10... | collective-permute-start | bytes 1990664 | tf_op jit(solution)/shard_map/ppermute | solution.py:38
  481.6 34.3 %collective-permute-start.61 = (bf16[432,768]{1,0:T(8,128)(2,1)S(1)}, bf16[432,768]{1,0:T(8,128)(2,1)S(1)}, u32[]{:S(2)}, u32[]{:S(2)}) collective-permute-start(bf16[432,768]{1,0:T(8,128)(2,1)S(1)} %dynamic-slice_bitcast_fusion), channel_id=1, source_target_pairs={{0,8},{8,0},{16,24},{24,16},{1,9},{9,1},{17,25},{25,17},{2,10},{10... | collective-permute-start | bytes 1990664 | tf_op jit(solution)/shard_map/ppermute | solution.py:38
  537.9 21.8 %collective-permute-start.65 = (bf16[216,768]{1,0:T(8,128)(2,1)S(1)}, bf16[216,768]{1,0:T(8,128)(2,1)S(1)}, u32[]{:S(2)}, u32[]{:S(2)}) collective-permute-start(bf16[216,768]{1,0:T(8,128)(2,1)S(1)} %fusion.4), channel_id=1, source_target_pairs={{0,16},{8,24},{16,0},{24,8},{1,17},{9,25},{17,1},{25,9},{2,18},{10... | collective-permute-start | bytes 995336 | tf_op jit(solution)/shard_map/ppermute | solution.py:38
  538.0 21.7 %collective-permute-start.64 = (bf16[80,768]{1,0:T(8,128)(2,1)S(1)}, bf16[80,768]{1,0:T(8,128)(2,1)S(1)}, u32[]{:S(2)}, u32[]{:S(2)}) collective-permute-start(bf16[80,768]{1,0:T(8,128)(2,1)S(1)} %dynamic-slice_bitcast_fusion.6), channel_id=1, source_target_pairs={{0,16},{8,24},{16,0},{24,8},{1,17},{9,25},{17,1},{25,9},{2,18},{10... | collective-permute-start | bytes 368648 | tf_op jit(solution)/shard_map/ppermute | solution.py:38
  (91 other events, 876.8 us)
Sparse Core Ops, SparseCore 0:
  25.9 35.1 all-gather.5
  67.6 95.5 all-gather.3
  165.7 80.5 all-gather.7
  273.7 95.2 reduce-scatter.2
  372.4 92.4 reduce-scatter.4

commit v4 on v3

--- a/solution.py
+++ b/solution.py
@@ -648,22 +648,38 @@
     return (yield from dp_steps(total, dp_size, dp_me))
 
 
+def dp_direct_steps(total, dp_size, dp_me):
+    rows, width = total.shape
+    if dp_size != 4:
+        return lax.psum(total, "dp")
+    pieces = total.reshape(dp_size, rows // dp_size, width)
+
+    def piece(m):
+        return lax.dynamic_index_in_dim(pieces, dp_me ^ m, 0, keepdims=False)
+
+    own, *leave = yield [piece(m) for m in range(dp_size)]
+    arrived = yield [exchange(leave[m - 1], "dp", dp_size, m) for m in range(1, dp_size)]
+    mine = sum((item.astype(F32) for item in arrived), own.astype(F32)).astype(BF16)
+    arrived = yield [exchange(mine, "dp", dp_size, m) for m in range(1, dp_size)]
+    return jnp.concatenate(in_order([mine] + list(arrived), dp_me), axis=0)
+
+
 def dp_steps(total, dp_size, dp_me):
     rows, width = total.shape
     if dp_size != 4:
         return lax.psum(total, "dp")
-    bits = [(dp_me >> b) & 1 for b in range(2)]
-    for b in range(2):
-        halves = total.reshape(2, -1, width)
-        leave = lax.dynamic_index_in_dim(halves, 1 - bits[b], 0, keepdims=False)
-        (arrived,) = yield [exchange(leave, "dp", dp_size, 1 << b)]
-        total = add_low(lax.dynamic_index_in_dim(halves, bits[b], 0, keepdims=False), arrived)
-    for b in (1, 0):
-        (arrived,) = yield [exchange(total, "dp", dp_size, 1 << b)]
-        flip = bits[b] != 0
-        pair = [jnp.where(flip, arrived, total), jnp.where(flip, total, arrived)]
-        total = jnp.concatenate(pair, axis=0)
-    return total
+    pieces = total.reshape(dp_size, rows // dp_size, width)
+
+    def piece(m):
+        return lax.dynamic_index_in_dim(pieces, dp_me ^ m, 0, keepdims=False)
+
+    (passing,) = yield [exchange(piece(3), "dp", dp_size, 1)]
+    across = add_low(piece(2), passing)
+    arrived = yield [exchange(piece(1), "dp", dp_size, 1), exchange(across, "dp", dp_size, 2)]
+    mine = sum((item.astype(F32) for item in arrived), piece(0).astype(F32)).astype(BF16)
+    near, far = yield [exchange(mine, "dp", dp_size, 1), exchange(mine, "dp", dp_size, 2)]
+    (last,) = yield [exchange(far, "dp", dp_size, 1)]
+    return jnp.concatenate(in_order([mine, near, far, last], dp_me), axis=0)
 
 
 def in_order(stack, place):
@@ -743,8 +759,10 @@
     def gathered(shard):
         return lax.all_gather(shard, both, axis=0, tiled=True)
 
-    def over_dp(shard):
-        return [exchange(shard, "dp", dp_size, m) for m in range(1, dp_size)]
+    def over_dp(shard, relay=True):
+        near, far = (exchange(shard, "dp", dp_size, m) for m in (1, 2))
+        last = exchange(far, "dp", dp_size, 1) if relay else exchange(shard, "dp", dp_size, 3)
+        return [near, far, last]
 
     def over_seq(shard, arrived):
         stack = jnp.stack(in_order([shard] + list(arrived), dp_me))
@@ -779,7 +797,7 @@
             if layer + 1 < LAYERS:
                 parts.append(project_weight[layer + 1])
             shards.append(jnp.concatenate(parts, axis=1))
-        arrived, shards[0] = lax.optimization_barrier((over_dp(starting), shards[0]))
+        arrived = over_dp(starting, relay=False)
         ahead = over_dp(shards[0])
         whole = over_seq(starting, arrived)
         table = whole[:, 3 * width :].reshape(everyone, depth, 128)
@@ -870,35 +888,37 @@
             terms.reshape(-1, width), "seq", scatter_dimension=0, tiled=True
         )
         grad_mixed = tick(behind, tuple(grad_mixed))
+        if layer + 1 < LAYERS:
+            grad_mixed, later = lax.optimization_barrier((grad_mixed, shares[layer + 1]))
+            feeds[layer + 1] = Stream(dp_direct_steps(later, dp_size, dp_me))
+            grad_mixed = tick([feeds[layer + 1]], grad_mixed)
+            behind = behind + [feeds[layer + 1]]
         grads = tuple(swap_groups(grad_mixed))
-        grads = tick(behind, grads)
         if layer + 1 < LAYERS:
-            grads, later = lax.optimization_barrier((grads, shares[layer + 1]))
-            feeds[layer + 1] = Stream(dp_steps(later, dp_size, dp_me))
-            behind = behind + [feeds[layer + 1]]
-        grad_query, kept_kv, *sent_kv = attend_back(
+            grads = tick([backs[layer + 1]], grads)
+        made = attend_back(
             active, seg_row, seg_col, parts, grads, exact, log_total, groups, members
         )
+        grad_query, kept_kv, *sent_kv = tick(behind, tuple(made))
         for j in range(1, members):
             kept_kv = kept_kv + exchange(sent_kv[j - 1], "seq", seq_size, j).astype(F32)
         messages = tuple(
             jnp.concatenate([grad_query[r][None], kept_kv[r].astype(BF16)], axis=0)
             for r in range(groups)
         )
-        messages = tick(behind, messages)
         pieces = tuple(swap_groups(messages))
-        pieces = tick(behind, pieces)
-        own, send, grad = project_back(
+        made = project_back(
             order, place, entered, grad_first, w_project[layer], small, pieces, seq_size
         )
-        if layer + 1 < LAYERS:
-            own, send = tick(behind, (own, send))
+        own, send, grad = tick(behind, tuple(made))
         backs[layer] = Stream(sum_steps(own, send, seq_size, dp_size, dp_me))
-        behind = behind + [backs[layer]]
-    tick(behind)
-    tick(behind)
-    feeds[0] = Stream(dp_steps(shares[0], dp_size, dp_me))
-    behind = behind + [feeds[0]]
+        behind = [backs[layer]]
+    last = tick(backs, shares[0])
+    feeds[0] = Stream(dp_steps(last, dp_size, dp_me))
+    behind = backs + feeds
+    for unused in range(2):
+        tick(behind)
+        tick(backs)
     while any(item.flying is not None for item in behind):
         tick(behind)
     small = jnp.stack(

time: 602 us -> 553 us (0.919)
  waiting for transfers between devices: 300 us -> 244 us
  starting transfers between devices: 70.9 us -> 86.6 us
    ppermute x69 -> x77, waiting for transfers between devices: 276 us -> 220 us  [exchange(): return lax.ppermute(value, axis, [(i, i ^ mask) for i in range(size)])]
    ppermute x69 -> x77, starting transfers between devices: 70.3 us -> 86 us  [exchange(): return lax.ppermute(value, axis, [(i, i ^ mask) for i in range(size)])]
    reduce_scatter x2, waiting for transfers between devices: 0.01 us -> 7.65 us  [per_device(): lax.psum_scatter(terms.reshape(-1, width), 'seq', scatter_dimension=0, ti...]
    all_gather x3, waiting for transfers between devices: 23.9 us -> 16.7 us  [over_seq(): return lax.all_gather(stack, 'seq', axis=1, tiled=True).reshape(width, -1)]
  transfers between devices with their start and end apart: 74 -> 82, of which waited for: 43 -> 41; matrix products, arithmetic and copies ran while one was open for 7% -> 6% of each run, Pallas kernels for 22% -> 23%
where the time goes in v4:
time: 553 us; the launch traced here: 551 us
  waiting for transfers between devices  244 us (44%)
  Pallas kernels  157 us (28%)
  starting transfers between devices  86.6 us (16%)
  other arithmetic  30.6 us (6%)
  local copies, waits for them, and re-layouts  18.3 us (3%)
  between operations  14.8 us (3%)
    ppermute x77, waiting for transfers between devices, exchange(): return lax.ppermute(value, axis, [(i, i ^ mask) for i in range(size)])  220 us
    ppermute x77, starting transfers between devices, exchange(): return lax.ppermute(value, axis, [(i, i ^ mask) for i in range(size)])  86 us
    pallas_call x2, Pallas kernels, attend_back(): pl.pallas_call(functools.partial(attend_back_body, groups, members, heads...  41.7 us
    pallas_call x2, Pallas kernels, feed_back(): pl.pallas_call(functools.partial(feed_back_body, groups, span, blocks, de...  34.4 us
    pallas_call x2, Pallas kernels, attend(): pl.pallas_call(functools.partial(attend_body, groups, members, heads), ou...  34.1 us
    pallas_call x2, Pallas kernels, feed(): pl.pallas_call(functools.partial(feed_body, groups, span, blocks, pieces,...  20 us
    all_gather x3, waiting for transfers between devices, over_seq(): return lax.all_gather(stack, 'seq', axis=1, tiled=True).reshape(width, -1)  16.7 us
    pallas_call x2, Pallas kernels, project_back(): pl.pallas_call(functools.partial(project_back_body, groups, span, devices...  14.9 us
  transfers between devices with their start and end apart: 82, of which 41 were waited for; matrix products, arithmetic and copies ran while one was open for 6% of the time, Pallas kernels for 23%

profile of v4, /device:TPU:0, one launch (start us, length us, event | category | flops | bytes accessed | tf_op | source)
XLA Modules:
  0.0 551.1 jit_solution(7419726300174370037)
XLA Ops:
  29.2 18.3 %collective-permute-done = bf16[24,9216]{1,0:T(8,128)(2,1)S(1)} collective-permute-done((bf16[24,9216]{1,0:T(8,128)(2,1)S(1)}, bf16[24,9216]{1,0:T(8,128)(2,1)S(1)}, u32[]{:S(2)}, u32[]{:S(2)}) %collective-permute-start) | collective-permute-done | bytes 442400 | tf_op jit(solution)/shard_map/ppermute | solution.py:38
  47.8 11.9 %collective-permute-done.1 = bf16[24,9216]{1,0:T(8,128)(2,1)S(1)} collective-permute-done((bf16[24,9216]{1,0:T(8,128)(2,1)S(1)}, bf16[24,9216]{1,0:T(8,128)(2,1)S(1)}, u32[]{:S(2)}, u32[]{:S(2)}) %collective-permute-start.1) | collective-permute-done | bytes 442400 | tf_op jit(solution)/shard_map/ppermute | solution.py:38
  74.1 11.2 %collective-permute-done.6.rest_1_ = bf16[3,192,256]{2,1,0:T(8,128)(2,1)S(1)} collective-permute-done((bf16[3,192,256]{2,1,0:T(8,128)(2,1)}, bf16[3,192,256]{2,1,0:T(8,128)(2,1)S(1)}, u32[]{:S(2)}, u32[]{:S(2)}) %collective-permute-start.6) | collective-permute-done | bytes 294944 | tf_op jit(solution)/shard_map/ppermute | solution.py:38
  89.4 7.8 %collective-permute-done.8.rest_3_ = bf16[3,192,256]{2,1,0:T(8,128)(2,1)S(1)} collective-permute-done((bf16[3,192,256]{2,1,0:T(8,128)(2,1)}, bf16[3,192,256]{2,1,0:T(8,128)(2,1)S(1)}, u32[]{:S(2)}, u32[]{:S(2)}) %collective-permute-start.8) | collective-permute-done | bytes 294944 | tf_op jit(solution)/shard_map/ppermute | solution.py:38
  100.8 14.8 %collective-permute-done.17 = bf16[24,6912]{1,0:T(8,128)(2,1)S(1)} collective-permute-done((bf16[24,6912]{1,0:T(8,128)(2,1)S(1)}, bf16[24,6912]{1,0:T(8,128)(2,1)S(1)}, u32[]{:S(2)}, u32[]{:S(2)}) %collective-permute-start.17) | collective-permute-done | bytes 331808 | tf_op jit(solution)/shard_map/ppermute | solution.py:38
  116.3 17.1 %attend.2 = (bf16[192,256]{1,0:T(8,128)(2,1)}, bf16[192,256]{1,0:T(8,128)(2,1)}, bf16[192,256]{1,0:T(8,128)(2,1)}, bf16[192,256]{1,0:T(8,128)(2,1)}, f32[4,192,256]{2,1,0:T(8,128)}, /*index=5*/f32[4,3,1,256]{3,2,1,0:T(1,128)}) custom-call(s32[4,8]{1,0:T(4,128)} %and_convert_fusion.active, s32[4,1,256]{2,1,0:T(1,128)} %broadcast_in_dim.37.seg_row, ...), custom_call_target="tpu_custom_call" | custom-call | flops 805306368 | bytes 3932160 | tf_op jit(solution)/shard_map/attend/pallas_call | solution.py:198
  155.4 10.0 %feed.2 = (f32[256,768]{1,0:T(8,128)}, bf16[256,768]{1,0:T(8,128)(2,1)}, f32[256,768]{1,0:T(8,128)}, f32[256,768]{1,0:T(8,128)}) custom-call(s32[4]{0:T(128)} %iota_xor_fusion.order, f32[256,768]{1,0:T(8,128)} %bitcast_convert_fusion.1.x_ref, bf16[768,9216]{1,0:T(8,128)(2,1)} %bitcast.254, bf16[768,9216]{1,0:T(8,128)(2,1)} %bitcast.255, ...), custom_call_target="tpu_custom_call" | custom-call | flops 2717908992 | bytes 10616832 | tf_op jit(solution)/shard_map/feed/pallas_call | solution.py:373
  174.0 12.9 %collective-permute-done.19.rest_1_ = bf16[3,192,256]{2,1,0:T(8,128)(2,1)S(1)} collective-permute-done((bf16[3,192,256]{2,1,0:T(8,128)(2,1)}, bf16[3,192,256]{2,1,0:T(8,128)(2,1)S(1)}, u32[]{:S(2)}, u32[]{:S(2)}) %collective-permute-start.19) | collective-permute-done | bytes 294944 | tf_op jit(solution)/shard_map/ppermute | solution.py:38
  198.8 17.0 %attend.3 = (bf16[192,256]{1,0:T(8,128)(2,1)}, bf16[192,256]{1,0:T(8,128)(2,1)}, bf16[192,256]{1,0:T(8,128)(2,1)}, bf16[192,256]{1,0:T(8,128)(2,1)}, f32[4,192,256]{2,1,0:T(8,128)}, /*index=5*/f32[4,3,1,256]{3,2,1,0:T(1,128)}) custom-call(s32[4,8]{1,0:T(4,128)} %and_convert_fusion.active, s32[4,1,256]{2,1,0:T(1,128)} %broadcast_in_dim.37.seg_row, ...), custom_call_target="tpu_custom_call" | custom-call | flops 805306368 | bytes 3932160 | tf_op jit(solution)/shard_map/attend/pallas_call | solution.py:198
  227.9 10.6 %all-gather.8.cloned.1.call-done = bf16[4,192,6912]{2,1,0:T(8,128)(2,1)} async-done(((bf16[4,24,6912]{2,1,0:T(8,128)(2,1)}), bf16[4,192,6912]{2,1,0:T(8,128)(2,1)}) %all-gather.8.cloned.1.call-update) | async-done | bytes 10616848 | tf_op jit(solution)/shard_map/all_gather | solution.py:769
  238.5 10.0 %feed.3 = (f32[256,768]{1,0:T(8,128)}, bf16[256,768]{1,0:T(8,128)(2,1)}, f32[256,768]{1,0:T(8,128)}, f32[256,768]{1,0:T(8,128)}) custom-call(s32[4]{0:T(128)} %iota_xor_fusion.order, f32[256,768]{1,0:T(8,128)} %get-tuple-element.172.x_ref, bf16[768,6912]{1,0:T(8,128)(2,1)} %bitcast.262, bf16[768,6912]{1,0:T(8,128)(2,1)} %bitcast.263, ...), custom_call_target="tpu_custom_call" | custom-call | flops 2717908992 | bytes 10616832 | tf_op jit(solution)/shard_map/feed/pallas_call | solution.py:373
  248.5 17.2 %feed_back.2 = (bf16[8,864,768]{2,1,0:T(8,128)(2,1)}, f32[256,768]{1,0:T(8,128)}, f32[16,768]{1,0:T(8,128)}, bf16[192,256]{1,0:T(8,128)(2,1)}, bf16[192,256]{1,0...) custom-call(s32[4]{0:T(128)} %iota_xor_fusion.order, f32[256,768]{1,0:T(8,128)} %bitcast_convert_fusion.grad_ref, ...), custom_call_target="tpu_custom_call" | custom-call | flops 6643777536 | bytes 21233664 | tf_op jit(solution)/shard_map/feed_back/pallas_call | solution.py:484
  275.6 21.4 %attend_back.2 = (bf16[4,192,256]{2,1,0:T(8,128)(2,1)}, f32[4,2,192,256]{3,2,1,0:T(8,128)}, bf16[4,2,192,256]{3,2,1,0:T(8,128)(2,1)}) custom-call(s32[4,8]{1,0:T(4,128)} %and_convert_fusion.active, s32[4,1,256]{2,1,0:T(1,128)} %broadcast_in_dim.37.seg_row, s32[8,256,1]{2,1,0:T(8,128)} %select_convert_fusion.seg_col, ...), custom_call_target="tpu_custom_call" | custom-call | flops 2013265920 | bytes 7864320 | tf_op jit(solution)/shard_map/attend_back/pallas_call | solution.py:284
  305.9 11.8 %collective-permute-done.33.rest_1_ = bf16[3,192,256]{2,1,0:T(8,128)(2,1)S(1)} collective-permute-done((bf16[3,192,256]{2,1,0:T(8,128)(2,1)S(1)}, bf16[3,192,256]{2,1,0:T(8,128)(2,1)S(1)}, u32[]{:S(2)}, u32[]{:S(2)}) %collective-permute-start.33) | collective-permute-done | bytes 294944 | tf_op jit(solution)/shard_map/ppermute | solution.py:38
  318.5 11.4 %collective-permute-done.35.rest_3_ = bf16[3,192,256]{2,1,0:T(8,128)(2,1)S(1)} collective-permute-done((bf16[3,192,256]{2,1,0:T(8,128)(2,1)S(1)}, bf16[3,192,256]{2,1,0:T(8,128)(2,1)S(1)}, u32[]{:S(2)}, u32[]{:S(2)}) %collective-permute-start.35) | collective-permute-done | bytes 294944 | tf_op jit(solution)/shard_map/ppermute | solution.py:38
  330.7 7.6 %project_back.2 = (bf16[4,320,768]{2,1,0:T(8,128)(2,1)}, bf16[4,320,768]{2,1,0:T(8,128)(2,1)}, f32[256,768]{1,0:T(8,128)}) custom-call(s32[4]{0:T(128)} %iota_xor_fusion.order, s32[1]{0:T(128)} %bitcast.43.place, f32[256,768]{1,0:T(8,128)} %get-tuple-element.172.x_ref, f32[256,768]{1,0:T(8,128)} %get-tuple-element.188.grad_ref, bf16[768,9216]{1,0:T(8,128)(2,1)} %bitcast.258, ...), custom_call_target="tpu_custom_call" | custom-call | flops 1811939328 | bytes 7077888 | tf_op jit(solution)/shard_map/project_back/pallas_call | solution.py:572
  338.2 17.2 %feed_back.3 = (bf16[8,864,768]{2,1,0:T(8,128)(2,1)}, f32[256,768]{1,0:T(8,128)}, f32[16,768]{1,0:T(8,128)}, bf16[192,256]{1,0:T(8,128)(2,1)}, bf16[192,256]{1,0...) custom-call(s32[4]{0:T(128)} %iota_xor_fusion.order, f32[256,768]{1,0:T(8,128)} %get-tuple-element.203.grad_ref, ...), custom_call_target="tpu_custom_call" | custom-call | flops 6643777536 | bytes 21233664 | tf_op jit(solution)/shard_map/feed_back/pallas_call | solution.py:484
  386.4 20.2 %attend_back.3 = (bf16[4,192,256]{2,1,0:T(8,128)(2,1)}, f32[4,2,192,256]{3,2,1,0:T(8,128)}, bf16[4,2,192,256]{3,2,1,0:T(8,128)(2,1)}) custom-call(s32[4,8]{1,0:T(4,128)} %and_convert_fusion.active, s32[4,1,256]{2,1,0:T(1,128)} %broadcast_in_dim.37.seg_row, s32[8,256,1]{2,1,0:T(8,128)} %select_convert_fusion.seg_col, ...), custom_call_target="tpu_custom_call" | custom-call | flops 2013265920 | bytes 7864320 | tf_op jit(solution)/shard_map/attend_back/pallas_call | solution.py:284
  417.7 11.1 %collective-permute-done.48.rest_1_ = bf16[3,192,256]{2,1,0:T(8,128)(2,1)S(1)} collective-permute-done((bf16[3,192,256]{2,1,0:T(8,128)(2,1)S(1)}, bf16[3,192,256]{2,1,0:T(8,128)(2,1)S(1)}, u32[]{:S(2)}, u32[]{:S(2)}) %collective-permute-start.48) | collective-permute-done | bytes 294944 | tf_op jit(solution)/shard_map/ppermute | solution.py:38
  436.6 7.4 %project_back.3 = (bf16[4,320,768]{2,1,0:T(8,128)(2,1)}, bf16[4,320,768]{2,1,0:T(8,128)(2,1)}, f32[256,768]{1,0:T(8,128)}) custom-call(s32[4]{0:T(128)} %iota_xor_fusion.order, s32[1]{0:T(128)} %bitcast.43.place, f32[256,768]{1,0:T(8,128)} %bitcast_convert_fusion.1.x_ref, f32[256,768]{1,0:T(8,128)} %get-tuple-element.207.grad_ref, ...), custom_call_target="tpu_custom_call" | custom-call | flops 1811939328 | bytes 7077888 | tf_op jit(solution)/shard_map/project_back/pallas_call | solution.py:572
  452.2 7.6 %reduce-scatter.5.cloned.1.call-done = bf16[864,768]{1,0:T(8,128)(2,1)} async-done(((bf16[6912,768]{1,0:T(8,128)(2,1)}), bf16[864,768]{1,0:T(8,128)(2,1)}) %reduce-scatter.5.cloned.1.call-update) | async-done | bytes 1327120 | tf_op jit(solution)/shard_map/reduce_scatter | solution.py:887
  469.9 8.5 %collective-permute-done.60 = bf16[80,768]{1,0:T(8,128)(2,1)S(1)} collective-permute-done((bf16[80,768]{1,0:T(8,128)(2,1)S(1)}, bf16[80,768]{1,0:T(8,128)(2,1)S(1)}, u32[]{:S(2)}, u32[]{:S(2)}) %collective-permute-start.60) | collective-permute-done | bytes 122912 | tf_op jit(solution)/shard_map/ppermute | solution.py:38
  485.5 12.9 %collective-permute-done.65 = bf16[80,768]{1,0:T(8,128)(2,1)S(1)} collective-permute-done((bf16[80,768]{1,0:T(8,128)(2,1)S(1)}, bf16[80,768]{1,0:T(8,128)(2,1)S(1)}, u32[]{:S(2)}, u32[]{:S(2)}) %collective-permute-start.65) | collective-permute-done | bytes 122912 | tf_op jit(solution)/shard_map/ppermute | solution.py:38
  517.4 7.4 %collective-permute-done.71 = bf16[80,768]{1,0:T(8,128)(2,1)S(1)} collective-permute-done((bf16[80,768]{1,0:T(8,128)(2,1)S(1)}, bf16[80,768]{1,0:T(8,128)(2,1)S(1)}, u32[]{:S(2)}, u32[]{:S(2)}) %collective-permute-start.71) | collective-permute-done | bytes 122912 | tf_op jit(solution)/shard_map/ppermute | solution.py:38
  (372 shorter events, 232.8 us)
Async XLA Ops:
  7.2 56.0 %all-gather.6.cloned.1.call-start = ((), (), s32[]{:S(2)}) async-start(), calls=%async_computation.3 | async-start | bytes 4202496 | tf_op jit(solution)/shard_map/all_gather | solution.py:769
  25.9 129.5 %all-gather.4.cloned.1.call-start = ((), (), s32[]{:S(2)}) async-start(), calls=%async_computation.2 | async-start | bytes 15925248 | tf_op jit(solution)/shard_map/all_gather | solution.py:769
  26.1 21.4 %collective-permute-start = (bf16[24,9216]{1,0:T(8,128)(2,1)S(1)}, bf16[24,9216]{1,0:T(8,128)(2,1)S(1)}, u32[]{:S(2)}, u32[]{:S(2)}) collective-permute-start(bf16[24,9216]{1,0:T(8,128)(2,1)S(1)} %bitcast_dynamic-update-slice_fusion.2), channel_id=1, source_target_pairs={{0,16},{8,24},{16,0},{24,8},{1,17},{9,25},{17,1},{25,9},{2,18},{10... | collective-permute-start | bytes 1327112 | tf_op jit(solution)/shard_map/ppermute | solution.py:38
  26.4 21.3 %collective-permute-start.2 = (bf16[24,9216]{1,0:T(8,128)(2,1)S(1)}, bf16[24,9216]{1,0:T(8,128)(2,1)S(1)}, u32[]{:S(2)}, u32[]{:S(2)}) collective-permute-start(bf16[24,9216]{1,0:T(8,128)(2,1)S(1)} %bitcast_dynamic-update-slice_fusion.2), channel_id=1, source_target_pairs={{0,8},{8,0},{16,24},{24,16},{1,9},{9,1},{17,25},{25,17},{2,10},{10... | collective-permute-start | bytes 1327112 | tf_op jit(solution)/shard_map/ppermute | solution.py:38
  61.2 177.2 %all-gather.8.cloned.1.call-start = ((), (), s32[]{:S(2)}) async-start(), calls=%async_computation.4 | async-start | bytes 11943936 | tf_op jit(solution)/shard_map/all_gather | solution.py:769
  72.9 24.2 %collective-permute-start.8 = (bf16[3,192,256]{2,1,0:T(8,128)(2,1)}, bf16[3,192,256]{2,1,0:T(8,128)(2,1)S(1)}, u32[]{:S(2)}, u32[]{:S(2)}) collective-permute-start(bf16[3,192,256]{2,1,0:T(8,128)(2,1)} %get-tuple-element.154), channel_id=1, source_target_pairs={{0,6},{1,7},{2,4},{3,5},{4,2},{5,3},{6,0},{7,1},{8,14},{9,15},{10,... | collective-permute-start | bytes 884744 | tf_op jit(solution)/shard_map/ppermute | solution.py:38
  73.5 24.9 %collective-permute-start.9 = (bf16[3,192,256]{2,1,0:T(8,128)(2,1)}, bf16[3,192,256]{2,1,0:T(8,128)(2,1)S(1)}, u32[]{:S(2)}, u32[]{:S(2)}) collective-permute-start(bf16[3,192,256]{2,1,0:T(8,128)(2,1)} %get-tuple-element.155.rest_0_), channel_id=1, source_target_pairs={{0,1},{1,0},{2,3},{3,2},{4,5},{5,4},{6,7},{7,6},{8,9},{9,8},{10,11... | collective-permute-start | bytes 884744 | tf_op jit(solution)/shard_map/ppermute | solution.py:38
  100.1 45.6 %collective-permute-start.16 = (bf16[24,6912]{1,0:T(8,128)(2,1)S(1)}, bf16[24,6912]{1,0:T(8,128)(2,1)S(1)}, u32[]{:S(2)}, u32[]{:S(2)}) collective-permute-start(bf16[24,6912]{1,0:T(8,128)(2,1)S(1)} %get-tuple-element.167), channel_id=1, source_target_pairs={{0,8},{8,0},{16,24},{24,16},{1,9},{9,1},{17,25},{25,17},{2,10},{10... | collective-permute-start | bytes 995336 | tf_op jit(solution)/shard_map/ppermute | solution.py:38
  115.6 30.1 %collective-permute-start.18 = (bf16[24,6912]{1,0:T(8,128)(2,1)S(1)}, bf16[24,6912]{1,0:T(8,128)(2,1)S(1)}, u32[]{:S(2)}, u32[]{:S(2)}) collective-permute-start(bf16[24,6912]{1,0:T(8,128)(2,1)S(1)} %collective-permute-done.17), channel_id=1, source_target_pairs={{0,8},{8,0},{16,24},{24,16},{1,9},{9,1},{17,25},{25,17},{2,10},{10... | collective-permute-start | bytes 995336 | tf_op jit(solution)/shard_map/ppermute | solution.py:38
  147.1 219.2 %reduce-scatter.3.cloned.1.call-start = ((), (), s32[]{:S(2)}) async-start(), calls=%async_computation.5 | async-start | bytes 11943936 | tf_op jit(solution)/shard_map/reduce_scatter | solution.py:887
  172.7 23.8 %collective-permute-start.21 = (bf16[3,192,256]{2,1,0:T(8,128)(2,1)}, bf16[3,192,256]{2,1,0:T(8,128)(2,1)S(1)}, u32[]{:S(2)}, u32[]{:S(2)}) collective-permute-start(bf16[3,192,256]{2,1,0:T(8,128)(2,1)} %get-tuple-element.179), channel_id=1, source_target_pairs={{0,6},{1,7},{2,4},{3,5},{4,2},{5,3},{6,0},{7,1},{8,14},{9,15},{10,... | collective-permute-start | bytes 884744 | tf_op jit(solution)/shard_map/ppermute | solution.py:38
  174.0 22.5 %collective-permute-start.22 = (bf16[3,192,256]{2,1,0:T(8,128)(2,1)}, bf16[3,192,256]{2,1,0:T(8,128)(2,1)S(1)}, u32[]{:S(2)}, u32[]{:S(2)}) collective-permute-start(bf16[3,192,256]{2,1,0:T(8,128)(2,1)} %get-tuple-element.176.rest_0_), channel_id=1, source_target_pairs={{0,1},{1,0},{2,3},{3,2},{4,5},{5,4},{6,7},{7,6},{8,9},{9,8},{10,11... | collective-permute-start | bytes 884744 | tf_op jit(solution)/shard_map/ppermute | solution.py:38
  265.8 194.0 %reduce-scatter.5.cloned.1.call-start = ((), (), s32[]{:S(2)}) async-start(), calls=%async_computation.6 | async-start | bytes 11943936 | tf_op jit(solution)/shard_map/reduce_scatter | solution.py:887
  303.3 26.7 %collective-permute-start.35 = (bf16[3,192,256]{2,1,0:T(8,128)(2,1)S(1)}, bf16[3,192,256]{2,1,0:T(8,128)(2,1)S(1)}, u32[]{:S(2)}, u32[]{:S(2)}) collective-permute-start(bf16[3,192,256]{2,1,0:T(8,128)(2,1)S(1)} %pad_maximum_fusion.10), channel_id=1, source_target_pairs={{0,6},{1,7},{2,4},{3,5},{4,2},{5,3},{6,0},{7,1},{8,14},{9,15},{10,... | collective-permute-start | bytes 884744 | tf_op jit(solution)/shard_map/ppermute | solution.py:38
  378.1 28.6 %collective-permute-start.44 = (bf16[216,768]{1,0:T(8,128)(2,1)}, bf16[216,768]{1,0:T(8,128)(2,1)}, u32[]{:S(2)}, u32[]{:S(2)}) collective-permute-start(bf16[216,768]{1,0:T(8,128)(2,1)} %get-tuple-element.241), channel_id=1, source_target_pairs={{0,8},{8,0},{16,24},{24,16},{1,9},{9,1},{17,25},{25,17},{2,10},{10... | collective-permute-start | bytes 995336 | tf_op jit(solution)/shard_map/ppermute | solution.py:38
  379.6 27.1 %collective-permute-start.45 = (bf16[216,768]{1,0:T(8,128)(2,1)S(1)}, bf16[216,768]{1,0:T(8,128)(2,1)S(1)}, u32[]{:S(2)}, u32[]{:S(2)}) collective-permute-start(bf16[216,768]{1,0:T(8,128)(2,1)S(1)} %get-tuple-element.242), channel_id=1, source_target_pairs={{0,16},{8,24},{16,0},{24,8},{1,17},{9,25},{17,1},{25,9},{2,18},{10... | collective-permute-start | bytes 995336 | tf_op jit(solution)/shard_map/ppermute | solution.py:38
  382.0 24.7 %collective-permute-start.46 = (bf16[216,768]{1,0:T(8,128)(2,1)S(1)}, bf16[216,768]{1,0:T(8,128)(2,1)}, u32[]{:S(2)}, u32[]{:S(2)}) collective-permute-start(bf16[216,768]{1,0:T(8,128)(2,1)S(1)} %get-tuple-element.243), channel_id=1, source_target_pairs={{0,24},{8,16},{16,8},{24,0},{1,25},{9,17},{17,9},{25,1},{2,26},{10... | collective-permute-start | bytes 995336 | tf_op jit(solution)/shard_map/ppermute | solution.py:38
  383.7 23.0 %collective-permute-start.42 = (bf16[160,768]{1,0:T(8,128)(2,1)S(1)}, bf16[160,768]{1,0:T(8,128)(2,1)S(1)}, u32[]{:S(2)}, u32[]{:S(2)}) collective-permute-start(bf16[160,768]{1,0:T(8,128)(2,1)S(1)} %slice_bitcast_fusion.11), channel_id=1, source_target_pairs={{0,4},{1,5},{2,6},{3,7},{4,0},{5,1},{6,2},{7,3},{8,12},{9,13},{10,... | collective-permute-start | bytes 737288 | tf_op jit(solution)/shard_map/ppermute | solution.py:38
  385.3 21.4 %collective-permute-start.43 = (bf16[160,768]{1,0:T(8,128)(2,1)S(1)}, bf16[160,768]{1,0:T(8,128)(2,1)S(1)}, u32[]{:S(2)}, u32[]{:S(2)}) collective-permute-start(bf16[160,768]{1,0:T(8,128)(2,1)S(1)} %slice_bitcast_fusion.10), channel_id=1, source_target_pairs={{0,2},{1,3},{2,0},{3,1},{4,6},{5,7},{6,4},{7,5},{8,10},{9,11},{10,... | collective-permute-start | bytes 737288 | tf_op jit(solution)/shard_map/ppermute | solution.py:38
  408.2 35.7 %collective-permute-start.52 = (bf16[216,768]{1,0:T(8,128)(2,1)S(1)}, bf16[216,768]{1,0:T(8,128)(2,1)S(1)}, u32[]{:S(2)}, u32[]{:S(2)}) collective-permute-start(bf16[216,768]{1,0:T(8,128)(2,1)S(1)} %add_convert_fusion.8), channel_id=1, source_target_pairs={{0,8},{8,0},{16,24},{24,16},{1,9},{9,1},{17,25},{25,17},{2,10},{10... | collective-permute-start | bytes 995336 | tf_op jit(solution)/shard_map/ppermute | solution.py:38
  412.0 31.9 %collective-permute-start.53 = (bf16[216,768]{1,0:T(8,128)(2,1)S(1)}, bf16[216,768]{1,0:T(8,128)(2,1)S(1)}, u32[]{:S(2)}, u32[]{:S(2)}) collective-permute-start(bf16[216,768]{1,0:T(8,128)(2,1)S(1)} %add_convert_fusion.8), channel_id=1, source_target_pairs={{0,16},{8,24},{16,0},{24,8},{1,17},{9,25},{17,1},{25,9},{2,18},{10... | collective-permute-start | bytes 995336 | tf_op jit(solution)/shard_map/ppermute | solution.py:38
  480.9 20.0 %collective-permute-start.68 = (bf16[216,768]{1,0:T(8,128)(2,1)S(1)}, bf16[216,768]{1,0:T(8,128)(2,1)S(1)}, u32[]{:S(2)}, u32[]{:S(2)}) collective-permute-start(bf16[216,768]{1,0:T(8,128)(2,1)S(1)} %get-tuple-element.311), channel_id=1, source_target_pairs={{0,8},{8,0},{16,24},{24,16},{1,9},{9,1},{17,25},{25,17},{2,10},{10... | collective-permute-start | bytes 995336 | tf_op jit(solution)/shard_map/ppermute | solution.py:38
  505.6 23.4 %collective-permute-start.73 = (bf16[216,768]{1,0:T(8,128)(2,1)S(1)}, bf16[216,768]{1,0:T(8,128)(2,1)S(1)}, u32[]{:S(2)}, u32[]{:S(2)}) collective-permute-start(bf16[216,768]{1,0:T(8,128)(2,1)S(1)} %fusion.3), channel_id=1, source_target_pairs={{0,8},{8,0},{16,24},{24,16},{1,9},{9,1},{17,25},{25,17},{2,10},{10... | collective-permute-start | bytes 995336 | tf_op jit(solution)/shard_map/ppermute | solution.py:38
  508.2 20.9 %collective-permute-start.74 = (bf16[216,768]{1,0:T(8,128)(2,1)S(1)}, bf16[216,768]{1,0:T(8,128)(2,1)S(1)}, u32[]{:S(2)}, u32[]{:S(2)}) collective-permute-start(bf16[216,768]{1,0:T(8,128)(2,1)S(1)} %fusion.3), channel_id=1, source_target_pairs={{0,16},{8,24},{16,0},{24,8},{1,17},{9,25},{17,1},{25,9},{2,18},{10... | collective-permute-start | bytes 995336 | tf_op jit(solution)/shard_map/ppermute | solution.py:38
  (110 other events, 1104.6 us)
Sparse Core Ops, SparseCore 0:
  26.0 34.7 all-gather.5
  63.3 92.0 all-gather.3
  157.9 80.5 all-gather.7
  265.9 95.2 reduce-scatter.2
  364.6 95.2 reduce-scatter.4

commit v5 on v4

--- a/solution.py
+++ b/solution.py
@@ -403,6 +403,7 @@
     devices,
     pieces,
     depth,
+    apart,
     order,
     grad_ref,
     first_ref,
@@ -412,8 +413,11 @@
 ):
     wo_ref, wu_ref, wd_ref, vec, ub_ref = rest[:5]
     contexts, rest = rest[5 : 5 + groups], rest[5 + groups :]
-    shares, grad_first, small = rest[:3]
-    grad_contexts, rest = rest[3 : 3 + groups], rest[3 + groups :]
+    shares, rest = rest[0], rest[1:]
+    if apart:
+        out_shares, rest = rest[0], rest[1:]
+    grad_first, small = rest[:2]
+    grad_contexts, rest = rest[2 : 2 + groups], rest[2 + groups :]
     grad_out, grad_hidden, tile, down = rest
     width = vec.shape[-1]
     j = pl.program_id(0)
@@ -469,22 +473,40 @@
             grad_contexts[r][...] = nt(wo_ref[pl.ds(start, span), :], low).astype(BF16)
         last = down_share + blocks * share
         for i in range(devices):
-            shares[i, last : last + share, :] = tile[i * share : (i + 1) * share, :]
+            rows = tile[i * share : (i + 1) * share, :]
+            if apart:
+                out_shares[i] = rows
+            else:
+                shares[i, last : last + share, :] = rows
 
 
 def feed_back(
-    order, grad, first, second, low, w_output, w_up, w_down, vectors, up_bias, contexts, devices
+    order,
+    grad,
+    first,
+    second,
+    low,
+    w_output,
+    w_up,
+    w_down,
+    vectors,
+    up_bias,
+    contexts,
+    devices,
+    apart,
 ):
     (w_output, at_output), (w_up, at_up), (w_down, pieces, depth) = w_output, w_up, w_down
     tokens, width = grad.shape
     groups, span = len(contexts), contexts[0].shape[0]
     blocks = up_bias.shape[0]
     share = width // devices
-    kept = (devices, (2 * blocks + 1) * share, width)
+    kept = [(devices, (2 * blocks + 1) * share, width)]
+    if apart:
+        kept = [(devices, 2 * blocks * share, width), (devices, share, width)]
     return pl.pallas_call(
-        functools.partial(feed_back_body, groups, span, blocks, devices, pieces, depth),
-        out_shape=[
-            jax.ShapeDtypeStruct(kept, BF16),
+        functools.partial(feed_back_body, groups, span, blocks, devices, pieces, depth, apart),
+        out_shape=[jax.ShapeDtypeStruct(item, BF16) for item in kept]
+        + [
             jax.ShapeDtypeStruct((tokens, width), F32),
             jax.ShapeDtypeStruct((SMALL_ROWS, width), F32),
         ]
@@ -500,7 +522,8 @@
             pl.BlockSpec((1, 1, width), lambda j: (j, 0, 0)),
         ]
         + [resident((span, tokens))] * groups,
-        out_specs=[resident(kept), resident((tokens, width)), resident((SMALL_ROWS, width))]
+        out_specs=[resident(item) for item in kept]
+        + [resident((tokens, width)), resident((SMALL_ROWS, width))]
         + [resident((span, tokens))] * groups,
         scratch_shapes=[
             pltpu.VMEM((tokens, width), BF16),
@@ -749,6 +772,10 @@
             exchange(items[r], "seq", seq_size, r * members) for r in range(1, groups)
         ]
 
+    def over_devices(terms):
+        rows = terms.reshape(-1, width)
+        return lax.psum_scatter(rows, "seq", scatter_dimension=0, tiled=True)
+
     def with_members(items):
         items = list(items)
         own = list(items)
@@ -870,7 +897,7 @@
     for layer in reversed(range(LAYERS)):
         w_output, w_up, w_down = w_rest[layer]
         entered, parts, exact, log_total, contexts, sum_first, low, sum_second = saved[layer]
-        terms, grad_first, small, *grad_mixed = feed_back(
+        terms, *made = feed_back(
             order,
             grad,
             sum_first,
@@ -883,10 +910,12 @@
             up_biases[layer],
             contexts,
             seq_size,
+            layer == 0,
         )
-        shares[layer] = lax.psum_scatter(
-            terms.reshape(-1, width), "seq", scatter_dimension=0, tiled=True
-        )
+        if layer == 0:
+            out_terms, *made = made
+        grad_first, small, *grad_mixed = made
+        shares[layer] = over_devices(terms)
         grad_mixed = tick(behind, tuple(grad_mixed))
         if layer + 1 < LAYERS:
             grad_mixed, later = lax.optimization_barrier((grad_mixed, shares[layer + 1]))
@@ -896,6 +925,9 @@
         grads = tuple(swap_groups(grad_mixed))
         if layer + 1 < LAYERS:
             grads = tick([backs[layer + 1]], grads)
+        if layer == 0:
+            grads, out_terms = lax.optimization_barrier((grads, out_terms))
+            out_share = over_devices(out_terms)
         made = attend_back(
             active, seg_row, seg_col, parts, grads, exact, log_total, groups, members
         )
@@ -907,18 +939,23 @@
             for r in range(groups)
         )
         pieces = tuple(swap_groups(messages))
+        if layer + 1 < LAYERS:
+            pieces = tick([backs[layer + 1]], pieces)
         made = project_back(
             order, place, entered, grad_first, w_project[layer], small, pieces, seq_size
         )
-        own, send, grad = tick(behind, tuple(made))
+        own, send, grad = tick([item for item in feeds if item is not None], tuple(made))
         backs[layer] = Stream(sum_steps(own, send, seq_size, dp_size, dp_me))
         behind = [backs[layer]]
-    last = tick(backs, shares[0])
+    last = tick(backs[:1], shares[0])
     feeds[0] = Stream(dp_steps(last, dp_size, dp_me))
     behind = backs + feeds
-    for unused in range(2):
-        tick(behind)
-        tick(backs)
+    tick(behind)
+    tick(backs)
+    last = tick(behind, out_share)
+    out_stream = Stream(dp_direct_steps(last, dp_size, dp_me))
+    tick(backs + [out_stream])
+    behind = behind + [out_stream]
     while any(item.flying is not None for item in behind):
         tick(behind)
     small = jnp.stack(
@@ -936,7 +973,8 @@
     g_project = jnp.stack([columns(item[1], range(3)) for item in results])
     g_up = jnp.stack([columns(item[0], range(blocks, 2 * blocks)) for item in results])
     g_down = jnp.stack([item[0][:down_rows].astype(F32) for item in results])
-    g_output = jnp.stack([item[0][down_rows + blocks * share :].astype(F32) for item in results])
+    outs = [out_stream.result] + [item[0][down_rows + blocks * share :] for item in results[1:]]
+    g_output = jnp.stack(outs).astype(F32)
     wide = small[:, SMALL_UP : SMALL_UP + blocks].reshape(LAYERS, blocks * width)
     return (
         output,

time: 553 us -> 560 us (1.013)
  waiting for transfers between devices: 244 us -> 234 us
  starting transfers between devices: 86.6 us -> 95 us
    ppermute x77 -> x83, starting transfers between devices: 86 us -> 94.1 us  [exchange(): return lax.ppermute(value, axis, [(i, i ^ mask) for i in range(size)])]
    reduce_scatter x2 -> x3, waiting for transfers between devices: 7.65 us -> 0.01 us  [over_devices(): return lax.psum_scatter(rows, 'seq', scatter_dimension=0, tiled=True)]
    ppermute x77 -> x83, waiting for transfers between devices: 220 us -> 217 us  [exchange(): return lax.ppermute(value, axis, [(i, i ^ mask) for i in range(size)])]
  transfers between devices with their start and end apart: 82 -> 89, of which waited for: 41 -> 49; matrix products, arithmetic and copies ran while one was open for 6% -> 7% of each run, Pallas kernels for 23% -> 23%
where the time goes in v5:
time: 560 us; the launch traced here: 556 us
  waiting for transfers between devices  234 us (42%)
  Pallas kernels  157 us (28%)
  starting transfers between devices  95 us (17%)
  other arithmetic  34 us (6%)
  local copies, waits for them, and re-layouts  20.8 us (4%)
  between operations  15.2 us (3%)
    ppermute x83, waiting for transfers between devices, exchange(): return lax.ppermute(value, axis, [(i, i ^ mask) for i in range(size)])  217 us
    ppermute x83, starting transfers between devices, exchange(): return lax.ppermute(value, axis, [(i, i ^ mask) for i in range(size)])  94.1 us
    pallas_call x2, Pallas kernels, attend_back(): pl.pallas_call(functools.partial(attend_back_body, groups, members, heads...  41.7 us
    pallas_call x2, Pallas kernels, feed_back(): pl.pallas_call(functools.partial(feed_back_body, groups, span, blocks, de...  34.4 us
    pallas_call x2, Pallas kernels, attend(): pl.pallas_call(functools.partial(attend_body, groups, members, heads), ou...  34.1 us
    pallas_call x2, Pallas kernels, feed(): pl.pallas_call(functools.partial(feed_body, groups, span, blocks, pieces,...  20.1 us
    all_gather x3, waiting for transfers between devices, over_seq(): return lax.all_gather(stack, 'seq', axis=1, tiled=True).reshape(width, -1)  16.8 us
    pallas_call x2, Pallas kernels, project_back(): pl.pallas_call(functools.partial(project_back_body, groups, span, devices...  15 us
  transfers between devices with their start and end apart: 89, of which 49 were waited for; matrix products, arithmetic and copies ran while one was open for 7% of the time, Pallas kernels for 23%

profile of v5, /device:TPU:0, one launch (start us, length us, event | category | flops | bytes accessed | tf_op | source)
XLA Modules:
  0.0 556.0 jit_solution(4928650480839406365)
XLA Ops:
  29.2 18.3 %collective-permute-done = bf16[24,9216]{1,0:T(8,128)(2,1)S(1)} collective-permute-done((bf16[24,9216]{1,0:T(8,128)(2,1)S(1)}, bf16[24,9216]{1,0:T(8,128)(2,1)S(1)}, u32[]{:S(2)}, u32[]{:S(2)}) %collective-permute-start) | collective-permute-done | bytes 442400 | tf_op jit(solution)/shard_map/ppermute | solution.py:38
  47.8 11.9 %collective-permute-done.1 = bf16[24,9216]{1,0:T(8,128)(2,1)S(1)} collective-permute-done((bf16[24,9216]{1,0:T(8,128)(2,1)S(1)}, bf16[24,9216]{1,0:T(8,128)(2,1)S(1)}, u32[]{:S(2)}, u32[]{:S(2)}) %collective-permute-start.1) | collective-permute-done | bytes 442400 | tf_op jit(solution)/shard_map/ppermute | solution.py:38
  74.1 11.2 %collective-permute-done.6.rest_1_ = bf16[3,192,256]{2,1,0:T(8,128)(2,1)S(1)} collective-permute-done((bf16[3,192,256]{2,1,0:T(8,128)(2,1)}, bf16[3,192,256]{2,1,0:T(8,128)(2,1)S(1)}, u32[]{:S(2)}, u32[]{:S(2)}) %collective-permute-start.6) | collective-permute-done | bytes 294944 | tf_op jit(solution)/shard_map/ppermute | solution.py:38
  89.4 7.8 %collective-permute-done.8.rest_3_ = bf16[3,192,256]{2,1,0:T(8,128)(2,1)S(1)} collective-permute-done((bf16[3,192,256]{2,1,0:T(8,128)(2,1)}, bf16[3,192,256]{2,1,0:T(8,128)(2,1)S(1)}, u32[]{:S(2)}, u32[]{:S(2)}) %collective-permute-start.8) | collective-permute-done | bytes 294944 | tf_op jit(solution)/shard_map/ppermute | solution.py:38
  100.9 14.8 %collective-permute-done.17 = bf16[24,6912]{1,0:T(8,128)(2,1)S(1)} collective-permute-done((bf16[24,6912]{1,0:T(8,128)(2,1)S(1)}, bf16[24,6912]{1,0:T(8,128)(2,1)S(1)}, u32[]{:S(2)}, u32[]{:S(2)}) %collective-permute-start.17) | collective-permute-done | bytes 331808 | tf_op jit(solution)/shard_map/ppermute | solution.py:38
  116.3 17.1 %attend.2 = (bf16[192,256]{1,0:T(8,128)(2,1)}, bf16[192,256]{1,0:T(8,128)(2,1)}, bf16[192,256]{1,0:T(8,128)(2,1)}, bf16[192,256]{1,0:T(8,128)(2,1)}, f32[4,192,256]{2,1,0:T(8,128)}, /*index=5*/f32[4,3,1,256]{3,2,1,0:T(1,128)}) custom-call(s32[4,8]{1,0:T(4,128)} %and_convert_fusion.active, s32[4,1,256]{2,1,0:T(1,128)} %broadcast_in_dim.37.seg_row, ...), custom_call_target="tpu_custom_call" | custom-call | flops 805306368 | bytes 3932160 | tf_op jit(solution)/shard_map/attend/pallas_call | solution.py:198
  155.4 10.0 %feed.2 = (f32[256,768]{1,0:T(8,128)}, bf16[256,768]{1,0:T(8,128)(2,1)}, f32[256,768]{1,0:T(8,128)}, f32[256,768]{1,0:T(8,128)}) custom-call(s32[4]{0:T(128)} %iota_xor_fusion.order, f32[256,768]{1,0:T(8,128)} %bitcast_convert_fusion.1.x_ref, bf16[768,9216]{1,0:T(8,128)(2,1)} %bitcast.266, bf16[768,9216]{1,0:T(8,128)(2,1)} %bitcast.267, ...), custom_call_target="tpu_custom_call" | custom-call | flops 2717908992 | bytes 10616832 | tf_op jit(solution)/shard_map/feed/pallas_call | solution.py:373
  174.0 12.9 %collective-permute-done.19.rest_1_ = bf16[3,192,256]{2,1,0:T(8,128)(2,1)S(1)} collective-permute-done((bf16[3,192,256]{2,1,0:T(8,128)(2,1)}, bf16[3,192,256]{2,1,0:T(8,128)(2,1)S(1)}, u32[]{:S(2)}, u32[]{:S(2)}) %collective-permute-start.19) | collective-permute-done | bytes 294944 | tf_op jit(solution)/shard_map/ppermute | solution.py:38
  189.2 7.3 %collective-permute-done.21.rest_3_ = bf16[3,192,256]{2,1,0:T(8,128)(2,1)S(1)} collective-permute-done((bf16[3,192,256]{2,1,0:T(8,128)(2,1)}, bf16[3,192,256]{2,1,0:T(8,128)(2,1)S(1)}, u32[]{:S(2)}, u32[]{:S(2)}) %collective-permute-start.21) | collective-permute-done | bytes 294944 | tf_op jit(solution)/shard_map/ppermute | solution.py:38
  198.8 17.0 %attend.3 = (bf16[192,256]{1,0:T(8,128)(2,1)}, bf16[192,256]{1,0:T(8,128)(2,1)}, bf16[192,256]{1,0:T(8,128)(2,1)}, bf16[192,256]{1,0:T(8,128)(2,1)}, f32[4,192,256]{2,1,0:T(8,128)}, /*index=5*/f32[4,3,1,256]{3,2,1,0:T(1,128)}) custom-call(s32[4,8]{1,0:T(4,128)} %and_convert_fusion.active, s32[4,1,256]{2,1,0:T(1,128)} %broadcast_in_dim.37.seg_row, ...), custom_call_target="tpu_custom_call" | custom-call | flops 805306368 | bytes 3932160 | tf_op jit(solution)/shard_map/attend/pallas_call | solution.py:198
  227.9 10.7 %all-gather.8.cloned.1.call-done = bf16[4,192,6912]{2,1,0:T(8,128)(2,1)} async-done(((bf16[4,24,6912]{2,1,0:T(8,128)(2,1)}), bf16[4,192,6912]{2,1,0:T(8,128)(2,1)}) %all-gather.8.cloned.1.call-update) | async-done | bytes 10616848 | tf_op jit(solution)/shard_map/all_gather | solution.py:796
  238.5 10.1 %feed.3 = (f32[256,768]{1,0:T(8,128)}, bf16[256,768]{1,0:T(8,128)(2,1)}, f32[256,768]{1,0:T(8,128)}, f32[256,768]{1,0:T(8,128)}) custom-call(s32[4]{0:T(128)} %iota_xor_fusion.order, f32[256,768]{1,0:T(8,128)} %get-tuple-element.193.x_ref, bf16[768,6912]{1,0:T(8,128)(2,1)} %bitcast.274, bf16[768,6912]{1,0:T(8,128)(2,1)} %bitcast.275, ...), custom_call_target="tpu_custom_call" | custom-call | flops 2717908992 | bytes 10616832 | tf_op jit(solution)/shard_map/feed/pallas_call | solution.py:373
  248.6 17.1 %feed_back.2 = (bf16[8,864,768]{2,1,0:T(8,128)(2,1)}, f32[256,768]{1,0:T(8,128)}, f32[16,768]{1,0:T(8,128)}, bf16[192,256]{1,0:T(8,128)(2,1)}, bf16[192,256]{1,0...) custom-call(s32[4]{0:T(128)} %iota_xor_fusion.order, f32[256,768]{1,0:T(8,128)} %bitcast_convert_fusion.grad_ref, ...), custom_call_target="tpu_custom_call" | custom-call | flops 6643777536 | bytes 21233664 | tf_op jit(solution)/shard_map/feed_back/pallas_call | solution.py:506
  275.5 21.4 %attend_back.2 = (bf16[4,192,256]{2,1,0:T(8,128)(2,1)}, f32[4,2,192,256]{3,2,1,0:T(8,128)}, bf16[4,2,192,256]{3,2,1,0:T(8,128)(2,1)}) custom-call(s32[4,8]{1,0:T(4,128)} %and_convert_fusion.active, s32[4,1,256]{2,1,0:T(1,128)} %broadcast_in_dim.37.seg_row, s32[8,256,1]{2,1,0:T(8,128)} %select_convert_fusion.seg_col, ...), custom_call_target="tpu_custom_call" | custom-call | flops 2013265920 | bytes 7864320 | tf_op jit(solution)/shard_map/attend_back/pallas_call | solution.py:284
  305.9 11.8 %collective-permute-done.33.rest_1_ = bf16[3,192,256]{2,1,0:T(8,128)(2,1)S(1)} collective-permute-done((bf16[3,192,256]{2,1,0:T(8,128)(2,1)S(1)}, bf16[3,192,256]{2,1,0:T(8,128)(2,1)S(1)}, u32[]{:S(2)}, u32[]{:S(2)}) %collective-permute-start.33) | collective-permute-done | bytes 294944 | tf_op jit(solution)/shard_map/ppermute | solution.py:38
  318.5 11.4 %collective-permute-done.35.rest_3_ = bf16[3,192,256]{2,1,0:T(8,128)(2,1)S(1)} collective-permute-done((bf16[3,192,256]{2,1,0:T(8,128)(2,1)S(1)}, bf16[3,192,256]{2,1,0:T(8,128)(2,1)S(1)}, u32[]{:S(2)}, u32[]{:S(2)}) %collective-permute-start.35) | collective-permute-done | bytes 294944 | tf_op jit(solution)/shard_map/ppermute | solution.py:38
  330.7 7.6 %project_back.2 = (bf16[4,320,768]{2,1,0:T(8,128)(2,1)}, bf16[4,320,768]{2,1,0:T(8,128)(2,1)}, f32[256,768]{1,0:T(8,128)}) custom-call(s32[4]{0:T(128)} %iota_xor_fusion.order, s32[1]{0:T(128)} %bitcast.43.place, f32[256,768]{1,0:T(8,128)} %get-tuple-element.193.x_ref, f32[256,768]{1,0:T(8,128)} %get-tuple-element.209.grad_ref, bf16[768,9216]{1,0:T(8,128)(2,1)} %bitcast.270, ...), custom_call_target="tpu_custom_call" | custom-call | flops 1811939328 | bytes 7077888 | tf_op jit(solution)/shard_map/project_back/pallas_call | solution.py:595
  338.2 17.3 %feed_back.3 = (bf16[8,768,768]{2,1,0:T(8,128)(2,1)}, bf16[8,96,768]{2,1,0:T(8,128)(2,1)}, f32[256,768]{1,0:T(8,128)}, f32[16,768]{1,0:T(8,128)}, bf16[192,256]{...) custom-call(s32[4]{0:T(128)} %iota_xor_fusion.order, ...), custom_call_target="tpu_custom_call" | custom-call | flops 6643777536 | bytes 21233664 | tf_op jit(solution)/shard_map/feed_back/pallas_call | solution.py:506
  387.2 20.2 %attend_back.3 = (bf16[4,192,256]{2,1,0:T(8,128)(2,1)}, f32[4,2,192,256]{3,2,1,0:T(8,128)}, bf16[4,2,192,256]{3,2,1,0:T(8,128)(2,1)}) custom-call(s32[4,8]{1,0:T(4,128)} %and_convert_fusion.active, s32[4,1,256]{2,1,0:T(1,128)} %broadcast_in_dim.37.seg_row, s32[8,256,1]{2,1,0:T(8,128)} %select_convert_fusion.seg_col, ...), custom_call_target="tpu_custom_call" | custom-call | flops 2013265920 | bytes 7864320 | tf_op jit(solution)/shard_map/attend_back/pallas_call | solution.py:284
  432.6 7.4 %project_back.3 = (bf16[4,320,768]{2,1,0:T(8,128)(2,1)}, bf16[4,320,768]{2,1,0:T(8,128)(2,1)}, f32[256,768]{1,0:T(8,128)}) custom-call(s32[4]{0:T(128)} %iota_xor_fusion.order, s32[1]{0:T(128)} %bitcast.43.place, f32[256,768]{1,0:T(8,128)} %bitcast_convert_fusion.1.x_ref, f32[256,768]{1,0:T(8,128)} %get-tuple-element.228.grad_ref, ...), custom_call_target="tpu_custom_call" | custom-call | flops 1811939328 | bytes 7077888 | tf_op jit(solution)/shard_map/project_back/pallas_call | solution.py:595
  445.3 7.1 %collective-permute-start.58 = (bf16[80,768]{1,0:T(8,128)(2,1)}, bf16[80,768]{1,0:T(8,128)(2,1)}, u32[]{:S(2)}, u32[]{:S(2)}) collective-permute-start(bf16[80,768]{1,0:T(8,128)(2,1)} %get-tuple-element.381), channel_id=1, source_target_pairs={{0,8},{8,0},{16,24},{24,16},{1,9},{9,1},{17,25},{25,17},{2,10},{10... | collective-permute-start | bytes 368648 | tf_op jit(solution)/shard_map/ppermute | solution.py:38
  463.3 7.0 %collective-permute-done.60 = bf16[192,768]{1,0:T(8,128)(2,1)S(1)} collective-permute-done((bf16[192,768]{1,0:T(8,128)(2,1)S(1)}, bf16[192,768]{1,0:T(8,128)(2,1)S(1)}, u32[]{:S(2)}, u32[]{:S(2)}) %collective-permute-start.60) | collective-permute-done | bytes 294944 | tf_op jit(solution)/shard_map/ppermute | solution.py:38
  481.9 9.0 %collective-permute-done.64 = bf16[80,768]{1,0:T(8,128)(2,1)} collective-permute-done((bf16[80,768]{1,0:T(8,128)(2,1)S(1)}, bf16[80,768]{1,0:T(8,128)(2,1)}, u32[]{:S(2)}, u32[]{:S(2)}) %collective-permute-start.64) | collective-permute-done | bytes 122912 | tf_op jit(solution)/shard_map/ppermute | solution.py:38
  505.6 12.8 %collective-permute-done.70 = bf16[80,768]{1,0:T(8,128)(2,1)S(1)} collective-permute-done((bf16[80,768]{1,0:T(8,128)(2,1)S(1)}, bf16[80,768]{1,0:T(8,128)(2,1)S(1)}, u32[]{:S(2)}, u32[]{:S(2)}) %collective-permute-start.70) | collective-permute-done | bytes 122912 | tf_op jit(solution)/shard_map/ppermute | solution.py:38
  (401 shorter events, 241.8 us)
Async XLA Ops:
  7.2 56.0 %all-gather.6.cloned.1.call-start = ((), (), s32[]{:S(2)}) async-start(), calls=%async_computation.4 | async-start | bytes 4202496 | tf_op jit(solution)/shard_map/all_gather | solution.py:796
  25.9 129.5 %all-gather.4.cloned.1.call-start = ((), (), s32[]{:S(2)}) async-start(), calls=%async_computation.3 | async-start | bytes 15925248 | tf_op jit(solution)/shard_map/all_gather | solution.py:796
  26.1 21.4 %collective-permute-start = (bf16[24,9216]{1,0:T(8,128)(2,1)S(1)}, bf16[24,9216]{1,0:T(8,128)(2,1)S(1)}, u32[]{:S(2)}, u32[]{:S(2)}) collective-permute-start(bf16[24,9216]{1,0:T(8,128)(2,1)S(1)} %bitcast_dynamic-update-slice_fusion.2), channel_id=1, source_target_pairs={{0,16},{8,24},{16,0},{24,8},{1,17},{9,25},{17,1},{25,9},{2,18},{10... | collective-permute-start | bytes 1327112 | tf_op jit(solution)/shard_map/ppermute | solution.py:38
  61.2 177.3 %all-gather.8.cloned.1.call-start = ((), (), s32[]{:S(2)}) async-start(), calls=%async_computation.5 | async-start | bytes 11943936 | tf_op jit(solution)/shard_map/all_gather | solution.py:796
  72.9 24.2 %collective-permute-start.8 = (bf16[3,192,256]{2,1,0:T(8,128)(2,1)}, bf16[3,192,256]{2,1,0:T(8,128)(2,1)S(1)}, u32[]{:S(2)}, u32[]{:S(2)}) collective-permute-start(bf16[3,192,256]{2,1,0:T(8,128)(2,1)} %get-tuple-element.175), channel_id=1, source_target_pairs={{0,6},{1,7},{2,4},{3,5},{4,2},{5,3},{6,0},{7,1},{8,14},{9,15},{10,... | collective-permute-start | bytes 884744 | tf_op jit(solution)/shard_map/ppermute | solution.py:38
  73.5 24.9 %collective-permute-start.9 = (bf16[3,192,256]{2,1,0:T(8,128)(2,1)}, bf16[3,192,256]{2,1,0:T(8,128)(2,1)S(1)}, u32[]{:S(2)}, u32[]{:S(2)}) collective-permute-start(bf16[3,192,256]{2,1,0:T(8,128)(2,1)} %get-tuple-element.176.rest_0_), channel_id=1, source_target_pairs={{0,1},{1,0},{2,3},{3,2},{4,5},{5,4},{6,7},{7,6},{8,9},{9,8},{10,11... | collective-permute-start | bytes 884744 | tf_op jit(solution)/shard_map/ppermute | solution.py:38
  100.2 45.5 %collective-permute-start.16 = (bf16[24,6912]{1,0:T(8,128)(2,1)S(1)}, bf16[24,6912]{1,0:T(8,128)(2,1)S(1)}, u32[]{:S(2)}, u32[]{:S(2)}) collective-permute-start(bf16[24,6912]{1,0:T(8,128)(2,1)S(1)} %get-tuple-element.188), channel_id=1, source_target_pairs={{0,8},{8,0},{16,24},{24,16},{1,9},{9,1},{17,25},{25,17},{2,10},{10... | collective-permute-start | bytes 995336 | tf_op jit(solution)/shard_map/ppermute | solution.py:38
  115.6 30.1 %collective-permute-start.18 = (bf16[24,6912]{1,0:T(8,128)(2,1)S(1)}, bf16[24,6912]{1,0:T(8,128)(2,1)S(1)}, u32[]{:S(2)}, u32[]{:S(2)}) collective-permute-start(bf16[24,6912]{1,0:T(8,128)(2,1)S(1)} %collective-permute-done.17), channel_id=1, source_target_pairs={{0,8},{8,0},{16,24},{24,16},{1,9},{9,1},{17,25},{25,17},{2,10},{10... | collective-permute-start | bytes 995336 | tf_op jit(solution)/shard_map/ppermute | solution.py:38
  147.1 219.3 %reduce-scatter.4.cloned.1.call-start = ((), (), s32[]{:S(2)}) async-start(), calls=%async_computation.6 | async-start | bytes 11943936 | tf_op jit(solution)/shard_map/reduce_scatter | solution.py:777
  172.7 23.8 %collective-permute-start.21 = (bf16[3,192,256]{2,1,0:T(8,128)(2,1)}, bf16[3,192,256]{2,1,0:T(8,128)(2,1)S(1)}, u32[]{:S(2)}, u32[]{:S(2)}) collective-permute-start(bf16[3,192,256]{2,1,0:T(8,128)(2,1)} %get-tuple-element.200), channel_id=1, source_target_pairs={{0,6},{1,7},{2,4},{3,5},{4,2},{5,3},{6,0},{7,1},{8,14},{9,15},{10,... | collective-permute-start | bytes 884744 | tf_op jit(solution)/shard_map/ppermute | solution.py:38
  174.0 22.5 %collective-permute-start.22 = (bf16[3,192,256]{2,1,0:T(8,128)(2,1)}, bf16[3,192,256]{2,1,0:T(8,128)(2,1)S(1)}, u32[]{:S(2)}, u32[]{:S(2)}) collective-permute-start(bf16[3,192,256]{2,1,0:T(8,128)(2,1)} %get-tuple-element.197.rest_0_), channel_id=1, source_target_pairs={{0,1},{1,0},{2,3},{3,2},{4,5},{5,4},{6,7},{7,6},{8,9},{9,8},{10,11... | collective-permute-start | bytes 884744 | tf_op jit(solution)/shard_map/ppermute | solution.py:38
  265.8 189.5 %reduce-scatter.6.cloned.1.call-start = ((), (), s32[]{:S(2)}) async-start(), calls=%async_computation.7 | async-start | bytes 10616832 | tf_op jit(solution)/shard_map/reduce_scatter | solution.py:777
  303.3 26.7 %collective-permute-start.35 = (bf16[3,192,256]{2,1,0:T(8,128)(2,1)S(1)}, bf16[3,192,256]{2,1,0:T(8,128)(2,1)S(1)}, u32[]{:S(2)}, u32[]{:S(2)}) collective-permute-start(bf16[3,192,256]{2,1,0:T(8,128)(2,1)S(1)} %pad_maximum_fusion.9), channel_id=1, source_target_pairs={{0,6},{1,7},{2,4},{3,5},{4,2},{5,3},{6,0},{7,1},{8,14},{9,15},{10,... | collective-permute-start | bytes 884744 | tf_op jit(solution)/shard_map/ppermute | solution.py:38
  355.6 138.3 %reduce-scatter.8.cloned.1.call-start = ((), (), s32[]{:S(2)}) async-start(), calls=%async_computation.8 | async-start | bytes 1327104 | tf_op jit(solution)/shard_map/reduce_scatter | solution.py:777
  378.2 29.3 %collective-permute-start.44 = (bf16[216,768]{1,0:T(8,128)(2,1)}, bf16[216,768]{1,0:T(8,128)(2,1)S(1)}, u32[]{:S(2)}, u32[]{:S(2)}) collective-permute-start(bf16[216,768]{1,0:T(8,128)(2,1)} %get-tuple-element.267), channel_id=1, source_target_pairs={{0,8},{8,0},{16,24},{24,16},{1,9},{9,1},{17,25},{25,17},{2,10},{10... | collective-permute-start | bytes 995336 | tf_op jit(solution)/shard_map/ppermute | solution.py:38
  379.7 27.8 %collective-permute-start.45 = (bf16[216,768]{1,0:T(8,128)(2,1)S(1)}, bf16[216,768]{1,0:T(8,128)(2,1)S(1)}, u32[]{:S(2)}, u32[]{:S(2)}) collective-permute-start(bf16[216,768]{1,0:T(8,128)(2,1)S(1)} %get-tuple-element.268), channel_id=1, source_target_pairs={{0,16},{8,24},{16,0},{24,8},{1,17},{9,25},{17,1},{25,9},{2,18},{10... | collective-permute-start | bytes 995336 | tf_op jit(solution)/shard_map/ppermute | solution.py:38
  382.1 25.4 %collective-permute-start.46 = (bf16[216,768]{1,0:T(8,128)(2,1)S(1)}, bf16[216,768]{1,0:T(8,128)(2,1)S(1)}, u32[]{:S(2)}, u32[]{:S(2)}) collective-permute-start(bf16[216,768]{1,0:T(8,128)(2,1)S(1)} %get-tuple-element.269), channel_id=1, source_target_pairs={{0,24},{8,16},{16,8},{24,0},{1,25},{9,17},{17,9},{25,1},{2,26},{10... | collective-permute-start | bytes 995336 | tf_op jit(solution)/shard_map/ppermute | solution.py:38
  384.6 23.0 %collective-permute-start.42 = (bf16[160,768]{1,0:T(8,128)(2,1)S(1)}, bf16[160,768]{1,0:T(8,128)(2,1)S(1)}, u32[]{:S(2)}, u32[]{:S(2)}) collective-permute-start(bf16[160,768]{1,0:T(8,128)(2,1)S(1)} %slice_bitcast_fusion.11), channel_id=1, source_target_pairs={{0,4},{1,5},{2,6},{3,7},{4,0},{5,1},{6,2},{7,3},{8,12},{9,13},{10,... | collective-permute-start | bytes 737288 | tf_op jit(solution)/shard_map/ppermute | solution.py:38
  386.1 21.4 %collective-permute-start.43 = (bf16[160,768]{1,0:T(8,128)(2,1)S(1)}, bf16[160,768]{1,0:T(8,128)(2,1)S(1)}, u32[]{:S(2)}, u32[]{:S(2)}) collective-permute-start(bf16[160,768]{1,0:T(8,128)(2,1)S(1)} %slice_bitcast_fusion.10), channel_id=1, source_target_pairs={{0,2},{1,3},{2,0},{3,1},{4,6},{5,7},{6,4},{7,5},{8,10},{9,11},{10,... | collective-permute-start | bytes 737288 | tf_op jit(solution)/shard_map/ppermute | solution.py:38
  416.4 23.6 %collective-permute-start.52 = (bf16[216,768]{1,0:T(8,128)(2,1)S(1)}, bf16[216,768]{1,0:T(8,128)(2,1)S(1)}, u32[]{:S(2)}, u32[]{:S(2)}) collective-permute-start(bf16[216,768]{1,0:T(8,128)(2,1)S(1)} %add_convert_fusion.8), channel_id=1, source_target_pairs={{0,8},{8,0},{16,24},{24,16},{1,9},{9,1},{17,25},{25,17},{2,10},{10... | collective-permute-start | bytes 995336 | tf_op jit(solution)/shard_map/ppermute | solution.py:38
  418.1 24.6 %collective-permute-start.53 = (bf16[216,768]{1,0:T(8,128)(2,1)S(1)}, bf16[216,768]{1,0:T(8,128)(2,1)S(1)}, u32[]{:S(2)}, u32[]{:S(2)}) collective-permute-start(bf16[216,768]{1,0:T(8,128)(2,1)S(1)} %add_convert_fusion.8), channel_id=1, source_target_pairs={{0,16},{8,24},{16,0},{24,8},{1,17},{9,25},{17,1},{25,9},{2,18},{10... | collective-permute-start | bytes 995336 | tf_op jit(solution)/shard_map/ppermute | solution.py:38
  462.6 31.3 %collective-permute-start.68 = (bf16[192,768]{1,0:T(8,128)(2,1)}, bf16[192,768]{1,0:T(8,128)(2,1)}, u32[]{:S(2)}, u32[]{:S(2)}) collective-permute-start(bf16[192,768]{1,0:T(8,128)(2,1)} %get-tuple-element.361), channel_id=1, source_target_pairs={{0,8},{8,0},{16,24},{24,16},{1,9},{9,1},{17,25},{25,17},{2,10},{10... | collective-permute-start | bytes 884744 | tf_op jit(solution)/shard_map/ppermute | solution.py:38
  500.5 30.8 %collective-permute-start.73 = (bf16[192,768]{1,0:T(8,128)(2,1)S(1)}, bf16[192,768]{1,0:T(8,128)(2,1)S(1)}, u32[]{:S(2)}, u32[]{:S(2)}) collective-permute-start(bf16[192,768]{1,0:T(8,128)(2,1)S(1)} %fusion.4), channel_id=1, source_target_pairs={{0,8},{8,0},{16,24},{24,16},{1,9},{9,1},{17,25},{25,17},{2,10},{10... | collective-permute-start | bytes 884744 | tf_op jit(solution)/shard_map/ppermute | solution.py:38
  500.5 30.7 %collective-permute-start.74 = (bf16[192,768]{1,0:T(8,128)(2,1)S(1)}, bf16[192,768]{1,0:T(8,128)(2,1)S(1)}, u32[]{:S(2)}, u32[]{:S(2)}) collective-permute-start(bf16[192,768]{1,0:T(8,128)(2,1)S(1)} %fusion.4), channel_id=1, source_target_pairs={{0,16},{8,24},{16,0},{24,8},{1,17},{9,25},{17,1},{25,9},{2,18},{10... | collective-permute-start | bytes 884744 | tf_op jit(solution)/shard_map/ppermute | solution.py:38
  (122 other events, 1170.8 us)
Sparse Core Ops, SparseCore 0:
  26.0 34.7 all-gather.5
  63.3 92.0 all-gather.3
  157.9 80.5 all-gather.7
  265.9 95.2 reduce-scatter.3
  364.6 81.4 reduce-scatter.5
  449.1 41.0 reduce-scatter.7

commit v6 on v4

--- a/solution.py
+++ b/solution.py
@@ -907,6 +907,8 @@
             for r in range(groups)
         )
         pieces = tuple(swap_groups(messages))
+        if layer + 1 < LAYERS:
+            pieces = tick([backs[layer + 1]], pieces)
         made = project_back(
             order, place, entered, grad_first, w_project[layer], small, pieces, seq_size
         )
@@ -919,8 +921,10 @@
     for unused in range(2):
         tick(behind)
         tick(backs)
-    while any(item.flying is not None for item in behind):
-        tick(behind)
+    tick(behind)
+    for items in (feeds, backs):
+        while any(item.flying is not None for item in items):
+            tick(items)
     small = jnp.stack(
         [backs[layer].result[3 * share : 3 * share + SMALL_ROWS] for layer in range(LAYERS)]
     ).astype(F32)

time: 553 us -> 550 us (level)
    reduce_scatter x2, waiting for transfers between devices: 7.65 us -> 0.01 us  [per_device(): lax.psum_scatter(terms.reshape(-1, width), 'seq', scatter_dimension=0, ti...]
    ppermute x77, waiting for transfers between devices: 220 us -> 225 us  [exchange(): return lax.ppermute(value, axis, [(i, i ^ mask) for i in range(size)])]
  transfers between devices with their start and end apart: 82 -> 82, of which waited for: 41 -> 44; matrix products, arithmetic and copies ran while one was open for 6% -> 6% of each run, Pallas kernels for 23% -> 23%
where the time goes in v6:
time: 550 us; the launch traced here: 549 us
  waiting for transfers between devices  242 us (44%)
  Pallas kernels  158 us (29%)
  starting transfers between devices  88.9 us (16%)
  other arithmetic  27.3 us (5%)
  local copies, waits for them, and re-layouts  17.8 us (3%)
  between operations  14.8 us (3%)
    ppermute x77, waiting for transfers between devices, exchange(): return lax.ppermute(value, axis, [(i, i ^ mask) for i in range(size)])  225 us
    ppermute x77, starting transfers between devices, exchange(): return lax.ppermute(value, axis, [(i, i ^ mask) for i in range(size)])  88.5 us
    pallas_call x2, Pallas kernels, attend_back(): pl.pallas_call(functools.partial(attend_back_body, groups, members, heads...  41.9 us
    pallas_call x2, Pallas kernels, feed_back(): pl.pallas_call(functools.partial(feed_back_body, groups, span, blocks, de...  34.6 us
    pallas_call x2, Pallas kernels, attend(): pl.pallas_call(functools.partial(attend_body, groups, members, heads), ou...  34.1 us
    pallas_call x2, Pallas kernels, feed(): pl.pallas_call(functools.partial(feed_body, groups, span, blocks, pieces,...  20.1 us
    all_gather x3, waiting for transfers between devices, over_seq(): return lax.all_gather(stack, 'seq', axis=1, tiled=True).reshape(width, -1)  16.7 us
    pallas_call x2, Pallas kernels, project_back(): pl.pallas_call(functools.partial(project_back_body, groups, span, devices...  15.7 us
  transfers between devices with their start and end apart: 82, of which 44 were waited for; matrix products, arithmetic and copies ran while one was open for 6% of the time, Pallas kernels for 23%

profile of v6, /device:TPU:0, one launch (start us, length us, event | category | flops | bytes accessed | tf_op | source)
XLA Modules:
  0.0 548.7 jit_solution(17441368543236630864)
XLA Ops:
  29.2 18.3 %collective-permute-done = bf16[24,9216]{1,0:T(8,128)(2,1)S(1)} collective-permute-done((bf16[24,9216]{1,0:T(8,128)(2,1)S(1)}, bf16[24,9216]{1,0:T(8,128)(2,1)S(1)}, u32[]{:S(2)}, u32[]{:S(2)}) %collective-permute-start) | collective-permute-done | bytes 442400 | tf_op jit(solution)/shard_map/ppermute | solution.py:38
  47.8 11.9 %collective-permute-done.1 = bf16[24,9216]{1,0:T(8,128)(2,1)S(1)} collective-permute-done((bf16[24,9216]{1,0:T(8,128)(2,1)S(1)}, bf16[24,9216]{1,0:T(8,128)(2,1)S(1)}, u32[]{:S(2)}, u32[]{:S(2)}) %collective-permute-start.1) | collective-permute-done | bytes 442400 | tf_op jit(solution)/shard_map/ppermute | solution.py:38
  74.2 11.2 %collective-permute-done.6.rest_1_ = bf16[3,192,256]{2,1,0:T(8,128)(2,1)S(1)} collective-permute-done((bf16[3,192,256]{2,1,0:T(8,128)(2,1)}, bf16[3,192,256]{2,1,0:T(8,128)(2,1)S(1)}, u32[]{:S(2)}, u32[]{:S(2)}) %collective-permute-start.6) | collective-permute-done | bytes 294944 | tf_op jit(solution)/shard_map/ppermute | solution.py:38
  89.4 7.8 %collective-permute-done.8.rest_3_ = bf16[3,192,256]{2,1,0:T(8,128)(2,1)S(1)} collective-permute-done((bf16[3,192,256]{2,1,0:T(8,128)(2,1)}, bf16[3,192,256]{2,1,0:T(8,128)(2,1)S(1)}, u32[]{:S(2)}, u32[]{:S(2)}) %collective-permute-start.8) | collective-permute-done | bytes 294944 | tf_op jit(solution)/shard_map/ppermute | solution.py:38
  100.9 14.8 %collective-permute-done.17 = bf16[24,6912]{1,0:T(8,128)(2,1)S(1)} collective-permute-done((bf16[24,6912]{1,0:T(8,128)(2,1)S(1)}, bf16[24,6912]{1,0:T(8,128)(2,1)S(1)}, u32[]{:S(2)}, u32[]{:S(2)}) %collective-permute-start.17) | collective-permute-done | bytes 331808 | tf_op jit(solution)/shard_map/ppermute | solution.py:38
  116.4 17.1 %attend.2 = (bf16[192,256]{1,0:T(8,128)(2,1)}, bf16[192,256]{1,0:T(8,128)(2,1)}, bf16[192,256]{1,0:T(8,128)(2,1)}, bf16[192,256]{1,0:T(8,128)(2,1)}, f32[4,192,256]{2,1,0:T(8,128)}, /*index=5*/f32[4,3,1,256]{3,2,1,0:T(1,128)}) custom-call(s32[4,8]{1,0:T(4,128)} %and_convert_fusion.active, s32[4,1,256]{2,1,0:T(1,128)} %broadcast_in_dim.37.seg_row, ...), custom_call_target="tpu_custom_call" | custom-call | flops 805306368 | bytes 3932160 | tf_op jit(solution)/shard_map/attend/pallas_call | solution.py:198
  155.4 10.0 %feed.2 = (f32[256,768]{1,0:T(8,128)}, bf16[256,768]{1,0:T(8,128)(2,1)}, f32[256,768]{1,0:T(8,128)}, f32[256,768]{1,0:T(8,128)}) custom-call(s32[4]{0:T(128)} %iota_xor_fusion.order, f32[256,768]{1,0:T(8,128)} %bitcast_convert_fusion.1.x_ref, bf16[768,9216]{1,0:T(8,128)(2,1)} %bitcast.254, bf16[768,9216]{1,0:T(8,128)(2,1)} %bitcast.255, ...), custom_call_target="tpu_custom_call" | custom-call | flops 2717908992 | bytes 10616832 | tf_op jit(solution)/shard_map/feed/pallas_call | solution.py:373
  174.0 12.9 %collective-permute-done.19.rest_1_ = bf16[3,192,256]{2,1,0:T(8,128)(2,1)S(1)} collective-permute-done((bf16[3,192,256]{2,1,0:T(8,128)(2,1)}, bf16[3,192,256]{2,1,0:T(8,128)(2,1)S(1)}, u32[]{:S(2)}, u32[]{:S(2)}) %collective-permute-start.19) | collective-permute-done | bytes 294944 | tf_op jit(solution)/shard_map/ppermute | solution.py:38
  198.8 17.0 %attend.3 = (bf16[192,256]{1,0:T(8,128)(2,1)}, bf16[192,256]{1,0:T(8,128)(2,1)}, bf16[192,256]{1,0:T(8,128)(2,1)}, bf16[192,256]{1,0:T(8,128)(2,1)}, f32[4,192,256]{2,1,0:T(8,128)}, /*index=5*/f32[4,3,1,256]{3,2,1,0:T(1,128)}) custom-call(s32[4,8]{1,0:T(4,128)} %and_convert_fusion.active, s32[4,1,256]{2,1,0:T(1,128)} %broadcast_in_dim.37.seg_row, ...), custom_call_target="tpu_custom_call" | custom-call | flops 805306368 | bytes 3932160 | tf_op jit(solution)/shard_map/attend/pallas_call | solution.py:198
  227.9 10.6 %all-gather.8.cloned.1.call-done = bf16[4,192,6912]{2,1,0:T(8,128)(2,1)} async-done(((bf16[4,24,6912]{2,1,0:T(8,128)(2,1)}), bf16[4,192,6912]{2,1,0:T(8,128)(2,1)}) %all-gather.8.cloned.1.call-update) | async-done | bytes 10616848 | tf_op jit(solution)/shard_map/all_gather | solution.py:769
  238.5 10.0 %feed.3 = (f32[256,768]{1,0:T(8,128)}, bf16[256,768]{1,0:T(8,128)(2,1)}, f32[256,768]{1,0:T(8,128)}, f32[256,768]{1,0:T(8,128)}) custom-call(s32[4]{0:T(128)} %iota_xor_fusion.order, f32[256,768]{1,0:T(8,128)} %get-tuple-element.174.x_ref, bf16[768,6912]{1,0:T(8,128)(2,1)} %bitcast.262, bf16[768,6912]{1,0:T(8,128)(2,1)} %bitcast.263, ...), custom_call_target="tpu_custom_call" | custom-call | flops 2717908992 | bytes 10616832 | tf_op jit(solution)/shard_map/feed/pallas_call | solution.py:373
  248.5 17.3 %feed_back.2 = (bf16[8,864,768]{2,1,0:T(8,128)(2,1)}, f32[256,768]{1,0:T(8,128)}, f32[16,768]{1,0:T(8,128)}, bf16[192,256]{1,0:T(8,128)(2,1)}, bf16[192,256]{1,0...) custom-call(s32[4]{0:T(128)} %iota_xor_fusion.order, f32[256,768]{1,0:T(8,128)} %bitcast_convert_fusion.grad_ref, ...), custom_call_target="tpu_custom_call" | custom-call | flops 6643777536 | bytes 21233664 | tf_op jit(solution)/shard_map/feed_back/pallas_call | solution.py:484
  275.6 21.6 %attend_back.2 = (bf16[4,192,256]{2,1,0:T(8,128)(2,1)}, f32[4,2,192,256]{3,2,1,0:T(8,128)}, bf16[4,2,192,256]{3,2,1,0:T(8,128)(2,1)}) custom-call(s32[4,8]{1,0:T(4,128)} %and_convert_fusion.active, s32[4,1,256]{2,1,0:T(1,128)} %broadcast_in_dim.37.seg_row, s32[8,256,1]{2,1,0:T(8,128)} %select_convert_fusion.seg_col, ...), custom_call_target="tpu_custom_call" | custom-call | flops 2013265920 | bytes 7864320 | tf_op jit(solution)/shard_map/attend_back/pallas_call | solution.py:284
  306.3 11.8 %collective-permute-done.33.rest_1_ = bf16[3,192,256]{2,1,0:T(8,128)(2,1)S(1)} collective-permute-done((bf16[3,192,256]{2,1,0:T(8,128)(2,1)S(1)}, bf16[3,192,256]{2,1,0:T(8,128)(2,1)S(1)}, u32[]{:S(2)}, u32[]{:S(2)}) %collective-permute-start.33) | collective-permute-done | bytes 294944 | tf_op jit(solution)/shard_map/ppermute | solution.py:38
  318.8 11.5 %collective-permute-done.35.rest_3_ = bf16[3,192,256]{2,1,0:T(8,128)(2,1)S(1)} collective-permute-done((bf16[3,192,256]{2,1,0:T(8,128)(2,1)S(1)}, bf16[3,192,256]{2,1,0:T(8,128)(2,1)S(1)}, u32[]{:S(2)}, u32[]{:S(2)}) %collective-permute-start.35) | collective-permute-done | bytes 294944 | tf_op jit(solution)/shard_map/ppermute | solution.py:38
  330.9 7.6 %project_back.2 = (bf16[4,320,768]{2,1,0:T(8,128)(2,1)}, bf16[4,320,768]{2,1,0:T(8,128)(2,1)}, f32[256,768]{1,0:T(8,128)}) custom-call(s32[4]{0:T(128)} %iota_xor_fusion.order, s32[1]{0:T(128)} %bitcast.43.place, f32[256,768]{1,0:T(8,128)} %get-tuple-element.174.x_ref, f32[256,768]{1,0:T(8,128)} %get-tuple-element.190.grad_ref, bf16[768,9216]{1,0:T(8,128)(2,1)} %bitcast.258, ...), custom_call_target="tpu_custom_call" | custom-call | flops 1811939328 | bytes 7077888 | tf_op jit(solution)/shard_map/project_back/pallas_call | solution.py:572
  338.5 17.3 %feed_back.3 = (bf16[8,864,768]{2,1,0:T(8,128)(2,1)}, f32[256,768]{1,0:T(8,128)}, f32[16,768]{1,0:T(8,128)}, bf16[192,256]{1,0:T(8,128)(2,1)}, bf16[192,256]{1,0...) custom-call(s32[4]{0:T(128)} %iota_xor_fusion.order, f32[256,768]{1,0:T(8,128)} %get-tuple-element.205.grad_ref, ...), custom_call_target="tpu_custom_call" | custom-call | flops 6643777536 | bytes 21233664 | tf_op jit(solution)/shard_map/feed_back/pallas_call | solution.py:484
  387.3 20.2 %attend_back.3 = (bf16[4,192,256]{2,1,0:T(8,128)(2,1)}, f32[4,2,192,256]{3,2,1,0:T(8,128)}, bf16[4,2,192,256]{3,2,1,0:T(8,128)(2,1)}) custom-call(s32[4,8]{1,0:T(4,128)} %and_convert_fusion.active, s32[4,1,256]{2,1,0:T(1,128)} %broadcast_in_dim.37.seg_row, s32[8,256,1]{2,1,0:T(8,128)} %select_convert_fusion.seg_col, ...), custom_call_target="tpu_custom_call" | custom-call | flops 2013265920 | bytes 7864320 | tf_op jit(solution)/shard_map/attend_back/pallas_call | solution.py:284
  420.4 8.0 %collective-permute-done.48.rest_1_ = bf16[3,192,256]{2,1,0:T(8,128)(2,1)S(1)} collective-permute-done((bf16[3,192,256]{2,1,0:T(8,128)(2,1)S(1)}, bf16[3,192,256]{2,1,0:T(8,128)(2,1)S(1)}, u32[]{:S(2)}, u32[]{:S(2)}) %collective-permute-start.48) | collective-permute-done | bytes 294944 | tf_op jit(solution)/shard_map/ppermute | solution.py:38
  438.4 8.1 %project_back.3 = (bf16[4,320,768]{2,1,0:T(8,128)(2,1)}, bf16[4,320,768]{2,1,0:T(8,128)(2,1)}, f32[256,768]{1,0:T(8,128)}) custom-call(s32[4]{0:T(128)} %iota_xor_fusion.order, s32[1]{0:T(128)} %bitcast.43.place, f32[256,768]{1,0:T(8,128)} %bitcast_convert_fusion.1.x_ref, f32[256,768]{1,0:T(8,128)} %get-tuple-element.209.grad_ref, ...), custom_call_target="tpu_custom_call" | custom-call | flops 1811939328 | bytes 7077888 | tf_op jit(solution)/shard_map/project_back/pallas_call | solution.py:572
  446.6 8.8 %collective-permute-done.53 = bf16[80,768]{1,0:T(8,128)(2,1)S(1)} collective-permute-done((bf16[80,768]{1,0:T(8,128)(2,1)S(1)}, bf16[80,768]{1,0:T(8,128)(2,1)S(1)}, u32[]{:S(2)}, u32[]{:S(2)}) %collective-permute-start.53) | collective-permute-done | bytes 122912 | tf_op jit(solution)/shard_map/ppermute | solution.py:38
  472.0 7.9 %collective-permute-done.62 = bf16[80,768]{1,0:T(8,128)(2,1)S(1)} collective-permute-done((bf16[80,768]{1,0:T(8,128)(2,1)S(1)}, bf16[80,768]{1,0:T(8,128)(2,1)S(1)}, u32[]{:S(2)}, u32[]{:S(2)}) %collective-permute-start.62) | collective-permute-done | bytes 122912 | tf_op jit(solution)/shard_map/ppermute | solution.py:38
  489.9 10.0 %collective-permute-done.68 = bf16[216,768]{1,0:T(8,128)(2,1)S(1)} collective-permute-done((bf16[216,768]{1,0:T(8,128)(2,1)S(1)}, bf16[216,768]{1,0:T(8,128)(2,1)S(1)}, u32[]{:S(2)}, u32[]{:S(2)}) %collective-permute-start.68) | collective-permute-done | bytes 331808 | tf_op jit(solution)/shard_map/ppermute | solution.py:38
  514.0 8.8 %collective-permute-done.71 = bf16[80,768]{1,0:T(8,128)(2,1)S(1)} collective-permute-done((bf16[80,768]{1,0:T(8,128)(2,1)S(1)}, bf16[80,768]{1,0:T(8,128)(2,1)S(1)}, u32[]{:S(2)}, u32[]{:S(2)}) %collective-permute-start.71) | collective-permute-done | bytes 122912 | tf_op jit(solution)/shard_map/ppermute | solution.py:38
  (378 shorter events, 233.3 us)
Async XLA Ops:
  7.2 56.0 %all-gather.6.cloned.1.call-start = ((), (), s32[]{:S(2)}) async-start(), calls=%async_computation.3 | async-start | bytes 4202496 | tf_op jit(solution)/shard_map/all_gather | solution.py:769
  25.9 129.5 %all-gather.4.cloned.1.call-start = ((), (), s32[]{:S(2)}) async-start(), calls=%async_computation.2 | async-start | bytes 15925248 | tf_op jit(solution)/shard_map/all_gather | solution.py:769
  26.1 21.4 %collective-permute-start = (bf16[24,9216]{1,0:T(8,128)(2,1)S(1)}, bf16[24,9216]{1,0:T(8,128)(2,1)S(1)}, u32[]{:S(2)}, u32[]{:S(2)}) collective-permute-start(bf16[24,9216]{1,0:T(8,128)(2,1)S(1)} %bitcast_dynamic-update-slice_fusion.2), channel_id=1, source_target_pairs={{0,16},{8,24},{16,0},{24,8},{1,17},{9,25},{17,1},{25,9},{2,18},{10... | collective-permute-start | bytes 1327112 | tf_op jit(solution)/shard_map/ppermute | solution.py:38
  26.4 21.3 %collective-permute-start.2 = (bf16[24,9216]{1,0:T(8,128)(2,1)S(1)}, bf16[24,9216]{1,0:T(8,128)(2,1)S(1)}, u32[]{:S(2)}, u32[]{:S(2)}) collective-permute-start(bf16[24,9216]{1,0:T(8,128)(2,1)S(1)} %bitcast_dynamic-update-slice_fusion.2), channel_id=1, source_target_pairs={{0,8},{8,0},{16,24},{24,16},{1,9},{9,1},{17,25},{25,17},{2,10},{10... | collective-permute-start | bytes 1327112 | tf_op jit(solution)/shard_map/ppermute | solution.py:38
  61.2 177.2 %all-gather.8.cloned.1.call-start = ((), (), s32[]{:S(2)}) async-start(), calls=%async_computation.4 | async-start | bytes 11943936 | tf_op jit(solution)/shard_map/all_gather | solution.py:769
  73.0 24.2 %collective-permute-start.8 = (bf16[3,192,256]{2,1,0:T(8,128)(2,1)}, bf16[3,192,256]{2,1,0:T(8,128)(2,1)S(1)}, u32[]{:S(2)}, u32[]{:S(2)}) collective-permute-start(bf16[3,192,256]{2,1,0:T(8,128)(2,1)} %get-tuple-element.156), channel_id=1, source_target_pairs={{0,6},{1,7},{2,4},{3,5},{4,2},{5,3},{6,0},{7,1},{8,14},{9,15},{10,... | collective-permute-start | bytes 884744 | tf_op jit(solution)/shard_map/ppermute | solution.py:38
  73.5 24.9 %collective-permute-start.9 = (bf16[3,192,256]{2,1,0:T(8,128)(2,1)}, bf16[3,192,256]{2,1,0:T(8,128)(2,1)S(1)}, u32[]{:S(2)}, u32[]{:S(2)}) collective-permute-start(bf16[3,192,256]{2,1,0:T(8,128)(2,1)} %get-tuple-element.157.rest_0_), channel_id=1, source_target_pairs={{0,1},{1,0},{2,3},{3,2},{4,5},{5,4},{6,7},{7,6},{8,9},{9,8},{10,11... | collective-permute-start | bytes 884744 | tf_op jit(solution)/shard_map/ppermute | solution.py:38
  100.2 45.6 %collective-permute-start.16 = (bf16[24,6912]{1,0:T(8,128)(2,1)S(1)}, bf16[24,6912]{1,0:T(8,128)(2,1)S(1)}, u32[]{:S(2)}, u32[]{:S(2)}) collective-permute-start(bf16[24,6912]{1,0:T(8,128)(2,1)S(1)} %get-tuple-element.169), channel_id=1, source_target_pairs={{0,8},{8,0},{16,24},{24,16},{1,9},{9,1},{17,25},{25,17},{2,10},{10... | collective-permute-start | bytes 995336 | tf_op jit(solution)/shard_map/ppermute | solution.py:38
  115.7 30.1 %collective-permute-start.18 = (bf16[24,6912]{1,0:T(8,128)(2,1)S(1)}, bf16[24,6912]{1,0:T(8,128)(2,1)S(1)}, u32[]{:S(2)}, u32[]{:S(2)}) collective-permute-start(bf16[24,6912]{1,0:T(8,128)(2,1)S(1)} %collective-permute-done.17), channel_id=1, source_target_pairs={{0,8},{8,0},{16,24},{24,16},{1,9},{9,1},{17,25},{25,17},{2,10},{10... | collective-permute-start | bytes 995336 | tf_op jit(solution)/shard_map/ppermute | solution.py:38
  147.2 219.4 %reduce-scatter.3.cloned.1.call-start = ((), (), s32[]{:S(2)}) async-start(), calls=%async_computation.5 | async-start | bytes 11943936 | tf_op jit(solution)/shard_map/reduce_scatter | solution.py:887
  172.8 23.7 %collective-permute-start.21 = (bf16[3,192,256]{2,1,0:T(8,128)(2,1)}, bf16[3,192,256]{2,1,0:T(8,128)(2,1)S(1)}, u32[]{:S(2)}, u32[]{:S(2)}) collective-permute-start(bf16[3,192,256]{2,1,0:T(8,128)(2,1)} %get-tuple-element.181), channel_id=1, source_target_pairs={{0,6},{1,7},{2,4},{3,5},{4,2},{5,3},{6,0},{7,1},{8,14},{9,15},{10,... | collective-permute-start | bytes 884744 | tf_op jit(solution)/shard_map/ppermute | solution.py:38
  174.0 22.5 %collective-permute-start.22 = (bf16[3,192,256]{2,1,0:T(8,128)(2,1)}, bf16[3,192,256]{2,1,0:T(8,128)(2,1)S(1)}, u32[]{:S(2)}, u32[]{:S(2)}) collective-permute-start(bf16[3,192,256]{2,1,0:T(8,128)(2,1)} %get-tuple-element.178.rest_0_), channel_id=1, source_target_pairs={{0,1},{1,0},{2,3},{3,2},{4,5},{5,4},{6,7},{7,6},{8,9},{9,8},{10,11... | collective-permute-start | bytes 884744 | tf_op jit(solution)/shard_map/ppermute | solution.py:38
  265.8 195.0 %reduce-scatter.5.cloned.1.call-start = ((), (), s32[]{:S(2)}) async-start(), calls=%async_computation.6 | async-start | bytes 11943936 | tf_op jit(solution)/shard_map/reduce_scatter | solution.py:887
  303.6 26.6 %collective-permute-start.35 = (bf16[3,192,256]{2,1,0:T(8,128)(2,1)S(1)}, bf16[3,192,256]{2,1,0:T(8,128)(2,1)S(1)}, u32[]{:S(2)}, u32[]{:S(2)}) collective-permute-start(bf16[3,192,256]{2,1,0:T(8,128)(2,1)S(1)} %pad_maximum_fusion.10), channel_id=1, source_target_pairs={{0,6},{1,7},{2,4},{3,5},{4,2},{5,3},{6,0},{7,1},{8,14},{9,15},{10,... | collective-permute-start | bytes 884744 | tf_op jit(solution)/shard_map/ppermute | solution.py:38
  378.5 29.1 %collective-permute-start.44 = (bf16[216,768]{1,0:T(8,128)(2,1)}, bf16[216,768]{1,0:T(8,128)(2,1)S(1)}, u32[]{:S(2)}, u32[]{:S(2)}) collective-permute-start(bf16[216,768]{1,0:T(8,128)(2,1)} %get-tuple-element.243), channel_id=1, source_target_pairs={{0,8},{8,0},{16,24},{24,16},{1,9},{9,1},{17,25},{25,17},{2,10},{10... | collective-permute-start | bytes 995336 | tf_op jit(solution)/shard_map/ppermute | solution.py:38
  380.0 27.6 %collective-permute-start.45 = (bf16[216,768]{1,0:T(8,128)(2,1)S(1)}, bf16[216,768]{1,0:T(8,128)(2,1)S(1)}, u32[]{:S(2)}, u32[]{:S(2)}) collective-permute-start(bf16[216,768]{1,0:T(8,128)(2,1)S(1)} %get-tuple-element.244), channel_id=1, source_target_pairs={{0,16},{8,24},{16,0},{24,8},{1,17},{9,25},{17,1},{25,9},{2,18},{10... | collective-permute-start | bytes 995336 | tf_op jit(solution)/shard_map/ppermute | solution.py:38
  382.4 25.3 %collective-permute-start.46 = (bf16[216,768]{1,0:T(8,128)(2,1)S(1)}, bf16[216,768]{1,0:T(8,128)(2,1)S(1)}, u32[]{:S(2)}, u32[]{:S(2)}) collective-permute-start(bf16[216,768]{1,0:T(8,128)(2,1)S(1)} %get-tuple-element.245), channel_id=1, source_target_pairs={{0,24},{8,16},{16,8},{24,0},{1,25},{9,17},{17,9},{25,1},{2,26},{10... | collective-permute-start | bytes 995336 | tf_op jit(solution)/shard_map/ppermute | solution.py:38
  384.8 22.8 %collective-permute-start.42 = (bf16[160,768]{1,0:T(8,128)(2,1)S(1)}, bf16[160,768]{1,0:T(8,128)(2,1)S(1)}, u32[]{:S(2)}, u32[]{:S(2)}) collective-permute-start(bf16[160,768]{1,0:T(8,128)(2,1)S(1)} %slice_bitcast_fusion.11), channel_id=1, source_target_pairs={{0,4},{1,5},{2,6},{3,7},{4,0},{5,1},{6,2},{7,3},{8,12},{9,13},{10,... | collective-permute-start | bytes 737288 | tf_op jit(solution)/shard_map/ppermute | solution.py:38
  386.4 21.3 %collective-permute-start.43 = (bf16[160,768]{1,0:T(8,128)(2,1)S(1)}, bf16[160,768]{1,0:T(8,128)(2,1)S(1)}, u32[]{:S(2)}, u32[]{:S(2)}) collective-permute-start(bf16[160,768]{1,0:T(8,128)(2,1)S(1)} %slice_bitcast_fusion.10), channel_id=1, source_target_pairs={{0,2},{1,3},{2,0},{3,1},{4,6},{5,7},{6,4},{7,5},{8,10},{9,11},{10,... | collective-permute-start | bytes 737288 | tf_op jit(solution)/shard_map/ppermute | solution.py:38
  414.6 21.3 %collective-permute-start.50 = (bf16[3,192,256]{2,1,0:T(8,128)(2,1)S(1)}, bf16[3,192,256]{2,1,0:T(8,128)(2,1)S(1)}, u32[]{:S(2)}, u32[]{:S(2)}) collective-permute-start(bf16[3,192,256]{2,1,0:T(8,128)(2,1)S(1)} %pad_maximum_fusion.14), channel_id=1, source_target_pairs={{0,6},{1,7},{2,4},{3,5},{4,2},{5,3},{6,0},{7,1},{8,14},{9,15},{10,... | collective-permute-start | bytes 884744 | tf_op jit(solution)/shard_map/ppermute | solution.py:38
  416.1 30.4 %collective-permute-start.54 = (bf16[216,768]{1,0:T(8,128)(2,1)S(1)}, bf16[216,768]{1,0:T(8,128)(2,1)S(1)}, u32[]{:S(2)}, u32[]{:S(2)}) collective-permute-start(bf16[216,768]{1,0:T(8,128)(2,1)S(1)} %add_convert_fusion.8), channel_id=1, source_target_pairs={{0,8},{8,0},{16,24},{24,16},{1,9},{9,1},{17,25},{25,17},{2,10},{10... | collective-permute-start | bytes 995336 | tf_op jit(solution)/shard_map/ppermute | solution.py:38
  419.1 27.4 %collective-permute-start.55 = (bf16[216,768]{1,0:T(8,128)(2,1)S(1)}, bf16[216,768]{1,0:T(8,128)(2,1)S(1)}, u32[]{:S(2)}, u32[]{:S(2)}) collective-permute-start(bf16[216,768]{1,0:T(8,128)(2,1)S(1)} %add_convert_fusion.8), channel_id=1, source_target_pairs={{0,16},{8,24},{16,0},{24,8},{1,17},{9,25},{17,1},{25,9},{2,18},{10... | collective-permute-start | bytes 995336 | tf_op jit(solution)/shard_map/ppermute | solution.py:38
  503.9 24.1 %collective-permute-start.73 = (bf16[216,768]{1,0:T(8,128)(2,1)S(1)}, bf16[216,768]{1,0:T(8,128)(2,1)S(1)}, u32[]{:S(2)}, u32[]{:S(2)}) collective-permute-start(bf16[216,768]{1,0:T(8,128)(2,1)S(1)} %fusion.3), channel_id=1, source_target_pairs={{0,8},{8,0},{16,24},{24,16},{1,9},{9,1},{17,25},{25,17},{2,10},{10... | collective-permute-start | bytes 995336 | tf_op jit(solution)/shard_map/ppermute | solution.py:38
  505.5 22.5 %collective-permute-start.74 = (bf16[216,768]{1,0:T(8,128)(2,1)S(1)}, bf16[216,768]{1,0:T(8,128)(2,1)S(1)}, u32[]{:S(2)}, u32[]{:S(2)}) collective-permute-start(bf16[216,768]{1,0:T(8,128)(2,1)S(1)} %fusion.3), channel_id=1, source_target_pairs={{0,16},{8,24},{16,0},{24,8},{1,17},{9,25},{17,1},{25,9},{2,18},{10... | collective-permute-start | bytes 995336 | tf_op jit(solution)/shard_map/ppermute | solution.py:38
  (113 other events, 1102.0 us)
Sparse Core Ops, SparseCore 0:
  26.0 34.7 all-gather.5
  63.3 92.0 all-gather.3
  157.9 80.5 all-gather.7
  265.9 95.2 reduce-scatter.2
  364.6 95.2 reduce-scatter.4
